TPU v7x, 512 devices: a whole 4x4x16 slice. The times are simulated.
512 devices in a mesh: dp: 2 (over core), ctx: 64 (over z, x), tp: 4 (over y).
Axes of the slice: x: 4, y: 4, z: 16, core: 2. Of those that a mesh axis runs over, the one named last changes fastest.
Arguments:
- query: bfloat16 [2, 8192, 8192], P('dp', 'ctx', 'tp'), may hold values from -80 to 80
- key: bfloat16 [2, 8192, 1024], P('dp', 'ctx', 'tp'), may hold values from -6 to 6
- value: bfloat16 [2, 8192, 1024], P('dp', 'ctx', 'tp'), may hold values from -6 to 6
- key_shift: float32 [2, 8192, 1024], P('dp', 'ctx', 'tp'), may hold values from -0.6 to 0.6
- value_shift: float32 [2, 8192, 1024], P('dp', 'ctx', 'tp'), may hold values from -0.6 to 0.6
- doc_ids: int32 [2, 8192], P('dp', 'ctx'), may hold values from 0 to 31, never falling along the last dimension, each value on 1 to 2048 neighbouring positions
- target: bfloat16 [2, 8192, 8192], P('dp', 'ctx', 'tp'), may hold values from -160 to 160
Outputs:
- attn: bfloat16 [2, 8192, 8192], P('dp', 'ctx', 'tp')
- new_key_shift: float32 [2, 8192, 1024], P('dp', 'ctx', 'tp')
- new_value_shift: float32 [2, 8192, 1024], P('dp', 'ctx', 'tp')
All inputs are finite; a program needn't handle non-finite values.
Results may differ from a plain program's by a relative error of at most 0.005.
Values may be sent and summed in bfloat16 or wider, within the bound.
No kernel may reach another device: no remote copies, remote signals or barrier semaphores. Data moves between devices by JAX's collectives and lax.ppermute only.
A program may use at most 128 MiB of HBM per device.

v0:
```python
import math

import jax
import jax.numpy as jnp
from jax import lax
from jax.sharding import PartitionSpec as P

HEADS = 64
KV_HEADS = 8
HEAD = 128


step_size = 0.1
radius_scale = 0.13


def passed_along(block, axis, distance):
    devices = range(lax.axis_size(axis))
    route = [(i - distance, i) for i in devices if i - distance in devices]
    return lax.ppermute(block, axis, route)


def for_sending(value):
    return jax.tree.map(lambda a: a.astype(jnp.bfloat16) if a.dtype == jnp.float32 else a, value)


def per_device(query, key, value, key_shift, value_shift, doc_ids, target):
    tokens = query.shape[1]
    kv_local = key.shape[2] // HEAD
    group = HEADS // KV_HEADS
    half = group // 2
    scale = 1.0 / math.sqrt(HEAD)
    ctx_count = lax.axis_size("ctx")
    seq_total = tokens * ctx_count
    doc_limit = min(2048, seq_total // 4)
    reach = (doc_limit + tokens - 2) // tokens
    width = (reach + 1) * tokens
    where_ctx = lax.axis_index("ctx")
    key_new = (key[0].astype(jnp.float32) + key_shift[0]).astype(jnp.bfloat16)
    val_new = (value[0].astype(jnp.float32) + value_shift[0]).astype(jnp.bfloat16)
    own_docs = doc_ids[0]
    local = (key_new, val_new, own_docs)
    pieces = [local]
    current = local
    for offset in range(reach):
        current = passed_along((current[0], current[1], current[2]), "ctx", 1)
        pieces.append(current)
    ordered = pieces[::-1]
    window_keys = jnp.concatenate([piece[0] for piece in ordered], 0)
    window_vals = jnp.concatenate([piece[1] for piece in ordered], 0)
    window_docs = jnp.concatenate([piece[2] for piece in ordered], 0)
    first = (where_ctx - reach) * tokens
    key_pos = first + jnp.arange(width, dtype=jnp.int32)
    query_pos = where_ctx * tokens + jnp.arange(tokens, dtype=jnp.int32)
    allowed = (
        (window_docs[None, :] == own_docs[:, None])
        & (key_pos[None, :] <= query_pos[:, None])
        & (key_pos[None, :] >= 0)
    )
    q_items = jnp.transpose(
        query[0].reshape(tokens, kv_local, 2, half, HEAD), (1, 2, 0, 3, 4)
    ).reshape(kv_local * 2, tokens, half, HEAD)
    t_items = jnp.transpose(
        target[0].reshape(tokens, kv_local, 2, half, HEAD), (1, 2, 0, 3, 4)
    ).reshape(kv_local * 2, tokens, half, HEAD)
    k_items = jnp.repeat(
        jnp.transpose(window_keys.reshape(width, kv_local, HEAD), (1, 0, 2)), 2, axis=0
    )
    v_items = jnp.repeat(
        jnp.transpose(window_vals.reshape(width, kv_local, HEAD), (1, 0, 2)), 2, axis=0
    )

    def per_item(items):
        q_item, t_item, k_item, v_item = items
        scores = (
            jnp.einsum("thd,wd->htw", q_item, k_item, preferred_element_type=jnp.float32) * scale
        )
        scores = jnp.where(allowed[None], scores, -jnp.inf)
        top = jnp.max(scores, -1, keepdims=True)
        expo = jnp.exp(scores - top)
        total = jnp.sum(expo, -1, keepdims=True)
        expo16 = expo.astype(jnp.bfloat16)
        out = jnp.einsum("htw,wd->htd", expo16, v_item, preferred_element_type=jnp.float32) / total
        dprob = jnp.einsum("thd,wd->htw", t_item, v_item, preferred_element_type=jnp.float32)
        delta = jnp.sum(
            jnp.transpose(t_item, (1, 0, 2)).astype(jnp.float32) * out, -1, keepdims=True
        )
        prob = expo / total
        ds16 = (prob * (dprob - delta)).astype(jnp.bfloat16)
        prob16 = prob.astype(jnp.bfloat16)
        dk = jnp.einsum("htw,thd->wd", ds16, q_item, preferred_element_type=jnp.float32) * scale
        dv = jnp.einsum("htw,thd->wd", prob16, t_item, preferred_element_type=jnp.float32)
        return (out.astype(jnp.bfloat16), dk, dv)

    out_items, dk_items, dv_items = lax.map(per_item, (q_items, t_items, k_items, v_items))
    attn = jnp.transpose(
        out_items.reshape(kv_local, 2, half, tokens, HEAD), (3, 0, 1, 2, 4)
    ).reshape(1, tokens, kv_local * group * HEAD)
    dk_heads = jnp.sum(dk_items.reshape(kv_local, 2, width, HEAD), 1)
    dv_heads = jnp.sum(dv_items.reshape(kv_local, 2, width, HEAD), 1)
    grad_window_k = jnp.transpose(dk_heads, (1, 0, 2)).reshape(reach + 1, tokens, kv_local * HEAD)
    grad_window_v = jnp.transpose(dv_heads, (1, 0, 2)).reshape(reach + 1, tokens, kv_local * HEAD)
    carried = (grad_window_k[0], grad_window_v[0])
    for index in range(1, reach + 1):
        moved = passed_along((for_sending(carried[0]), for_sending(carried[1])), "ctx", -1)
        carried = (moved[0] + grad_window_k[index], moved[1] + grad_window_v[index])
    grad_key, grad_val = carried
    local_sq = jnp.sum(grad_key * grad_key) + jnp.sum(grad_val * grad_val)
    overall = lax.psum(local_sq, ("dp", "ctx", "tp"))
    count = lax.axis_size("dp") * seq_total * 2 * KV_HEADS * HEAD
    rms = jnp.sqrt(overall / count + 1e-05)
    moved_key = key_shift[0] + step_size / rms * grad_key
    moved_val = value_shift[0] + step_size / rms * grad_val
    part_sq = jnp.sum(moved_key * moved_key, -1) + jnp.sum(moved_val * moved_val, -1)
    size_sq = lax.psum(part_sq, "tp")
    radius = radius_scale * math.sqrt(2 * KV_HEADS * HEAD)
    factor = jnp.minimum(1.0, radius / jnp.sqrt(size_sq + 1e-06))[:, None]
    return (attn, (moved_key * factor)[None], (moved_val * factor)[None])


def solution(mesh):
    in_specs = (
        P("dp", "ctx", "tp"),
        P("dp", "ctx", "tp"),
        P("dp", "ctx", "tp"),
        P("dp", "ctx", "tp"),
        P("dp", "ctx", "tp"),
        P("dp", "ctx"),
        P("dp", "ctx", "tp"),
    )
    out_specs = (P("dp", "ctx", "tp"), P("dp", "ctx", "tp"), P("dp", "ctx", "tp"))
    return jax.shard_map(
        per_device, mesh=mesh, in_specs=in_specs, out_specs=out_specs, check_vma=False
    )
```

profile of v0, /device:TPU:1, one launch (start us, length us, event | category | flops | bytes accessed | tf_op | source)
XLA Modules:
  0.0 664.7 jit_solution(8726955844077220050)
XLA Ops:
  0.6 4.1 collective-permute-start
  5.6 3.6 collective-permute-start.1
  9.8 3.6 collective-permute-start.2
  14.1 3.6 collective-permute-start.3
  18.4 4.3 collective-permute-start.4
  23.4 5.7 collective-permute-start.5
  29.8 5.7 collective-permute-start.6
  36.2 5.7 collective-permute-start.7
  42.6 5.7 collective-permute-start.8
  50.2 5.7 collective-permute-start.9
  56.0 5.7 collective-permute-start.16
  63.6 5.7 collective-permute-start.10
  69.4 4.5 collective-permute-start.32
  76.6 3.6 collective-permute-start.12
  80.8 3.6 collective-permute-start.13
  85.1 3.6 collective-permute-start.14
  89.4 5.5 collective-permute-start.15
  95.9 5.7 collective-permute-start.33
  101.6 5.7 collective-permute-start.17
  107.3 5.7 collective-permute-start.34
  113.0 5.5 collective-permute-start.18
  120.5 5.1 collective-permute-start.19
  127.6 5.6 collective-permute-start.20
  133.2 6.0 collective-permute-start.37
  139.3 5.7 collective-permute-start.21
  145.0 5.7 collective-permute-start.38
  150.7 5.5 collective-permute-start.22
  158.1 5.8 collective-permute-start.23
  164.0 4.6 collective-permute-start.40
  168.6 6.7 %collective-permute-start.24 = (bf16[128,256]{0,1:T(8,128)(2,1)S(1)}, bf16[128,256]{0,1:T(8,128)(2,1)S(1)}, u32[]{:S(2)}, u32[]{:S(2)}) collective-permute-start(bf16[128,256]{0,1:T(8,128)(2,1)S(1)} %collective-permute-done.23), channel_id=1, source_target_pairs={{0,4},{4,8},{8,12},{12,16},{16,20},{20,24},{24,28},{28,32},{32,36}... | collective-permute-start | bytes 196616 | tf_op jit(solution)/shard_map/ppermute | solution.py:20
  177.3 6.3 collective-permute-start.25
  185.6 6.3 collective-permute-start.26
  193.9 6.3 collective-permute-start.27
  202.6 5.9 collective-permute-start.28
  211.0 6.0 collective-permute-start.29
  219.3 5.9 collective-permute-start.30
  228.2 6.6 collective-permute-start.31
  241.3 73.5 %while.15 = (s32[]{:T(128)}, bf16[4,4,128,128]{2,3,1,0:T(8,128)(2,1)}, f32[4,2176,128]{2,1,0:T(8,128)}, f32[4,2176,128]{2,1,0:T(8,128)}, bf16[4,2176,128]{2,1,0:...) while((s32[]{:T(128)}, ...), condition=%wide.region_4.5_spmd.clone, body=%wide.region_0.4_spmd.clone.sunk | while | flops 1444493824 | bytes 45931848 | solution.py:95
  241.3 3.2 and_and_fusion.2
  250.7 4.9 fusion.100
  255.6 4.2 fusion.101
  259.7 3.2 and_and_fusion.2
  269.1 4.8 fusion.100
  273.9 4.1 fusion.101
  278.0 3.2 and_and_fusion.2
  287.4 4.9 fusion.100
  292.2 4.2 fusion.101
  296.4 3.2 and_and_fusion.2
  305.8 4.9 fusion.100
  310.7 4.1 fusion.101
  314.8 4.8 bitcast_reduce_fusion
  348.2 2.8 collective-permute-done.65
  356.1 3.3 collective-permute-done.66
  376.7 3.4 collective-permute-done.69
  398.4 4.0 collective-permute-done.72
  405.9 3.9 collective-permute-done.73
  413.3 3.6 collective-permute-done.74
  421.1 3.8 collective-permute-done.75
  428.4 3.8 collective-permute-done.76
  435.6 3.2 collective-permute-done.77
  442.8 3.1 collective-permute-done.78
  450.2 3.4 collective-permute-done.79
  458.9 195.1 %psum.14 = f32[]{:T(128)} all-reduce(f32[]{:T(128)S(6)} %add.192), channel_id=1, replica_groups=mesh['dp'=2,'ctx'=64,'tp'=4] {'dp','ctx','tp'}, use_global_device_ids=true, to_apply=%region_9.10 | all-reduce | flops 1 | bytes 8 | tf_op jit(solution)/shard_map/psum | solution.py:109
  654.8 8.3 %psum.15 = f32[128]{0:T(128)S(1)} all-reduce(f32[128]{0:T(128)S(1)} %add.196), channel_id=1, replica_groups=mesh['dp'=2,'ctx'=64,'tp'=4] {'tp'}, use_global_device_ids=true, to_apply=%region_12.13 | all-reduce | flops 128 | bytes 1024 | tf_op jit(solution)/shard_map/psum | solution.py:115
  (397 shorter events, 168.3 us)
Async XLA Ops:
  42.6 7.6 %collective-permute-start.8 = (s32[128]{0:T(128)S(1)}, s32[128]{0:T(128)S(1)}, u32[]{:S(2)}, u32[]{:S(2)}) collective-permute-start(s32[128]{0:T(128)S(1)} %collective-permute-done.7), channel_id=1, source_target_pairs={{0,4},{4,8},{8,12},{12,16},{16,20},{20,24},{24,28},{28,32},{32,36}... | collective-permute-start | bytes 1544 | tf_op jit(solution)/shard_map/ppermute | solution.py:20
  50.2 13.4 %collective-permute-start.9 = (s32[128]{0:T(128)S(1)}, s32[128]{0:T(128)S(1)}, u32[]{:S(2)}, u32[]{:S(2)}) collective-permute-start(s32[128]{0:T(128)S(1)} %collective-permute-done.8), channel_id=1, source_target_pairs={{0,4},{4,8},{8,12},{12,16},{16,20},{20,24},{24,28},{28,32},{32,36}... | collective-permute-start | bytes 1544 | tf_op jit(solution)/shard_map/ppermute | solution.py:20
  56.0 45.6 %collective-permute-start.16 = (bf16[128,256]{0,1:T(8,128)(2,1)S(1)}, bf16[128,256]{0,1:T(8,128)(2,1)S(1)}, u32[]{:S(2)}, u32[]{:S(2)}) collective-permute-start(bf16[128,256]{0,1:T(8,128)(2,1)S(1)} %fusion.48), channel_id=1, source_target_pairs={{0,4},{4,8},{8,12},{12,16},{16,20},{20,24},{24,28},{28,32},{32,36}... | collective-permute-start | bytes 196616 | tf_op jit(solution)/shard_map/ppermute | solution.py:20
  63.6 10.3 %collective-permute-start.10 = (s32[128]{0:T(128)S(1)}, s32[128]{0:T(128)S(1)}, u32[]{:S(2)}, u32[]{:S(2)}) collective-permute-start(s32[128]{0:T(128)S(1)} %collective-permute-done.9), channel_id=1, source_target_pairs={{0,4},{4,8},{8,12},{12,16},{16,20},{20,24},{24,28},{28,32},{32,36}... | collective-permute-start | bytes 1544 | tf_op jit(solution)/shard_map/ppermute | solution.py:20
  69.4 26.5 %collective-permute-start.32 = (bf16[128,256]{0,1:T(8,128)(2,1)S(1)}, bf16[128,256]{0,1:T(8,128)(2,1)S(1)}, u32[]{:S(2)}, u32[]{:S(2)}) collective-permute-start(bf16[128,256]{0,1:T(8,128)(2,1)S(1)} %fusion.47), channel_id=1, source_target_pairs={{0,4},{4,8},{8,12},{12,16},{16,20},{20,24},{24,28},{28,32},{32,36}... | collective-permute-start | bytes 196616 | tf_op jit(solution)/shard_map/ppermute | solution.py:20
  89.4 6.4 collective-permute-start.15
  95.9 11.4 %collective-permute-start.33 = (bf16[128,256]{0,1:T(8,128)(2,1)S(1)}, bf16[128,256]{0,1:T(8,128)(2,1)S(1)}, u32[]{:S(2)}, u32[]{:S(2)}) collective-permute-start(bf16[128,256]{0,1:T(8,128)(2,1)S(1)} %collective-permute-done.32), channel_id=1, source_target_pairs={{0,4},{4,8},{8,12},{12,16},{16,20},{20,24},{24,28},{28,32},{32,36}... | collective-permute-start | bytes 196616 | tf_op jit(solution)/shard_map/ppermute | solution.py:20
  101.6 11.4 %collective-permute-start.17 = (bf16[128,256]{0,1:T(8,128)(2,1)S(1)}, bf16[128,256]{0,1:T(8,128)(2,1)S(1)}, u32[]{:S(2)}, u32[]{:S(2)}) collective-permute-start(bf16[128,256]{0,1:T(8,128)(2,1)S(1)} %collective-permute-done.16), channel_id=1, source_target_pairs={{0,4},{4,8},{8,12},{12,16},{16,20},{20,24},{24,28},{28,32},{32,36}... | collective-permute-start | bytes 196616 | tf_op jit(solution)/shard_map/ppermute | solution.py:20
  107.3 11.2 %collective-permute-start.34 = (bf16[128,256]{0,1:T(8,128)(2,1)S(1)}, bf16[128,256]{0,1:T(8,128)(2,1)S(1)}, u32[]{:S(2)}, u32[]{:S(2)}) collective-permute-start(bf16[128,256]{0,1:T(8,128)(2,1)S(1)} %collective-permute-done.33), channel_id=1, source_target_pairs={{0,4},{4,8},{8,12},{12,16},{16,20},{20,24},{24,28},{28,32},{32,36}... | collective-permute-start | bytes 196616 | tf_op jit(solution)/shard_map/ppermute | solution.py:20
  113.0 7.5 %collective-permute-start.18 = (bf16[128,256]{0,1:T(8,128)(2,1)S(1)}, bf16[128,256]{0,1:T(8,128)(2,1)S(1)}, u32[]{:S(2)}, u32[]{:S(2)}) collective-permute-start(bf16[128,256]{0,1:T(8,128)(2,1)S(1)} %collective-permute-done.17), channel_id=1, source_target_pairs={{0,4},{4,8},{8,12},{12,16},{16,20},{20,24},{24,28},{28,32},{32,36}... | collective-permute-start | bytes 196616 | tf_op jit(solution)/shard_map/ppermute | solution.py:20
  118.5 7.1 %collective-permute-start.35 = (bf16[128,256]{0,1:T(8,128)(2,1)S(1)}, bf16[128,256]{0,1:T(8,128)(2,1)S(1)}, u32[]{:S(2)}, u32[]{:S(2)}) collective-permute-start(bf16[128,256]{0,1:T(8,128)(2,1)S(1)} %collective-permute-done.34), channel_id=1, source_target_pairs={{0,4},{4,8},{8,12},{12,16},{16,20},{20,24},{24,28},{28,32},{32,36}... | collective-permute-start | bytes 196616 | tf_op jit(solution)/shard_map/ppermute | solution.py:20
  120.5 7.1 %collective-permute-start.19 = (bf16[128,256]{0,1:T(8,128)(2,1)S(1)}, bf16[128,256]{0,1:T(8,128)(2,1)S(1)}, u32[]{:S(2)}, u32[]{:S(2)}) collective-permute-start(bf16[128,256]{0,1:T(8,128)(2,1)S(1)} %collective-permute-done.18), channel_id=1, source_target_pairs={{0,4},{4,8},{8,12},{12,16},{16,20},{20,24},{24,28},{28,32},{32,36}... | collective-permute-start | bytes 196616 | tf_op jit(solution)/shard_map/ppermute | solution.py:20
  125.6 7.6 %collective-permute-start.36 = (bf16[128,256]{0,1:T(8,128)(2,1)S(1)}, bf16[128,256]{0,1:T(8,128)(2,1)S(1)}, u32[]{:S(2)}, u32[]{:S(2)}) collective-permute-start(bf16[128,256]{0,1:T(8,128)(2,1)S(1)} %collective-permute-done.35), channel_id=1, source_target_pairs={{0,4},{4,8},{8,12},{12,16},{16,20},{20,24},{24,28},{28,32},{32,36}... | collective-permute-start | bytes 196616 | tf_op jit(solution)/shard_map/ppermute | solution.py:20
  127.6 11.6 %collective-permute-start.20 = (bf16[128,256]{0,1:T(8,128)(2,1)S(1)}, bf16[128,256]{0,1:T(8,128)(2,1)S(1)}, u32[]{:S(2)}, u32[]{:S(2)}) collective-permute-start(bf16[128,256]{0,1:T(8,128)(2,1)S(1)} %collective-permute-done.19), channel_id=1, source_target_pairs={{0,4},{4,8},{8,12},{12,16},{16,20},{20,24},{24,28},{28,32},{32,36}... | collective-permute-start | bytes 196616 | tf_op jit(solution)/shard_map/ppermute | solution.py:20
  133.2 11.7 %collective-permute-start.37 = (bf16[128,256]{0,1:T(8,128)(2,1)S(1)}, bf16[128,256]{0,1:T(8,128)(2,1)S(1)}, u32[]{:S(2)}, u32[]{:S(2)}) collective-permute-start(bf16[128,256]{0,1:T(8,128)(2,1)S(1)} %collective-permute-done.36), channel_id=1, source_target_pairs={{0,4},{4,8},{8,12},{12,16},{16,20},{20,24},{24,28},{28,32},{32,36}... | collective-permute-start | bytes 196616 | tf_op jit(solution)/shard_map/ppermute | solution.py:20
  139.3 11.4 %collective-permute-start.21 = (bf16[128,256]{0,1:T(8,128)(2,1)S(1)}, bf16[128,256]{0,1:T(8,128)(2,1)S(1)}, u32[]{:S(2)}, u32[]{:S(2)}) collective-permute-start(bf16[128,256]{0,1:T(8,128)(2,1)S(1)} %collective-permute-done.20), channel_id=1, source_target_pairs={{0,4},{4,8},{8,12},{12,16},{16,20},{20,24},{24,28},{28,32},{32,36}... | collective-permute-start | bytes 196616 | tf_op jit(solution)/shard_map/ppermute | solution.py:20
  145.0 11.2 %collective-permute-start.38 = (bf16[128,256]{0,1:T(8,128)(2,1)S(1)}, bf16[128,256]{0,1:T(8,128)(2,1)S(1)}, u32[]{:S(2)}, u32[]{:S(2)}) collective-permute-start(bf16[128,256]{0,1:T(8,128)(2,1)S(1)} %collective-permute-done.37), channel_id=1, source_target_pairs={{0,4},{4,8},{8,12},{12,16},{16,20},{20,24},{24,28},{28,32},{32,36}... | collective-permute-start | bytes 196616 | tf_op jit(solution)/shard_map/ppermute | solution.py:20
  150.7 7.5 %collective-permute-start.22 = (bf16[128,256]{0,1:T(8,128)(2,1)S(1)}, bf16[128,256]{0,1:T(8,128)(2,1)S(1)}, u32[]{:S(2)}, u32[]{:S(2)}) collective-permute-start(bf16[128,256]{0,1:T(8,128)(2,1)S(1)} %collective-permute-done.21), channel_id=1, source_target_pairs={{0,4},{4,8},{8,12},{12,16},{16,20},{20,24},{24,28},{28,32},{32,36}... | collective-permute-start | bytes 196616 | tf_op jit(solution)/shard_map/ppermute | solution.py:20
  156.2 7.8 %collective-permute-start.39 = (bf16[128,256]{0,1:T(8,128)(2,1)S(1)}, bf16[128,256]{0,1:T(8,128)(2,1)S(1)}, u32[]{:S(2)}, u32[]{:S(2)}) collective-permute-start(bf16[128,256]{0,1:T(8,128)(2,1)S(1)} %collective-permute-done.38), channel_id=1, source_target_pairs={{0,4},{4,8},{8,12},{12,16},{16,20},{20,24},{24,28},{28,32},{32,36}... | collective-permute-start | bytes 196616 | tf_op jit(solution)/shard_map/ppermute | solution.py:20
  158.1 10.4 %collective-permute-start.23 = (bf16[128,256]{0,1:T(8,128)(2,1)S(1)}, bf16[128,256]{0,1:T(8,128)(2,1)S(1)}, u32[]{:S(2)}, u32[]{:S(2)}) collective-permute-start(bf16[128,256]{0,1:T(8,128)(2,1)S(1)} %collective-permute-done.22), channel_id=1, source_target_pairs={{0,4},{4,8},{8,12},{12,16},{16,20},{20,24},{24,28},{28,32},{32,36}... | collective-permute-start | bytes 196616 | tf_op jit(solution)/shard_map/ppermute | solution.py:20
  164.0 11.3 %collective-permute-start.40 = (bf16[128,256]{0,1:T(8,128)(2,1)S(1)}, bf16[128,256]{0,1:T(8,128)(2,1)S(1)}, u32[]{:S(2)}, u32[]{:S(2)}) collective-permute-start(bf16[128,256]{0,1:T(8,128)(2,1)S(1)} %collective-permute-done.39), channel_id=1, source_target_pairs={{0,4},{4,8},{8,12},{12,16},{16,20},{20,24},{24,28},{28,32},{32,36}... | collective-permute-start | bytes 196616 | tf_op jit(solution)/shard_map/ppermute | solution.py:20
  168.6 8.7 %collective-permute-start.24 = (bf16[128,256]{0,1:T(8,128)(2,1)S(1)}, bf16[128,256]{0,1:T(8,128)(2,1)S(1)}, u32[]{:S(2)}, u32[]{:S(2)}) collective-permute-start(bf16[128,256]{0,1:T(8,128)(2,1)S(1)} %collective-permute-done.23), channel_id=1, source_target_pairs={{0,4},{4,8},{8,12},{12,16},{16,20},{20,24},{24,28},{28,32},{32,36}... | collective-permute-start | bytes 196616 | tf_op jit(solution)/shard_map/ppermute | solution.py:20
  175.3 8.3 %collective-permute-start.41 = (bf16[128,256]{0,1:T(8,128)(2,1)S(1)}, bf16[128,256]{0,1:T(8,128)(2,1)S(1)}, u32[]{:S(2)}, u32[]{:S(2)}) collective-permute-start(bf16[128,256]{0,1:T(8,128)(2,1)S(1)} %collective-permute-done.40), channel_id=1, source_target_pairs={{0,4},{4,8},{8,12},{12,16},{16,20},{20,24},{24,28},{28,32},{32,36}... | collective-permute-start | bytes 196616 | tf_op jit(solution)/shard_map/ppermute | solution.py:20
  177.3 8.3 %collective-permute-start.25 = (bf16[128,256]{0,1:T(8,128)(2,1)S(1)}, bf16[128,256]{0,1:T(8,128)(2,1)S(1)}, u32[]{:S(2)}, u32[]{:S(2)}) collective-permute-start(bf16[128,256]{0,1:T(8,128)(2,1)S(1)} %collective-permute-done.24), channel_id=1, source_target_pairs={{0,4},{4,8},{8,12},{12,16},{16,20},{20,24},{24,28},{28,32},{32,36}... | collective-permute-start | bytes 196616 | tf_op jit(solution)/shard_map/ppermute | solution.py:20
  183.6 8.3 %collective-permute-start.42 = (bf16[128,256]{0,1:T(8,128)(2,1)S(1)}, bf16[128,256]{0,1:T(8,128)(2,1)S(1)}, u32[]{:S(2)}, u32[]{:S(2)}) collective-permute-start(bf16[128,256]{0,1:T(8,128)(2,1)S(1)} %collective-permute-done.41), channel_id=1, source_target_pairs={{0,4},{4,8},{8,12},{12,16},{16,20},{20,24},{24,28},{28,32},{32,36}... | collective-permute-start | bytes 196616 | tf_op jit(solution)/shard_map/ppermute | solution.py:20
  185.6 8.3 %collective-permute-start.26 = (bf16[128,256]{0,1:T(8,128)(2,1)S(1)}, bf16[128,256]{0,1:T(8,128)(2,1)S(1)}, u32[]{:S(2)}, u32[]{:S(2)}) collective-permute-start(bf16[128,256]{0,1:T(8,128)(2,1)S(1)} %collective-permute-done.25), channel_id=1, source_target_pairs={{0,4},{4,8},{8,12},{12,16},{16,20},{20,24},{24,28},{28,32},{32,36}... | collective-permute-start | bytes 196616 | tf_op jit(solution)/shard_map/ppermute | solution.py:20
  191.9 8.3 %collective-permute-start.43 = (bf16[128,256]{0,1:T(8,128)(2,1)S(1)}, bf16[128,256]{0,1:T(8,128)(2,1)S(1)}, u32[]{:S(2)}, u32[]{:S(2)}) collective-permute-start(bf16[128,256]{0,1:T(8,128)(2,1)S(1)} %collective-permute-done.42), channel_id=1, source_target_pairs={{0,4},{4,8},{8,12},{12,16},{16,20},{20,24},{24,28},{28,32},{32,36}... | collective-permute-start | bytes 196616 | tf_op jit(solution)/shard_map/ppermute | solution.py:20
  193.9 8.7 %collective-permute-start.27 = (bf16[128,256]{0,1:T(8,128)(2,1)S(1)}, bf16[128,256]{0,1:T(8,128)(2,1)S(1)}, u32[]{:S(2)}, u32[]{:S(2)}) collective-permute-start(bf16[128,256]{0,1:T(8,128)(2,1)S(1)} %collective-permute-done.26), channel_id=1, source_target_pairs={{0,4},{4,8},{8,12},{12,16},{16,20},{20,24},{24,28},{28,32},{32,36}... | collective-permute-start | bytes 196616 | tf_op jit(solution)/shard_map/ppermute | solution.py:20
  200.3 8.3 %collective-permute-start.44 = (bf16[128,256]{0,1:T(8,128)(2,1)S(1)}, bf16[128,256]{0,1:T(8,128)(2,1)S(1)}, u32[]{:S(2)}, u32[]{:S(2)}) collective-permute-start(bf16[128,256]{0,1:T(8,128)(2,1)S(1)} %collective-permute-done.43), channel_id=1, source_target_pairs={{0,4},{4,8},{8,12},{12,16},{16,20},{20,24},{24,28},{28,32},{32,36}... | collective-permute-start | bytes 196616 | tf_op jit(solution)/shard_map/ppermute | solution.py:20
  202.6 8.3 %collective-permute-start.28 = (bf16[128,256]{0,1:T(8,128)(2,1)S(1)}, bf16[128,256]{0,1:T(8,128)(2,1)S(1)}, u32[]{:S(2)}, u32[]{:S(2)}) collective-permute-start(bf16[128,256]{0,1:T(8,128)(2,1)S(1)} %collective-permute-done.27), channel_id=1, source_target_pairs={{0,4},{4,8},{8,12},{12,16},{16,20},{20,24},{24,28},{28,32},{32,36}... | collective-permute-start | bytes 196616 | tf_op jit(solution)/shard_map/ppermute | solution.py:20
  208.6 8.3 %collective-permute-start.45 = (bf16[128,256]{0,1:T(8,128)(2,1)S(1)}, bf16[128,256]{0,1:T(8,128)(2,1)S(1)}, u32[]{:S(2)}, u32[]{:S(2)}) collective-permute-start(bf16[128,256]{0,1:T(8,128)(2,1)S(1)} %collective-permute-done.44), channel_id=1, source_target_pairs={{0,4},{4,8},{8,12},{12,16},{16,20},{20,24},{24,28},{28,32},{32,36}... | collective-permute-start | bytes 196616 | tf_op jit(solution)/shard_map/ppermute | solution.py:20
  211.0 8.3 %collective-permute-start.29 = (bf16[128,256]{0,1:T(8,128)(2,1)S(1)}, bf16[128,256]{0,1:T(8,128)(2,1)S(1)}, u32[]{:S(2)}, u32[]{:S(2)}) collective-permute-start(bf16[128,256]{0,1:T(8,128)(2,1)S(1)} %collective-permute-done.28), channel_id=1, source_target_pairs={{0,4},{4,8},{8,12},{12,16},{16,20},{20,24},{24,28},{28,32},{32,36}... | collective-permute-start | bytes 196616 | tf_op jit(solution)/shard_map/ppermute | solution.py:20
  216.9 8.3 %collective-permute-start.46 = (bf16[128,256]{0,1:T(8,128)(2,1)S(1)}, bf16[128,256]{0,1:T(8,128)(2,1)S(1)}, u32[]{:S(2)}, u32[]{:S(2)}) collective-permute-start(bf16[128,256]{0,1:T(8,128)(2,1)S(1)} %collective-permute-done.45), channel_id=1, source_target_pairs={{0,4},{4,8},{8,12},{12,16},{16,20},{20,24},{24,28},{28,32},{32,36}... | collective-permute-start | bytes 196616 | tf_op jit(solution)/shard_map/ppermute | solution.py:20
  219.3 9.0 %collective-permute-start.30 = (bf16[128,256]{0,1:T(8,128)(2,1)S(1)}, bf16[128,256]{0,1:T(8,128)(2,1)S(1)}, u32[]{:S(2)}, u32[]{:S(2)}) collective-permute-start(bf16[128,256]{0,1:T(8,128)(2,1)S(1)} %collective-permute-done.29), channel_id=1, source_target_pairs={{0,4},{4,8},{8,12},{12,16},{16,20},{20,24},{24,28},{28,32},{32,36}... | collective-permute-start | bytes 196616 | tf_op jit(solution)/shard_map/ppermute | solution.py:20
  225.2 9.6 %collective-permute-start.47 = (bf16[128,256]{0,1:T(8,128)(2,1)S(1)}, bf16[128,256]{0,1:T(8,128)(2,1)S(1)}, u32[]{:S(2)}, u32[]{:S(2)}) collective-permute-start(bf16[128,256]{0,1:T(8,128)(2,1)S(1)} %collective-permute-done.46), channel_id=1, source_target_pairs={{0,4},{4,8},{8,12},{12,16},{16,20},{20,24},{24,28},{28,32},{32,36}... | collective-permute-start | bytes 196616 | tf_op jit(solution)/shard_map/ppermute | solution.py:20
  228.2 7.7 %collective-permute-start.31 = (bf16[128,256]{0,1:T(8,128)(2,1)S(1)}, bf16[128,256]{0,1:T(8,128)(2,1)S(1)}, u32[]{:S(2)}, u32[]{:S(2)}) collective-permute-start(bf16[128,256]{0,1:T(8,128)(2,1)S(1)} %collective-permute-done.30), channel_id=1, source_target_pairs={{0,4},{4,8},{8,12},{12,16},{16,20},{20,24},{24,28},{28,32},{32,36}... | collective-permute-start | bytes 196616 | tf_op jit(solution)/shard_map/ppermute | solution.py:20
  321.6 22.0 %collective-permute-start.64 = (bf16[128,256]{0,1:T(8,128)(2,1)}, bf16[128,256]{0,1:T(8,128)(2,1)}, u32[]{:S(2)}, u32[]{:S(2)}) collective-permute-start(bf16[128,256]{0,1:T(8,128)(2,1)} %bitcast.39), channel_id=1, source_target_pairs={{4,0},{8,4},{12,8},{16,12},{20,16},{24,20},{28,24},{32,28},{36,32}... | collective-permute-start | bytes 196616 | tf_op jit(solution)/shard_map/ppermute | solution.py:20
  328.5 17.6 %collective-permute-start.48 = (bf16[128,256]{0,1:T(8,128)(2,1)}, bf16[128,256]{0,1:T(8,128)(2,1)}, u32[]{:S(2)}, u32[]{:S(2)}) collective-permute-start(bf16[128,256]{0,1:T(8,128)(2,1)} %bitcast.20), channel_id=1, source_target_pairs={{4,0},{8,4},{12,8},{16,12},{20,16},{24,20},{28,24},{32,28},{36,32}... | collective-permute-start | bytes 196616 | tf_op jit(solution)/shard_map/ppermute | solution.py:20
  346.9 6.9 %collective-permute-start.49 = (bf16[128,256]{0,1:T(8,128)(2,1)S(1)}, bf16[128,256]{0,1:T(8,128)(2,1)S(1)}, u32[]{:S(2)}, u32[]{:S(2)}) collective-permute-start(bf16[128,256]{0,1:T(8,128)(2,1)S(1)} %fusion.78), channel_id=1, source_target_pairs={{4,0},{8,4},{12,8},{16,12},{20,16},{24,20},{28,24},{32,28},{36,32}... | collective-permute-start | bytes 196616 | tf_op jit(solution)/shard_map/ppermute | solution.py:20
  351.9 7.4 %collective-permute-start.66 = (bf16[128,256]{0,1:T(8,128)(2,1)S(1)}, bf16[128,256]{0,1:T(8,128)(2,1)S(1)}, u32[]{:S(2)}, u32[]{:S(2)}) collective-permute-start(bf16[128,256]{0,1:T(8,128)(2,1)S(1)} %fusion.62), channel_id=1, source_target_pairs={{4,0},{8,4},{12,8},{16,12},{20,16},{24,20},{28,24},{32,28},{36,32}... | collective-permute-start | bytes 196616 | tf_op jit(solution)/shard_map/ppermute | solution.py:20
  354.8 7.0 %collective-permute-start.50 = (bf16[128,256]{0,1:T(8,128)(2,1)S(1)}, bf16[128,256]{0,1:T(8,128)(2,1)S(1)}, u32[]{:S(2)}, u32[]{:S(2)}) collective-permute-start(bf16[128,256]{0,1:T(8,128)(2,1)S(1)} %fusion.77), channel_id=1, source_target_pairs={{4,0},{8,4},{12,8},{16,12},{20,16},{24,20},{28,24},{32,28},{36,32}... | collective-permute-start | bytes 196616 | tf_op jit(solution)/shard_map/ppermute | solution.py:20
  365.5 7.1 %collective-permute-start.68 = (bf16[128,256]{0,1:T(8,128)(2,1)S(1)}, bf16[128,256]{0,1:T(8,128)(2,1)S(1)}, u32[]{:S(2)}, u32[]{:S(2)}) collective-permute-start(bf16[128,256]{0,1:T(8,128)(2,1)S(1)} %fusion.60), channel_id=1, source_target_pairs={{4,0},{8,4},{12,8},{16,12},{20,16},{24,20},{28,24},{32,28},{36,32}... | collective-permute-start | bytes 196616 | tf_op jit(solution)/shard_map/ppermute | solution.py:20
  368.5 6.9 %collective-permute-start.52 = (bf16[128,256]{0,1:T(8,128)(2,1)S(1)}, bf16[128,256]{0,1:T(8,128)(2,1)S(1)}, u32[]{:S(2)}, u32[]{:S(2)}) collective-permute-start(bf16[128,256]{0,1:T(8,128)(2,1)S(1)} %fusion.75), channel_id=1, source_target_pairs={{4,0},{8,4},{12,8},{16,12},{20,16},{24,20},{28,24},{32,28},{36,32}... | collective-permute-start | bytes 196616 | tf_op jit(solution)/shard_map/ppermute | solution.py:20
  372.5 7.6 %collective-permute-start.69 = (bf16[128,256]{0,1:T(8,128)(2,1)S(1)}, bf16[128,256]{0,1:T(8,128)(2,1)S(1)}, u32[]{:S(2)}, u32[]{:S(2)}) collective-permute-start(bf16[128,256]{0,1:T(8,128)(2,1)S(1)} %fusion.59), channel_id=1, source_target_pairs={{4,0},{8,4},{12,8},{16,12},{20,16},{24,20},{28,24},{32,28},{36,32}... | collective-permute-start | bytes 196616 | tf_op jit(solution)/shard_map/ppermute | solution.py:20
  375.4 8.4 %collective-permute-start.53 = (bf16[128,256]{0,1:T(8,128)(2,1)S(1)}, bf16[128,256]{0,1:T(8,128)(2,1)S(1)}, u32[]{:S(2)}, u32[]{:S(2)}) collective-permute-start(bf16[128,256]{0,1:T(8,128)(2,1)S(1)} %fusion.74), channel_id=1, source_target_pairs={{4,0},{8,4},{12,8},{16,12},{20,16},{24,20},{28,24},{32,28},{36,32}... | collective-permute-start | bytes 196616 | tf_op jit(solution)/shard_map/ppermute | solution.py:20
  380.2 6.9 %collective-permute-start.70 = (bf16[128,256]{0,1:T(8,128)(2,1)S(1)}, bf16[128,256]{0,1:T(8,128)(2,1)S(1)}, u32[]{:S(2)}, u32[]{:S(2)}) collective-permute-start(bf16[128,256]{0,1:T(8,128)(2,1)S(1)} %fusion.58), channel_id=1, source_target_pairs={{4,0},{8,4},{12,8},{16,12},{20,16},{24,20},{28,24},{32,28},{36,32}... | collective-permute-start | bytes 196616 | tf_op jit(solution)/shard_map/ppermute | solution.py:20
  383.8 7.2 %collective-permute-start.54 = (bf16[128,256]{0,1:T(8,128)(2,1)S(1)}, bf16[128,256]{0,1:T(8,128)(2,1)S(1)}, u32[]{:S(2)}, u32[]{:S(2)}) collective-permute-start(bf16[128,256]{0,1:T(8,128)(2,1)S(1)} %fusion.73), channel_id=1, source_target_pairs={{4,0},{8,4},{12,8},{16,12},{20,16},{24,20},{28,24},{32,28},{36,32}... | collective-permute-start | bytes 196616 | tf_op jit(solution)/shard_map/ppermute | solution.py:20
  387.2 7.3 %collective-permute-start.71 = (bf16[128,256]{0,1:T(8,128)(2,1)S(1)}, bf16[128,256]{0,1:T(8,128)(2,1)S(1)}, u32[]{:S(2)}, u32[]{:S(2)}) collective-permute-start(bf16[128,256]{0,1:T(8,128)(2,1)S(1)} %fusion.57), channel_id=1, source_target_pairs={{4,0},{8,4},{12,8},{16,12},{20,16},{24,20},{28,24},{32,28},{36,32}... | collective-permute-start | bytes 196616 | tf_op jit(solution)/shard_map/ppermute | solution.py:20
  394.4 8.0 %collective-permute-start.72 = (bf16[128,256]{0,1:T(8,128)(2,1)S(1)}, bf16[128,256]{0,1:T(8,128)(2,1)S(1)}, u32[]{:S(2)}, u32[]{:S(2)}) collective-permute-start(bf16[128,256]{0,1:T(8,128)(2,1)S(1)} %fusion.56), channel_id=1, source_target_pairs={{4,0},{8,4},{12,8},{16,12},{20,16},{24,20},{28,24},{32,28},{36,32}... | collective-permute-start | bytes 196616 | tf_op jit(solution)/shard_map/ppermute | solution.py:20
  397.1 7.5 %collective-permute-start.56 = (bf16[128,256]{0,1:T(8,128)(2,1)S(1)}, bf16[128,256]{0,1:T(8,128)(2,1)S(1)}, u32[]{:S(2)}, u32[]{:S(2)}) collective-permute-start(bf16[128,256]{0,1:T(8,128)(2,1)S(1)} %fusion.71), channel_id=1, source_target_pairs={{4,0},{8,4},{12,8},{16,12},{20,16},{24,20},{28,24},{32,28},{36,32}... | collective-permute-start | bytes 196616 | tf_op jit(solution)/shard_map/ppermute | solution.py:20
  402.5 7.3 %collective-permute-start.73 = (bf16[128,256]{0,1:T(8,128)(2,1)S(1)}, bf16[128,256]{0,1:T(8,128)(2,1)S(1)}, u32[]{:S(2)}, u32[]{:S(2)}) collective-permute-start(bf16[128,256]{0,1:T(8,128)(2,1)S(1)} %fusion.55), channel_id=1, source_target_pairs={{4,0},{8,4},{12,8},{16,12},{20,16},{24,20},{28,24},{32,28},{36,32}... | collective-permute-start | bytes 196616 | tf_op jit(solution)/shard_map/ppermute | solution.py:20
  404.6 7.4 %collective-permute-start.57 = (bf16[128,256]{0,1:T(8,128)(2,1)S(1)}, bf16[128,256]{0,1:T(8,128)(2,1)S(1)}, u32[]{:S(2)}, u32[]{:S(2)}) collective-permute-start(bf16[128,256]{0,1:T(8,128)(2,1)S(1)} %fusion.70), channel_id=1, source_target_pairs={{4,0},{8,4},{12,8},{16,12},{20,16},{24,20},{28,24},{32,28},{36,32}... | collective-permute-start | bytes 196616 | tf_op jit(solution)/shard_map/ppermute | solution.py:20
  409.8 7.1 %collective-permute-start.74 = (bf16[128,256]{0,1:T(8,128)(2,1)S(1)}, bf16[128,256]{0,1:T(8,128)(2,1)S(1)}, u32[]{:S(2)}, u32[]{:S(2)}) collective-permute-start(bf16[128,256]{0,1:T(8,128)(2,1)S(1)} %fusion.54), channel_id=1, source_target_pairs={{4,0},{8,4},{12,8},{16,12},{20,16},{24,20},{28,24},{32,28},{36,32}... | collective-permute-start | bytes 196616 | tf_op jit(solution)/shard_map/ppermute | solution.py:20
  412.0 7.7 %collective-permute-start.58 = (bf16[128,256]{0,1:T(8,128)(2,1)S(1)}, bf16[128,256]{0,1:T(8,128)(2,1)S(1)}, u32[]{:S(2)}, u32[]{:S(2)}) collective-permute-start(bf16[128,256]{0,1:T(8,128)(2,1)S(1)} %fusion.69), channel_id=1, source_target_pairs={{4,0},{8,4},{12,8},{16,12},{20,16},{24,20},{28,24},{32,28},{36,32}... | collective-permute-start | bytes 196616 | tf_op jit(solution)/shard_map/ppermute | solution.py:20
  416.9 8.0 %collective-permute-start.75 = (bf16[128,256]{0,1:T(8,128)(2,1)S(1)}, bf16[128,256]{0,1:T(8,128)(2,1)S(1)}, u32[]{:S(2)}, u32[]{:S(2)}) collective-permute-start(bf16[128,256]{0,1:T(8,128)(2,1)S(1)} %fusion.53), channel_id=1, source_target_pairs={{4,0},{8,4},{12,8},{16,12},{20,16},{24,20},{28,24},{32,28},{36,32}... | collective-permute-start | bytes 196616 | tf_op jit(solution)/shard_map/ppermute | solution.py:20
  419.8 7.3 %collective-permute-start.59 = (bf16[128,256]{0,1:T(8,128)(2,1)S(1)}, bf16[128,256]{0,1:T(8,128)(2,1)S(1)}, u32[]{:S(2)}, u32[]{:S(2)}) collective-permute-start(bf16[128,256]{0,1:T(8,128)(2,1)S(1)} %fusion.68), channel_id=1, source_target_pairs={{4,0},{8,4},{12,8},{16,12},{20,16},{24,20},{28,24},{32,28},{36,32}... | collective-permute-start | bytes 196616 | tf_op jit(solution)/shard_map/ppermute | solution.py:20
  424.9 7.4 %collective-permute-start.76 = (bf16[128,256]{0,1:T(8,128)(2,1)S(1)}, bf16[128,256]{0,1:T(8,128)(2,1)S(1)}, u32[]{:S(2)}, u32[]{:S(2)}) collective-permute-start(bf16[128,256]{0,1:T(8,128)(2,1)S(1)} %fusion.52), channel_id=1, source_target_pairs={{4,0},{8,4},{12,8},{16,12},{20,16},{24,20},{28,24},{32,28},{36,32}... | collective-permute-start | bytes 196616 | tf_op jit(solution)/shard_map/ppermute | solution.py:20
  427.1 7.2 %collective-permute-start.60 = (bf16[128,256]{0,1:T(8,128)(2,1)S(1)}, bf16[128,256]{0,1:T(8,128)(2,1)S(1)}, u32[]{:S(2)}, u32[]{:S(2)}) collective-permute-start(bf16[128,256]{0,1:T(8,128)(2,1)S(1)} %fusion.67), channel_id=1, source_target_pairs={{4,0},{8,4},{12,8},{16,12},{20,16},{24,20},{28,24},{32,28},{36,32}... | collective-permute-start | bytes 196616 | tf_op jit(solution)/shard_map/ppermute | solution.py:20
  432.3 6.5 collective-permute-start.77
  434.3 7.2 %collective-permute-start.61 = (bf16[128,256]{0,1:T(8,128)(2,1)S(1)}, bf16[128,256]{0,1:T(8,128)(2,1)S(1)}, u32[]{:S(2)}, u32[]{:S(2)}) collective-permute-start(bf16[128,256]{0,1:T(8,128)(2,1)S(1)} %fusion.66), channel_id=1, source_target_pairs={{4,0},{8,4},{12,8},{16,12},{20,16},{24,20},{28,24},{32,28},{36,32}... | collective-permute-start | bytes 196616 | tf_op jit(solution)/shard_map/ppermute | solution.py:20
  438.8 7.1 %collective-permute-start.78 = (bf16[128,256]{0,1:T(8,128)(2,1)S(1)}, bf16[128,256]{0,1:T(8,128)(2,1)S(1)}, u32[]{:S(2)}, u32[]{:S(2)}) collective-permute-start(bf16[128,256]{0,1:T(8,128)(2,1)S(1)} %fusion.50), channel_id=1, source_target_pairs={{4,0},{8,4},{12,8},{16,12},{20,16},{24,20},{28,24},{32,28},{36,32}... | collective-permute-start | bytes 196616 | tf_op jit(solution)/shard_map/ppermute | solution.py:20
  441.5 7.3 %collective-permute-start.62 = (bf16[128,256]{0,1:T(8,128)(2,1)S(1)}, bf16[128,256]{0,1:T(8,128)(2,1)S(1)}, u32[]{:S(2)}, u32[]{:S(2)}) collective-permute-start(bf16[128,256]{0,1:T(8,128)(2,1)S(1)} %fusion.65), channel_id=1, source_target_pairs={{4,0},{8,4},{12,8},{16,12},{20,16},{24,20},{28,24},{32,28},{36,32}... | collective-permute-start | bytes 196616 | tf_op jit(solution)/shard_map/ppermute | solution.py:20
  446.0 7.5 %collective-permute-start.79 = (bf16[128,256]{0,1:T(8,128)(2,1)S(1)}, bf16[128,256]{0,1:T(8,128)(2,1)S(1)}, u32[]{:S(2)}, u32[]{:S(2)}) collective-permute-start(bf16[128,256]{0,1:T(8,128)(2,1)S(1)} %fusion.49), channel_id=1, source_target_pairs={{4,0},{8,4},{12,8},{16,12},{20,16},{24,20},{28,24},{32,28},{36,32}... | collective-permute-start | bytes 196616 | tf_op jit(solution)/shard_map/ppermute | solution.py:20
  448.9 6.9 %collective-permute-start.63 = (bf16[128,256]{0,1:T(8,128)(2,1)S(1)}, bf16[128,256]{0,1:T(8,128)(2,1)S(1)}, u32[]{:S(2)}, u32[]{:S(2)}) collective-permute-start(bf16[128,256]{0,1:T(8,128)(2,1)S(1)} %fusion.64), channel_id=1, source_target_pairs={{4,0},{8,4},{12,8},{16,12},{20,16},{24,20},{28,24},{32,28},{36,32}... | collective-permute-start | bytes 196616 | tf_op jit(solution)/shard_map/ppermute | solution.py:20
  (76 other events, 1214.7 us)
where the time goes:
time: 668 us; the launch traced here: 665 us
  starting transfers between devices  262 us (39%)
  blocking collectives  203 us (30%)
  waiting for transfers between devices  72.7 us (11%)
  matrix products  49.6 us (7%)
  local copies, waits for them, and re-layouts  41.3 us (6%)
  other arithmetic  31.1 us (5%)
    ppermute x80, starting transfers between devices, passed_along(): return lax.ppermute(block, axis, route)  262 us
    psum x1, blocking collectives, per_device(): overall = lax.psum(local_sq, ('dp', 'ctx', 'tp'))  195 us
    ppermute x80, waiting for transfers between devices, passed_along(): return lax.ppermute(block, axis, route)  72.7 us
    dot_general x4, matrix products, per_item(): jnp.einsum('htw,thd->wd', ds16, q_item, preferred_element_type=jnp.float32)  19.5 us
    slice x34, local copies, waits for them, and re-layouts, per_device(): carried = (moved[0] + grad_window_k[index], moved[1] + grad_window_v[index])  17.2 us
    dot_general x4, matrix products, per_item(): jnp.einsum('htw,thd->wd', prob16, t_item, preferred_element_type=jnp.floa...  16.6 us
  transfers between devices with their start and end apart: 80, of which 42 were waited for; matrix products, arithmetic and copies ran while one was open for 5% of the time, Pallas kernels for 0%

commit v1 on v0

v1 whole, which is shorter than its diff:
```python
import functools
import math

import jax
import jax.numpy as jnp
from jax import lax
from jax.experimental import pallas as pl
from jax.experimental.pallas import tpu as pltpu
from jax.sharding import Mesh
from jax.sharding import PartitionSpec as P

HEADS = 64
KV_HEADS = 8
HEAD = 128
GROUP = HEADS // KV_HEADS
DOC_MAX = 2048

step_size = 0.1
radius_scale = 0.13

BF = jnp.bfloat16
F32 = jnp.float32
NT = (((1,), (1,)), ((), ()))
NN = (((1,), (0,)), ((), ()))
FAR = -1e30


def mm(a, b, dims=NN):
    return lax.dot_general(a, b, dims, preferred_element_type=F32)


def attn_kernel(
    own_rows, side_rows, q_ref, t_ref, own_ref, r1_ref, r2_ref, r3_ref, docs_ref,
    o_ref, gown_ref, g1_ref, g2_ref, g3_ref,
    kaug, vaug, vat, qaug, taug, s_ref, p_ref,
):
    tokens = q_ref.shape[0]
    rows_all = GROUP * tokens
    blocks = [(own_ref, gown_ref, b) for b in range(own_rows)]
    for r, g in ((r1_ref, g1_ref), (r2_ref, g2_ref), (r3_ref, g3_ref)):
        blocks += [(r, g, b) for b in range(side_rows)]
    docs = docs_ref[...]
    docs_sq = jnp.concatenate([docs, jnp.zeros((tokens - docs.shape[0], tokens), F32)], 0)
    doc_cols = docs_sq.T
    doc_row = docs[own_rows - 1 : own_rows, :]
    i_key = lax.broadcasted_iota(jnp.int32, (tokens, tokens), 0)
    i_qry = lax.broadcasted_iota(jnp.int32, (tokens, tokens), 1)
    one = jnp.ones((tokens, HEAD), BF)
    for j, (src, _, b) in enumerate(blocks):
        rows = slice(j * tokens, (j + 1) * tokens)
        kaug[rows, 0:HEAD] = src[b * tokens : (b + 1) * tokens, 0:HEAD]
        v = src[b * tokens : (b + 1) * tokens, HEAD : 2 * HEAD]
        vaug[rows, 0:HEAD] = v
        vaug[rows, HEAD : 2 * HEAD] = one
        vat[0:HEAD, rows] = v.T
        vat[HEAD : 2 * HEAD, rows] = one
        ok = doc_cols[:, j : j + 1] == doc_row
        if j == own_rows - 1:
            ok = ok & (i_key <= i_qry)
        kaug[rows, HEAD : HEAD + tokens] = jnp.where(ok, 0.0, FAR).astype(BF)
    eye = (i_key == i_qry).astype(F32).astype(BF)
    for h in range(GROUP):
        qaug[h * tokens : (h + 1) * tokens, 0:HEAD] = q_ref[:, h * HEAD : (h + 1) * HEAD]
        qaug[h * tokens : (h + 1) * tokens, HEAD : HEAD + tokens] = eye
    top = jnp.full((8, rows_all), -3e38, F32)
    for j in range(len(blocks)):
        rows = slice(j * tokens, (j + 1) * tokens)
        s = mm(kaug[rows, :], qaug[...], NT)
        s_ref[rows, :] = s
        top = jnp.maximum(top, jnp.max(s.reshape(tokens // 8, 8, rows_all), 0))
    top = jnp.max(top, 0, keepdims=True)
    c = math.log2(math.e) / math.sqrt(HEAD)
    for j in range(len(blocks)):
        rows = slice(j * tokens, (j + 1) * tokens)
        p = jnp.exp2((s_ref[rows, :] - top) * c)
        s_ref[rows, :] = p
        p_ref[rows, :] = p.astype(BF)
    lane = lax.broadcasted_iota(jnp.int32, (tokens, HEAD), 1)
    for pair in range(GROUP // 2):
        ot = mm(vat[...], p_ref[:, pair * 2 * tokens : (pair + 1) * 2 * tokens])
        for u in range(2):
            h = 2 * pair + u
            o = ot[:, u * tokens : (u + 1) * tokens].T
            inv = 1.0 / o[:, HEAD:]
            out = o[:, :HEAD] * inv
            o_ref[:, h * HEAD : (h + 1) * HEAD] = out.astype(BF)
            tp = (t_ref[:, h * HEAD : (h + 1) * HEAD].astype(F32) * inv).astype(BF)
            delta = jnp.sum(tp.astype(F32) * out, 1, keepdims=True)
            hi = delta.astype(BF).astype(F32)
            rest = delta - hi
            mid = rest.astype(BF).astype(F32)
            lo = rest - mid
            ext = jnp.where(
                lane == 0, -hi, jnp.where(lane == 1, -mid, jnp.where(lane == 2, -lo, 0.0))
            )
            taug[h * tokens : (h + 1) * tokens, 0:HEAD] = tp
            taug[h * tokens : (h + 1) * tokens, HEAD : 2 * HEAD] = ext.astype(BF)
    scale = 1.0 / math.sqrt(HEAD)
    for j, (_, g, b) in enumerate(blocks):
        rows = slice(j * tokens, (j + 1) * tokens)
        out_rows = slice(b * tokens, (b + 1) * tokens)
        x = mm(vaug[rows, :], taug[...], NT)
        ds = (s_ref[rows, :] * x).astype(BF)
        dk = mm(ds, qaug[:, 0:HEAD]) * scale
        dv = mm(p_ref[rows, :], taug[:, 0:HEAD])
        g[out_rows, 0:HEAD] = dk.astype(g.dtype)
        g[out_rows, HEAD : 2 * HEAD] = dv.astype(g.dtype)


def attention(q, t, own, r1, r2, r3, docs, own_rows, side_rows):
    tokens = q.shape[0]
    kv = q.shape[1] // (GROUP * HEAD)
    keys = (own_rows + 3 * side_rows) * tokens
    rows_all = GROUP * tokens
    wide = pl.BlockSpec((tokens, rows_all), lambda g: (0, g))

    def part(k):
        return pl.BlockSpec((k * tokens, 2 * HEAD), lambda g: (0, g))

    return pl.pallas_call(
        functools.partial(attn_kernel, own_rows, side_rows),
        grid=(kv,),
        in_specs=[wide, wide, part(own_rows)]
        + [part(side_rows)] * 3
        + [pl.BlockSpec(docs.shape, lambda g: (0, 0))],
        out_specs=[wide, part(own_rows)] + [part(side_rows)] * 3,
        out_shape=[
            jax.ShapeDtypeStruct((tokens, kv * rows_all), BF),
            jax.ShapeDtypeStruct((own_rows * tokens, kv * 2 * HEAD), F32),
        ]
        + [jax.ShapeDtypeStruct((side_rows * tokens, kv * 2 * HEAD), BF)] * 3,
        scratch_shapes=[
            pltpu.VMEM((keys, 2 * HEAD), BF),
            pltpu.VMEM((keys, 2 * HEAD), BF),
            pltpu.VMEM((2 * HEAD, keys), BF),
            pltpu.VMEM((rows_all, 2 * HEAD), BF),
            pltpu.VMEM((rows_all, 2 * HEAD), BF),
            pltpu.VMEM((keys, rows_all), F32),
            pltpu.VMEM((keys, rows_all), BF),
        ],
        compiler_params=pltpu.CompilerParams(vmem_limit_bytes=50 << 20),
        cost_estimate=pl.CostEstimate(
            flops=kv * keys * rows_all * HEAD * 10,
            bytes_accessed=8 << 20,
            transcendentals=kv * keys * rows_all,
        ),
    )(q, t, own, r1, r2, r3, docs)


def along_z(x, d):
    n = lax.axis_size("cz")
    return lax.ppermute(x, "cz", [(i - d, i) for i in range(n) if 0 <= i - d < n])


def along_x(x, d):
    n = lax.axis_size("cx")
    return lax.ppermute(x, "cx", [((i - d) % n, i) for i in range(n)])


def sum_among(x, axes):
    n = math.prod(lax.axis_size(a) for a in axes)
    return lax.all_to_all(jnp.broadcast_to(x[None], (n,) + x.shape), axes, 0, 0)


def per_device(query, key, value, key_shift, value_shift, doc_ids, target):
    tokens = query.shape[1]
    kv_local = key.shape[2] // HEAD
    far_rows = 4
    where_x = lax.axis_index("cx")
    key_new = (key[0].astype(F32) + key_shift[0]).astype(BF)
    val_new = (value[0].astype(F32) + value_shift[0]).astype(BF)
    lanes = []
    for h in range(kv_local):
        lanes += [key_new[:, h * HEAD : (h + 1) * HEAD], val_new[:, h * HEAD : (h + 1) * HEAD]]
    kv = jnp.concatenate(lanes, 1)
    width = kv.shape[1]
    docs = (doc_ids[0] + 1).astype(BF)[None, :]
    tail = jnp.pad(docs, ((0, 7), (0, width - tokens)))
    row = [jnp.concatenate([kv, tail], 0)]
    for k in range(1, far_rows + 1):
        row.append(along_z(row[0], k))
    keys_of = [r[:tokens] for r in row]
    docs_of = [r[tokens : tokens + 1] for r in row]
    sides = []
    for d in (1, 2, 3):
        ahead = where_x + d < lax.axis_size("cx")
        first = jnp.where(ahead, keys_of[0], keys_of[4])
        first_doc = jnp.where(ahead, docs_of[0], docs_of[4])
        pad = jnp.zeros((4, width), BF)
        sent = jnp.concatenate(
            [first, keys_of[3], keys_of[2], keys_of[1], first_doc, docs_of[3], docs_of[2], docs_of[1], pad], 0
        )
        sides.append(along_x(sent, d))
    own = jnp.concatenate([keys_of[4], keys_of[3], keys_of[2], keys_of[1], keys_of[0]], 0)
    docs_all = jnp.concatenate(
        [docs_of[4], docs_of[3], docs_of[2], docs_of[1], docs_of[0]]
        + [s[4 * tokens : 4 * tokens + 4] for s in sides],
        0,
    )[:, :tokens].astype(F32)
    docs_all = jnp.pad(docs_all, ((0, 32 - docs_all.shape[0]), (0, 0)))
    attn, gown, g1, g2, g3 = attention(
        query[0], target[0], own, sides[0], sides[1], sides[2], docs_all, 5, 4
    )
    back = [along_x(g, -d) for d, g in ((1, g1), (2, g2), (3, g3))]

    def piece(x, i):
        return x[i * tokens : (i + 1) * tokens].astype(F32)

    total = [None] * 5
    for k in (1, 2, 3):
        total[k] = piece(gown, 4 - k) + sum(piece(b, 4 - k) for b in back)
    total[0] = piece(gown, 4)
    total[4] = piece(gown, 0)
    for d, b in zip((1, 2, 3), back):
        ahead = where_x + d < lax.axis_size("cx")
        total[0] = total[0] + jnp.where(ahead, piece(b, 0), 0.0)
        total[4] = total[4] + jnp.where(ahead, 0.0, piece(b, 0))
    grad = total[0]
    for k in range(1, far_rows + 1):
        grad = grad + along_z(total[k].astype(BF), -k).astype(F32)
    grad_key = jnp.concatenate(
        [grad[:, 2 * h * HEAD : (2 * h + 1) * HEAD] for h in range(kv_local)], 1
    )
    grad_val = jnp.concatenate(
        [grad[:, (2 * h + 1) * HEAD : (2 * h + 2) * HEAD] for h in range(kv_local)], 1
    )
    ks, vs = key_shift[0], value_shift[0]
    sums = jnp.stack(
        [
            jnp.sum(ks * ks, -1) + jnp.sum(vs * vs, -1),
            jnp.sum(ks * grad_key, -1) + jnp.sum(vs * grad_val, -1),
            jnp.sum(grad_key * grad_key, -1) + jnp.sum(grad_val * grad_val, -1),
        ]
    )
    n_dp, n_x, n_tp = lax.axis_size("dp"), lax.axis_size("cx"), lax.axis_size("tp")
    plane = sum_among(sums, ("dp", "cx", "tp"))
    near = jnp.sum(
        lax.dynamic_slice_in_dim(
            plane, (lax.axis_index("dp") * n_x + where_x) * n_tp, n_tp, 0
        ),
        0,
    )
    square = jnp.sum(plane[:, 2])
    overall = jnp.sum(sum_among(jnp.full((1, 128), square), ("cz",))[:, 0, 0])
    count = n_dp * tokens * n_x * lax.axis_size("cz") * 2 * KV_HEADS * HEAD
    rms = jnp.sqrt(overall / count + 1e-05)
    a = step_size / rms
    size_sq = jnp.maximum(near[0] + 2.0 * a * near[1] + a * a * near[2], 0.0)
    radius = radius_scale * math.sqrt(2 * KV_HEADS * HEAD)
    factor = jnp.minimum(1.0, radius / jnp.sqrt(size_sq + 1e-06))[:, None]
    return (
        attn[None],
        ((ks + a * grad_key) * factor)[None],
        ((vs + a * grad_val) * factor)[None],
    )


def solution(mesh):
    sizes = mesh.devices.shape
    inner = Mesh(
        mesh.devices.reshape(sizes[0], sizes[1] // 4, 4, sizes[2]), ("dp", "cz", "cx", "tp")
    )
    whole = P("dp", ("cz", "cx"), "tp")
    in_specs = (whole,) * 5 + (P("dp", ("cz", "cx")), whole)
    return jax.shard_map(
        per_device, mesh=inner, in_specs=in_specs, out_specs=(whole,) * 3, check_vma=False
    )
```

time: 668 us -> 208 us (0.31)
  starting transfers between devices: 262 us -> 60.4 us
  blocking collectives: 203 us -> 15 us
  matrix products: 49.6 us -> 0 us
  local copies, waits for them, and re-layouts: 41.3 us -> 6.66 us
  Pallas kernels: 0 us -> 24.9 us
  other arithmetic: 31.1 us -> 8.33 us
  waiting for transfers between devices: 72.7 us -> 90.1 us
    ppermute x80 -> x14, starting transfers between devices: 262 us -> 47.2 us  [the longest x8 29.1 us: along_z(): lax.ppermute(x, 'cz', [(i - d, i) for i in range(n) if 0 <= i - d < n])]
    psum x2 -> x0, blocking collectives: 203 us -> none  [the longest x1 195 us: per_device(): overall = lax.psum(local_sq, ('dp', 'ctx', 'tp'))]
    dot_general x16 -> x0, matrix products: 49.6 us -> none  [the longest x4 19.5 us: per_item(): jnp.einsum('htw,thd->wd', ds16, q_item, preferred_element_type=jnp.float32)]
    pallas_call x0 -> x1, Pallas kernels: none -> 24.9 us  [attention(): pl.pallas_call(functools.partial(attn_kernel, own_rows, side_rows), grid=...]
    slice x38 -> x12, local copies, waits for them, and re-layouts: 19.3 us -> 0.83 us  [the longest x3 0.71 us: per_device(): s[4 * tokens:4 * tokens + 4]]
    all_to_all x0 -> x1, blocking collectives: none -> 15 us  [sum_among(): return lax.all_to_all(jnp.broadcast_to(x[None], (n,) + x.shape), axes, 0, 0)]
    all_to_all x0 -> x1, starting transfers between devices: none -> 13.2 us  [sum_among(): return lax.all_to_all(jnp.broadcast_to(x[None], (n,) + x.shape), axes, 0, 0)]
    and x4 -> x0, other arithmetic: 12.7 us -> none  [per_device(): (window_docs[None, :] == own_docs[:, None]) & (key_pos[None, :] <= query_...]
  transfers between devices with their start and end apart: 80 -> 15, of which waited for: 42 -> 9; matrix products, arithmetic and copies ran while one was open for 5% -> 2% of each run, Pallas kernels for 0% -> 0%
where the time goes in v1:
time: 208 us; the launch traced here: 207 us
  waiting for transfers between devices  90.1 us (43%)
  starting transfers between devices  60.4 us (29%)
  Pallas kernels  24.9 us (12%)
  blocking collectives  15 us (7%)
  other arithmetic  8.33 us (4%)
  local copies, waits for them, and re-layouts  6.66 us (3%)
    ppermute x8, waiting for transfers between devices, along_z(): lax.ppermute(x, 'cz', [(i - d, i) for i in range(n) if 0 <= i - d < n])  43.1 us
    ppermute x6, waiting for transfers between devices, along_x(): return lax.ppermute(x, 'cx', [((i - d) % n, i) for i in range(n)])  35.8 us
    ppermute x8, starting transfers between devices, along_z(): lax.ppermute(x, 'cz', [(i - d, i) for i in range(n) if 0 <= i - d < n])  29.1 us
    pallas_call x1, Pallas kernels, attention(): pl.pallas_call(functools.partial(attn_kernel, own_rows, side_rows), grid=...  24.9 us
    ppermute x6, starting transfers between devices, along_x(): return lax.ppermute(x, 'cx', [((i - d) % n, i) for i in range(n)])  18.1 us
    all_to_all x1, blocking collectives, sum_among(): return lax.all_to_all(jnp.broadcast_to(x[None], (n,) + x.shape), axes, 0, 0)  15 us
    all_to_all x1, starting transfers between devices, sum_among(): return lax.all_to_all(jnp.broadcast_to(x[None], (n,) + x.shape), axes, 0, 0)  13.2 us
    all_to_all x1, waiting for transfers between devices, sum_among(): return lax.all_to_all(jnp.broadcast_to(x[None], (n,) + x.shape), axes, 0, 0)  11.2 us
  transfers between devices with their start and end apart: 15, of which 9 were waited for; matrix products, arithmetic and copies ran while one was open for 2% of the time, Pallas kernels for 0%

profile of v1, /device:TPU:1, one launch (start us, length us, event | category | flops | bytes accessed | tf_op | source)
XLA Modules:
  0.0 207.1 jit_solution(5221679326534914709)
XLA Ops:
  0.6 0.7 add_convert_fusion.3
  1.3 0.9 fusion.16
  2.2 0.9 fusion.15
  3.2 4.4 %collective-permute-start.3 = (bf16[136,512]{1,0:T(8,128)(2,1)S(1)}, bf16[136,512]{1,0:T(8,128)(2,1)S(1)}, u32[]{:S(2)}, u32[]{:S(2)}) collective-permute-start(bf16[136,512]{1,0:T(8,128)(2,1)S(1)} %pad_maximum_fusion), channel_id=1, source_target_pairs={{0,16},{16,32},{32,48},{48,64},{64,80},{80,96},{96,112},{112,128},... | collective-permute-start | bytes 417800 | tf_op jit(solution)/shard_map/ppermute | solution.py:152
  7.6 4.9 %collective-permute-start.2 = (bf16[136,512]{1,0:T(8,128)(2,1)S(1)}, bf16[136,512]{1,0:T(8,128)(2,1)S(1)}, u32[]{:S(2)}, u32[]{:S(2)}) collective-permute-start(bf16[136,512]{1,0:T(8,128)(2,1)S(1)} %pad_maximum_fusion), channel_id=1, source_target_pairs={{0,32},{16,48},{32,64},{48,80},{64,96},{80,112},{96,128},{112,144}... | collective-permute-start | bytes 417800 | tf_op jit(solution)/shard_map/ppermute | solution.py:152
  12.5 8.8 %collective-permute-start = (bf16[136,512]{1,0:T(8,128)(2,1)S(1)}, bf16[136,512]{1,0:T(8,128)(2,1)S(1)}, u32[]{:S(2)}, u32[]{:S(2)}) collective-permute-start(bf16[136,512]{1,0:T(8,128)(2,1)S(1)} %pad_maximum_fusion), channel_id=1, source_target_pairs={{0,64},{16,80},{32,96},{48,112},{64,128},{80,144},{96,160},{112,17... | collective-permute-start | bytes 417800 | tf_op jit(solution)/shard_map/ppermute | solution.py:152
  21.3 5.7 %collective-permute-start.1 = (bf16[136,512]{1,0:T(8,128)(2,1)S(1)}, bf16[136,512]{1,0:T(8,128)(2,1)S(1)}, u32[]{:S(2)}, u32[]{:S(2)}) collective-permute-start(bf16[136,512]{1,0:T(8,128)(2,1)S(1)} %pad_maximum_fusion), channel_id=1, source_target_pairs={{0,48},{16,64},{32,80},{48,96},{64,112},{80,128},{96,144},{112,160... | collective-permute-start | bytes 417800 | tf_op jit(solution)/shard_map/ppermute | solution.py:152
  27.0 0.0 collective-permute-done.3
  27.0 0.0 collective-permute-done.2
  27.1 0.0 collective-permute-done
  27.1 0.1 broadcast_select_fusion
  27.2 1.9 collective-permute-done.1
  29.1 0.0 copy-start.4
  29.1 0.9 copy-done.4
  30.0 0.1 concatenate.58
  30.1 0.0 copy-start
  30.1 0.0 copy-start.1
  30.1 4.5 %collective-permute-start.6 = (bf16[520,512]{1,0:T(8,128)(2,1)S(1)}, bf16[520,512]{1,0:T(8,128)(2,1)}, u32[]{:S(2)}, u32[]{:S(2)}) collective-permute-start(bf16[520,512]{1,0:T(8,128)(2,1)S(1)} %concatenate.58), channel_id=1, source_target_pairs={{4,0},{8,4},{12,8},{0,12},{5,1},{9,5},{13,9},{1,13},{6,2},{10,6},{... | collective-permute-start | bytes 1597448 | tf_op jit(solution)/shard_map/ppermute | solution.py:157
  34.6 0.1 concatenate.56
  34.7 1.9 collective-permute-start.4
  36.6 3.3 %concatenate.57 = bf16[520,512]{1,0:T(8,128)(2,1)} concatenate(bf16[128,512]{1,0:T(8,128)(2,1)S(1)} %get-tuple-element.25, bf16[128,512]{1,0:T(8,128)(2,1)S(1)} %get-tuple-element.43, bf16[128,512]{1,0:T(8,128)(2,1)S(1)} %get-tuple-element.41, bf16[128,512]{1,0:T(8,128)(2,1)S(1)} %get-tuple-element.39, bf16[1,512]{1,0:T(2,128)(2,1)S(1)} %get-tuple-element.36, ...), dimensions={0} | concatenate | bytes 1064960 | tf_op jit(solution)/shard_map/concatenate | solution.py:190
  39.9 3.6 %collective-permute-start.5 = (bf16[520,512]{1,0:T(8,128)(2,1)}, bf16[520,512]{1,0:T(8,128)(2,1)S(1)}, u32[]{:S(2)}, u32[]{:S(2)}) collective-permute-start(bf16[520,512]{1,0:T(8,128)(2,1)} %concatenate.57), channel_id=1, source_target_pairs={{8,0},{12,4},{0,8},{4,12},{9,1},{13,5},{1,9},{5,13},{10,2},{14,6},... | collective-permute-start | bytes 1597448 | tf_op jit(solution)/shard_map/ppermute | solution.py:157
  43.5 0.7 constant_dynamic-update-slice_fusion.own_ref
  44.2 0.0 collective-permute-done.6.r3_ref
  44.2 0.7 slice.189
  44.9 4.8 %collective-permute-done.4.r1_ref = bf16[520,512]{1,0:T(8,128)(2,1)S(1)} collective-permute-done((bf16[520,512]{1,0:T(8,128)(2,1)S(1)}, bf16[520,512]{1,0:T(8,128)(2,1)S(1)}, u32[]{:S(2)}, u32[]{:S(2)}) %collective-permute-start.4) | collective-permute-done | bytes 532512 | tf_op jit(solution)/shard_map/ppermute | solution.py:157
  49.7 9.6 %collective-permute-done.5.r2_ref = bf16[520,512]{1,0:T(8,128)(2,1)S(1)} collective-permute-done((bf16[520,512]{1,0:T(8,128)(2,1)}, bf16[520,512]{1,0:T(8,128)(2,1)S(1)}, u32[]{:S(2)}, u32[]{:S(2)}) %collective-permute-start.5) | collective-permute-done | bytes 532512 | tf_op jit(solution)/shard_map/ppermute | solution.py:157
  59.3 0.2 concatenate.59
  59.5 0.0 copy-done
  59.5 0.0 copy-done.1
  59.5 24.9 %shard_map.94 = (bf16[128,2048]{1,0:T(8,128)(2,1)}, f32[640,512]{1,0:T(8,128)}, bf16[512,512]{1,0:T(8,128)(2,1)S(1)}, bf16[512,512]{1,0:T(8,128)(2,1)S(1)}, bf16[512,512]{1,0:T(8,128)(2,1)S(1)}) custom-call(bf16[128,2048]{1,0:T(8,128)(2,1)S(1)} %bitcast.42, bf16[128,2048]{1,0:T(8,128)(2,1)S(1)} %bitcast.43, ...), custom_call_target="tpu_custom_call" | custom-call | flops 5704253440 | bytes 8388608 | tf_op jit(solution)/shard_map/pallas_call | solution.py:120
  84.5 1.9 collective-permute-start.7
  86.4 3.4 %collective-permute-start.8 = (bf16[512,512]{1,0:T(8,128)(2,1)S(1)}, bf16[512,512]{1,0:T(8,128)(2,1)S(1)}, u32[]{:S(2)}, u32[]{:S(2)}) collective-permute-start(bf16[512,512]{1,0:T(8,128)(2,1)S(1)} %get-tuple-element.11), channel_id=1, source_target_pairs={{8,0},{12,4},{0,8},{4,12},{9,1},{13,5},{1,9},{5,13},{10,2},{14,6},... | collective-permute-start | bytes 1572872 | tf_op jit(solution)/shard_map/ppermute | solution.py:157
  89.8 2.8 %collective-permute-start.9 = (bf16[512,512]{1,0:T(8,128)(2,1)S(1)}, bf16[512,512]{1,0:T(8,128)(2,1)S(1)}, u32[]{:S(2)}, u32[]{:S(2)}) collective-permute-start(bf16[512,512]{1,0:T(8,128)(2,1)S(1)} %get-tuple-element.12), channel_id=1, source_target_pairs={{12,0},{0,4},{4,8},{8,12},{13,1},{1,5},{5,9},{9,13},{14,2},{2,6},{... | collective-permute-start | bytes 1572872 | tf_op jit(solution)/shard_map/ppermute | solution.py:157
  92.6 2.8 %collective-permute-done.7 = bf16[512,512]{1,0:T(8,128)(2,1)S(1)} collective-permute-done((bf16[512,512]{1,0:T(8,128)(2,1)S(1)}, bf16[512,512]{1,0:T(8,128)(2,1)S(1)}, u32[]{:S(2)}, u32[]{:S(2)}) %collective-permute-start.7) | collective-permute-done | bytes 524320 | tf_op jit(solution)/shard_map/ppermute | solution.py:157
  95.3 3.5 %collective-permute-done.8 = bf16[512,512]{1,0:T(8,128)(2,1)S(1)} collective-permute-done((bf16[512,512]{1,0:T(8,128)(2,1)S(1)}, bf16[512,512]{1,0:T(8,128)(2,1)S(1)}, u32[]{:S(2)}, u32[]{:S(2)}) %collective-permute-start.8) | collective-permute-done | bytes 524320 | tf_op jit(solution)/shard_map/ppermute | solution.py:157
  98.8 15.2 %collective-permute-done.9 = bf16[512,512]{1,0:T(8,128)(2,1)S(1)} collective-permute-done((bf16[512,512]{1,0:T(8,128)(2,1)S(1)}, bf16[512,512]{1,0:T(8,128)(2,1)S(1)}, u32[]{:S(2)}, u32[]{:S(2)}) %collective-permute-start.9) | collective-permute-done | bytes 524320 | tf_op jit(solution)/shard_map/ppermute | solution.py:157
  114.0 1.5 add_convert_fusion.2
  115.6 0.0 copy-start.3
  115.6 0.0 copy-start.2
  115.6 1.4 collective-permute-start.10
  117.0 1.3 collective-permute-start.13
  118.3 1.3 collective-permute-start.12
  119.6 1.3 collective-permute-start.11
  120.9 8.6 %collective-permute-done.10 = bf16[128,512]{1,0:T(8,128)(2,1)S(1)} collective-permute-done((bf16[128,512]{1,0:T(8,128)(2,1)S(1)}, bf16[128,512]{1,0:T(8,128)(2,1)S(1)}, u32[]{:S(2)}, u32[]{:S(2)}) %collective-permute-start.10) | collective-permute-done | bytes 131104 | tf_op jit(solution)/shard_map/ppermute | solution.py:152
  129.5 32.6 %collective-permute-done.13 = bf16[128,512]{1,0:T(8,128)(2,1)S(1)} collective-permute-done((bf16[128,512]{1,0:T(8,128)(2,1)S(1)}, bf16[128,512]{1,0:T(8,128)(2,1)S(1)}, u32[]{:S(2)}, u32[]{:S(2)}) %collective-permute-start.13) | collective-permute-done | bytes 131104 | tf_op jit(solution)/shard_map/ppermute | solution.py:152
  162.2 0.0 collective-permute-done.12
  162.2 0.0 collective-permute-done.11
  162.2 1.1 fusion.6
  163.3 0.0 copy-done.3
  163.3 0.1 fusion.17
  163.5 0.0 copy-done.2
  163.5 0.1 fusion.19
  163.7 15.0 %all_to_all.10 = f32[32,3,128]{2,1,0:T(4,128)S(1)} all-to-all(f32[32,3,128]{2,1,0:T(4,128)S(1)} %broadcast_in_dim.25), channel_id=1, replica_groups=mesh['dp'=2,'cz'=16,'cx'=4,'tp'=4] {'dp','cx','tp'}, dimensions={0} | all-to-all | bytes 98304 | tf_op jit(solution)/shard_map/all_to_all | solution.py:162
  178.7 0.6 reduce_sum.87
  179.3 1.2 broadcast_in_dim_broadcast_in_dim_broadcast_in_dim.3
  180.6 13.2 %all-to-all-start.1 = ((f32[16,1,128]{2,1,0:T(1,128)}), f32[16,1,128]{2,1,0:T(1,128)S(1)}, u32[]{:S(2)}, u32[]{:S(2)}) async-start(f32[16,1,128]{2,1,0:T(1,128)} %broadcast_in_dim_broadcast_in_dim_broadcast_in_dim.3), calls=%async_computation.1 | async-start | bytes 16384 | tf_op jit(solution)/shard_map/all_to_all | solution.py:162
  193.8 11.2 %all-to-all-done.1 = f32[16,1,128]{2,1,0:T(1,128)S(1)} async-done(((f32[16,1,128]{2,1,0:T(1,128)}), f32[16,1,128]{2,1,0:T(1,128)S(1)}, u32[]{:S(2)}, u32[]{:S(2)}) %all-to-all-start.1) | async-done | bytes 8224 | tf_op jit(solution)/shard_map/all_to_all | solution.py:162
  205.0 0.6 slice_reduce_fusion
  206.3 0.8 fusion.14
  (24 shorter events, 0.3 us)
Async XLA Ops:
  3.2 23.8 %collective-permute-start.3 = (bf16[136,512]{1,0:T(8,128)(2,1)S(1)}, bf16[136,512]{1,0:T(8,128)(2,1)S(1)}, u32[]{:S(2)}, u32[]{:S(2)}) collective-permute-start(bf16[136,512]{1,0:T(8,128)(2,1)S(1)} %pad_maximum_fusion), channel_id=1, source_target_pairs={{0,16},{16,32},{32,48},{48,64},{64,80},{80,96},{96,112},{112,128},... | collective-permute-start | bytes 417800 | tf_op jit(solution)/shard_map/ppermute | solution.py:152
  7.6 19.4 %collective-permute-start.2 = (bf16[136,512]{1,0:T(8,128)(2,1)S(1)}, bf16[136,512]{1,0:T(8,128)(2,1)S(1)}, u32[]{:S(2)}, u32[]{:S(2)}) collective-permute-start(bf16[136,512]{1,0:T(8,128)(2,1)S(1)} %pad_maximum_fusion), channel_id=1, source_target_pairs={{0,32},{16,48},{32,64},{48,80},{64,96},{80,112},{96,128},{112,144}... | collective-permute-start | bytes 417800 | tf_op jit(solution)/shard_map/ppermute | solution.py:152
  12.5 14.6 %collective-permute-start = (bf16[136,512]{1,0:T(8,128)(2,1)S(1)}, bf16[136,512]{1,0:T(8,128)(2,1)S(1)}, u32[]{:S(2)}, u32[]{:S(2)}) collective-permute-start(bf16[136,512]{1,0:T(8,128)(2,1)S(1)} %pad_maximum_fusion), channel_id=1, source_target_pairs={{0,64},{16,80},{32,96},{48,112},{64,128},{80,144},{96,160},{112,17... | collective-permute-start | bytes 417800 | tf_op jit(solution)/shard_map/ppermute | solution.py:152
  21.3 7.7 %collective-permute-start.1 = (bf16[136,512]{1,0:T(8,128)(2,1)S(1)}, bf16[136,512]{1,0:T(8,128)(2,1)S(1)}, u32[]{:S(2)}, u32[]{:S(2)}) collective-permute-start(bf16[136,512]{1,0:T(8,128)(2,1)S(1)} %pad_maximum_fusion), channel_id=1, source_target_pairs={{0,48},{16,64},{32,80},{48,96},{64,112},{80,128},{96,144},{112,160... | collective-permute-start | bytes 417800 | tf_op jit(solution)/shard_map/ppermute | solution.py:152
  29.1 0.9 copy-start.4
  30.1 29.5 %copy-start = (bf16[1,128,2048]{2,1,0:T(8,128)(2,1)S(1)}, bf16[1,128,2048]{2,1,0:T(8,128)(2,1)}, u32[]{:S(2)}) copy-start(bf16[1,128,2048]{2,1,0:T(8,128)(2,1)} %param.7) | copy-start | bytes 1572868
  30.1 29.5 %copy-start.1 = (bf16[1,128,2048]{2,1,0:T(8,128)(2,1)S(1)}, bf16[1,128,2048]{2,1,0:T(8,128)(2,1)}, u32[]{:S(2)}) copy-start(bf16[1,128,2048]{2,1,0:T(8,128)(2,1)} %param.13) | copy-start | bytes 1572868
  30.1 14.1 %collective-permute-start.6 = (bf16[520,512]{1,0:T(8,128)(2,1)S(1)}, bf16[520,512]{1,0:T(8,128)(2,1)}, u32[]{:S(2)}, u32[]{:S(2)}) collective-permute-start(bf16[520,512]{1,0:T(8,128)(2,1)S(1)} %concatenate.58), channel_id=1, source_target_pairs={{4,0},{8,4},{12,8},{0,12},{5,1},{9,5},{13,9},{1,13},{6,2},{10,6},{... | collective-permute-start | bytes 1597448 | tf_op jit(solution)/shard_map/ppermute | solution.py:157
  34.7 15.0 %collective-permute-start.4 = (bf16[520,512]{1,0:T(8,128)(2,1)S(1)}, bf16[520,512]{1,0:T(8,128)(2,1)S(1)}, u32[]{:S(2)}, u32[]{:S(2)}) collective-permute-start(bf16[520,512]{1,0:T(8,128)(2,1)S(1)} %concatenate.56), channel_id=1, source_target_pairs={{12,0},{0,4},{4,8},{8,12},{13,1},{1,5},{5,9},{9,13},{14,2},{2,6},{... | collective-permute-start | bytes 1597448 | tf_op jit(solution)/shard_map/ppermute | solution.py:157
  39.9 19.4 %collective-permute-start.5 = (bf16[520,512]{1,0:T(8,128)(2,1)}, bf16[520,512]{1,0:T(8,128)(2,1)S(1)}, u32[]{:S(2)}, u32[]{:S(2)}) collective-permute-start(bf16[520,512]{1,0:T(8,128)(2,1)} %concatenate.57), channel_id=1, source_target_pairs={{8,0},{12,4},{0,8},{4,12},{9,1},{13,5},{1,9},{5,13},{10,2},{14,6},... | collective-permute-start | bytes 1597448 | tf_op jit(solution)/shard_map/ppermute | solution.py:157
  84.5 10.9 %collective-permute-start.7 = (bf16[512,512]{1,0:T(8,128)(2,1)S(1)}, bf16[512,512]{1,0:T(8,128)(2,1)S(1)}, u32[]{:S(2)}, u32[]{:S(2)}) collective-permute-start(bf16[512,512]{1,0:T(8,128)(2,1)S(1)} %get-tuple-element.10), channel_id=1, source_target_pairs={{4,0},{8,4},{12,8},{0,12},{5,1},{9,5},{13,9},{1,13},{6,2},{10,6},{... | collective-permute-start | bytes 1572872 | tf_op jit(solution)/shard_map/ppermute | solution.py:157
  86.4 12.4 %collective-permute-start.8 = (bf16[512,512]{1,0:T(8,128)(2,1)S(1)}, bf16[512,512]{1,0:T(8,128)(2,1)S(1)}, u32[]{:S(2)}, u32[]{:S(2)}) collective-permute-start(bf16[512,512]{1,0:T(8,128)(2,1)S(1)} %get-tuple-element.11), channel_id=1, source_target_pairs={{8,0},{12,4},{0,8},{4,12},{9,1},{13,5},{1,9},{5,13},{10,2},{14,6},... | collective-permute-start | bytes 1572872 | tf_op jit(solution)/shard_map/ppermute | solution.py:157
  89.8 24.2 %collective-permute-start.9 = (bf16[512,512]{1,0:T(8,128)(2,1)S(1)}, bf16[512,512]{1,0:T(8,128)(2,1)S(1)}, u32[]{:S(2)}, u32[]{:S(2)}) collective-permute-start(bf16[512,512]{1,0:T(8,128)(2,1)S(1)} %get-tuple-element.12), channel_id=1, source_target_pairs={{12,0},{0,4},{4,8},{8,12},{13,1},{1,5},{5,9},{9,13},{14,2},{2,6},{... | collective-permute-start | bytes 1572872 | tf_op jit(solution)/shard_map/ppermute | solution.py:157
  115.6 47.8 %copy-start.3 = (f32[1,128,256]{2,1,0:T(8,128)S(1)}, f32[1,128,256]{2,1,0:T(8,128)}, u32[]{:S(2)}) copy-start(f32[1,128,256]{2,1,0:T(8,128)} %param.11) | copy-start | bytes 393220
  115.6 47.9 %copy-start.2 = (f32[1,128,256]{2,1,0:T(8,128)S(1)}, f32[1,128,256]{2,1,0:T(8,128)}, u32[]{:S(2)}) copy-start(f32[1,128,256]{2,1,0:T(8,128)} %param.10) | copy-start | bytes 393220
  115.6 13.9 %collective-permute-start.10 = (bf16[128,512]{1,0:T(8,128)(2,1)S(1)}, bf16[128,512]{1,0:T(8,128)(2,1)S(1)}, u32[]{:S(2)}, u32[]{:S(2)}) collective-permute-start(bf16[128,512]{1,0:T(8,128)(2,1)S(1)} %get-tuple-element.19), channel_id=1, source_target_pairs={{16,0},{32,16},{48,32},{64,48},{80,64},{96,80},{112,96},{128,112},... | collective-permute-start | bytes 393224 | tf_op jit(solution)/shard_map/ppermute | solution.py:152
  117.0 45.1 %collective-permute-start.13 = (bf16[128,512]{1,0:T(8,128)(2,1)S(1)}, bf16[128,512]{1,0:T(8,128)(2,1)S(1)}, u32[]{:S(2)}, u32[]{:S(2)}) collective-permute-start(bf16[128,512]{1,0:T(8,128)(2,1)S(1)} %get-tuple-element.20), channel_id=1, source_target_pairs={{64,0},{80,16},{96,32},{112,48},{128,64},{144,80},{160,96},{176,11... | collective-permute-start | bytes 393224 | tf_op jit(solution)/shard_map/ppermute | solution.py:152
  118.3 43.8 %collective-permute-start.12 = (bf16[128,512]{1,0:T(8,128)(2,1)S(1)}, bf16[128,512]{1,0:T(8,128)(2,1)S(1)}, u32[]{:S(2)}, u32[]{:S(2)}) collective-permute-start(bf16[128,512]{1,0:T(8,128)(2,1)S(1)} %get-tuple-element.21), channel_id=1, source_target_pairs={{48,0},{64,16},{80,32},{96,48},{112,64},{128,80},{144,96},{160,112... | collective-permute-start | bytes 393224 | tf_op jit(solution)/shard_map/ppermute | solution.py:152
  119.6 42.5 %collective-permute-start.11 = (bf16[128,512]{1,0:T(8,128)(2,1)S(1)}, bf16[128,512]{1,0:T(8,128)(2,1)S(1)}, u32[]{:S(2)}, u32[]{:S(2)}) collective-permute-start(bf16[128,512]{1,0:T(8,128)(2,1)S(1)} %get-tuple-element.22), channel_id=1, source_target_pairs={{32,0},{48,16},{64,32},{80,48},{96,64},{112,80},{128,96},{144,112}... | collective-permute-start | bytes 393224 | tf_op jit(solution)/shard_map/ppermute | solution.py:152
  180.6 24.5 %all-to-all-start.1 = ((f32[16,1,128]{2,1,0:T(1,128)}), f32[16,1,128]{2,1,0:T(1,128)S(1)}, u32[]{:S(2)}, u32[]{:S(2)}) async-start(f32[16,1,128]{2,1,0:T(1,128)} %broadcast_in_dim_broadcast_in_dim_broadcast_in_dim.3), calls=%async_computation.1 | async-start | bytes 16384 | tf_op jit(solution)/shard_map/all_to_all | solution.py:162

commit v2 on v1

v2 whole, which is shorter than its diff:
```python
import functools
import math

import jax
import jax.numpy as jnp
from jax import lax
from jax.experimental import pallas as pl
from jax.experimental.pallas import tpu as pltpu
from jax.sharding import Mesh
from jax.sharding import PartitionSpec as P

HEADS = 64
KV_HEADS = 8
HEAD = 128
GROUP = HEADS // KV_HEADS
DOC_MAX = 2048

step_size = 0.1
radius_scale = 0.13

BF = jnp.bfloat16
F32 = jnp.float32
NT = (((1,), (1,)), ((), ()))
NN = (((1,), (0,)), ((), ()))
FAR = -1e30
ROWS = 4
HEADS_AT_ONCE = 1


def mm(a, b, dims=NN):
    return lax.dot_general(a, b, dims, preferred_element_type=F32)


def attn_kernel(
    q_ref, t_ref, win_ref, own_ref, _, o_ref, gwin_ref, gown_ref,
    kaug, vaug, vat, qaug, taug, s_ref, p_ref,
):
    tokens = q_ref.shape[0]
    rows_all = GROUP * tokens
    blocks = []
    for x in range(win_ref.shape[0]):
        for b in range(ROWS):
            blocks.append((win_ref.at[x], gwin_ref.at[x], b * tokens, ROWS * tokens + 8 * b))
    blocks.append((own_ref, gown_ref, 0, tokens))
    docs = jnp.concatenate([src[d : d + 1, 0:tokens] for src, _, _, d in blocks], 0).astype(F32)
    docs_sq = jnp.concatenate([docs, jnp.zeros((tokens - docs.shape[0], tokens), F32)], 0)
    doc_cols = docs_sq.T
    doc_row = docs[len(blocks) - 1 :, :]
    i_key = lax.broadcasted_iota(jnp.int32, (tokens, tokens), 0)
    i_qry = lax.broadcasted_iota(jnp.int32, (tokens, tokens), 1)
    one = jnp.ones((tokens, HEAD), BF)
    for j, (src, _, b, _) in enumerate(blocks):
        rows = slice(j * tokens, (j + 1) * tokens)
        kaug[rows, 0:HEAD] = src[b : b + tokens, 0:HEAD]
        v = src[b : b + tokens, HEAD : 2 * HEAD]
        vaug[rows, 0:HEAD] = v
        vaug[rows, HEAD : 2 * HEAD] = one
        vat[0:HEAD, rows] = v.T
        vat[HEAD : 2 * HEAD, rows] = one
        ok = doc_cols[:, j : j + 1] == doc_row
        if j == len(blocks) - 1:
            ok = ok & (i_key <= i_qry)
        kaug[rows, HEAD : HEAD + tokens] = jnp.where(ok, 0.0, FAR).astype(BF)
    eye = (i_key == i_qry).astype(F32).astype(BF)
    for h in range(GROUP):
        qaug[h * tokens : (h + 1) * tokens, 0:HEAD] = q_ref[:, h * HEAD : (h + 1) * HEAD]
        qaug[h * tokens : (h + 1) * tokens, HEAD : HEAD + tokens] = eye
    top = jnp.full((8, rows_all), -3e38, F32)
    for j in range(len(blocks)):
        rows = slice(j * tokens, (j + 1) * tokens)
        s = mm(kaug[rows, :], qaug[...], NT)
        s_ref[rows, :] = s
        top = jnp.maximum(top, jnp.max(s.reshape(tokens // 8, 8, rows_all), 0))
    top = jnp.max(top, 0, keepdims=True)
    c = math.log2(math.e) / math.sqrt(HEAD)
    for j in range(len(blocks)):
        rows = slice(j * tokens, (j + 1) * tokens)
        p = jnp.exp2((s_ref[rows, :] - top) * c)
        s_ref[rows, :] = p
        p_ref[rows, :] = p.astype(BF)
    lane = lax.broadcasted_iota(jnp.int32, (tokens, HEAD), 1)
    for pair in range(GROUP // 2):
        ot = mm(vat[...], p_ref[:, pair * 2 * tokens : (pair + 1) * 2 * tokens])
        for u in range(2):
            h = 2 * pair + u
            o = ot[:, u * tokens : (u + 1) * tokens].T
            inv = 1.0 / o[:, HEAD:]
            out = o[:, :HEAD] * inv
            o_ref[:, h * HEAD : (h + 1) * HEAD] = out.astype(BF)
            tp = (t_ref[:, h * HEAD : (h + 1) * HEAD].astype(F32) * inv).astype(BF)
            delta = jnp.sum(tp.astype(F32) * out, 1, keepdims=True)
            hi = delta.astype(BF).astype(F32)
            rest = delta - hi
            mid = rest.astype(BF).astype(F32)
            lo = rest - mid
            ext = jnp.where(
                lane == 0, -hi, jnp.where(lane == 1, -mid, jnp.where(lane == 2, -lo, 0.0))
            )
            taug[h * tokens : (h + 1) * tokens, 0:HEAD] = tp
            taug[h * tokens : (h + 1) * tokens, HEAD : 2 * HEAD] = ext.astype(BF)
    scale = 1.0 / math.sqrt(HEAD)
    for j, (_, g, b, _) in enumerate(blocks):
        rows = slice(j * tokens, (j + 1) * tokens)
        out_rows = slice(b, b + tokens)
        x = mm(vaug[rows, :], taug[...], NT)
        ds = (s_ref[rows, :] * x).astype(BF)
        dk = mm(ds, qaug[:, 0:HEAD]) * scale
        dv = mm(p_ref[rows, :], taug[:, 0:HEAD])
        g[out_rows, 0:HEAD] = dk.astype(g.dtype)
        g[out_rows, HEAD : 2 * HEAD] = dv.astype(g.dtype)


def attention(q, t, win, own, attn, first, heads):
    tokens = q.shape[0]
    n = win.shape[0]
    keys = (ROWS * n + 1) * tokens
    rows_all = GROUP * tokens
    wide = pl.BlockSpec((tokens, rows_all), lambda g: (0, g + first))

    def many(rows):
        return pl.BlockSpec((n, rows, 2 * HEAD), lambda g: (0, 0, g))

    def one(rows):
        return pl.BlockSpec((rows, 2 * HEAD), lambda g: (0, g))

    return pl.pallas_call(
        attn_kernel,
        grid=(heads,),
        in_specs=[wide, wide, many(win.shape[1]), one(own.shape[0]), pl.BlockSpec(memory_space=pl.ANY)],
        out_specs=[wide, many(ROWS * tokens), one(tokens)],
        out_shape=[
            jax.ShapeDtypeStruct(q.shape, BF),
            jax.ShapeDtypeStruct((n, ROWS * tokens, heads * 2 * HEAD), BF),
            jax.ShapeDtypeStruct((tokens, heads * 2 * HEAD), F32),
        ],
        input_output_aliases={4: 0} if first else {},
        scratch_shapes=[
            pltpu.VMEM((keys, 2 * HEAD), BF),
            pltpu.VMEM((keys, 2 * HEAD), BF),
            pltpu.VMEM((2 * HEAD, keys), BF),
            pltpu.VMEM((rows_all, 2 * HEAD), BF),
            pltpu.VMEM((rows_all, 2 * HEAD), BF),
            pltpu.VMEM((keys, rows_all), F32),
            pltpu.VMEM((keys, rows_all), BF),
        ],
        compiler_params=pltpu.CompilerParams(vmem_limit_bytes=40 << 20),
        cost_estimate=pl.CostEstimate(
            flops=heads * keys * rows_all * HEAD * 10,
            bytes_accessed=heads * 4 << 20,
            transcendentals=heads * keys * rows_all,
        ),
    )(q, t, win, own, attn)


def along_z(x, d):
    n = lax.axis_size("cz")
    return lax.ppermute(x, "cz", [(i - d, i) for i in range(n) if 0 <= i - d < n])


def swap_x(x):
    return lax.all_to_all(x, "cx", 0, 0)


def sum_among(x, axes):
    n = math.prod(lax.axis_size(a) for a in axes)
    return lax.all_to_all(jnp.broadcast_to(x[None], (n,) + x.shape), axes, 0, 0)


def per_device(query, key, value, key_shift, value_shift, doc_ids, target):
    tokens = query.shape[1]
    kv_local = key.shape[2] // HEAD
    where_x = lax.axis_index("cx")
    n_x = lax.axis_size("cx")
    key_new = (key[0].astype(F32) + key_shift[0]).astype(BF)
    val_new = (value[0].astype(F32) + value_shift[0]).astype(BF)
    docs = (doc_ids[0] + 1).astype(BF)[None, :]
    later = jnp.arange(n_x)[:, None, None] > where_x
    own, wins = [], []
    for h in range(0, kv_local, HEADS_AT_ONCE):
        lanes = []
        for i in range(h, h + HEADS_AT_ONCE):
            part = slice(i * HEAD, (i + 1) * HEAD)
            lanes += [key_new[:, part], val_new[:, part]]
        kv = jnp.concatenate(lanes, 1)
        tail = jnp.pad(docs, ((0, 7), (0, kv.shape[1] - tokens)))
        row = jnp.concatenate([kv, tail], 0)
        one, two = along_z(row, 1), along_z(row, 2)
        near = jnp.concatenate([one[:tokens], two[:tokens], one[tokens:], two[tokens:]], 0)
        far = along_z(near, 2)
        keep = 2 * tokens
        mixed = jnp.where(later, row[None, :tokens], far[None, tokens:keep])
        mixed_docs = jnp.where(later, row[None, tokens:], far[None, keep + 8 :])

        def each(x):
            return jnp.broadcast_to(x[None], (n_x,) + x.shape)

        sent = jnp.concatenate(
            [mixed, each(near[:keep]), each(far[:tokens]), mixed_docs, each(near[keep:]), each(far[keep : keep + 8])], 1
        )
        own.append(row)
        wins.append(swap_x(sent))
    attn = query[0]
    grads = []
    for i, h in enumerate(range(0, kv_local, HEADS_AT_ONCE)):
        attn, gwin, gown = attention(query[0], target[0], wins[i], own[i], attn, h, HEADS_AT_ONCE)
        back = swap_x(gwin)

        def piece(b):
            return back[:, b * tokens : (b + 1) * tokens].astype(F32)

        part0 = gown + jnp.sum(jnp.where(later, piece(0), 0.0), 0)
        part4 = jnp.sum(jnp.where(later, 0.0, piece(0)), 0)
        part3 = jnp.sum(piece(3), 0)
        far = along_z(jnp.concatenate([part3, part4], 0).astype(BF), -2).astype(F32)
        part1 = jnp.sum(piece(1), 0) + far[:tokens]
        part2 = jnp.sum(piece(2), 0) + far[tokens:]
        two = along_z(part2.astype(BF), -2)
        one = along_z(part1.astype(BF), -1)
        grads.append(part0 + two.astype(F32) + one.astype(F32))
    grad = jnp.concatenate(grads, 1)
    grad_key = jnp.concatenate(
        [grad[:, 2 * h * HEAD : (2 * h + 1) * HEAD] for h in range(kv_local)], 1
    )
    grad_val = jnp.concatenate(
        [grad[:, (2 * h + 1) * HEAD : (2 * h + 2) * HEAD] for h in range(kv_local)], 1
    )
    ks, vs = key_shift[0], value_shift[0]
    sums = jnp.stack(
        [
            jnp.sum(ks * ks, -1) + jnp.sum(vs * vs, -1),
            jnp.sum(ks * grad_key, -1) + jnp.sum(vs * grad_val, -1),
            jnp.sum(grad_key * grad_key, -1) + jnp.sum(grad_val * grad_val, -1),
        ]
    )
    n_dp, n_tp = lax.axis_size("dp"), lax.axis_size("tp")
    plane = sum_among(sums, ("dp", "cx", "tp"))
    near = jnp.sum(
        lax.dynamic_slice_in_dim(
            plane, (lax.axis_index("dp") * n_x + where_x) * n_tp, n_tp, 0
        ),
        0,
    )
    square = jnp.sum(plane[:, 2])
    overall = jnp.sum(sum_among(jnp.full((1, 128), square), ("cz",))[:, 0, 0])
    count = n_dp * tokens * n_x * lax.axis_size("cz") * 2 * KV_HEADS * HEAD
    rms = jnp.sqrt(overall / count + 1e-05)
    a = step_size / rms
    size_sq = jnp.maximum(near[0] + 2.0 * a * near[1] + a * a * near[2], 0.0)
    radius = radius_scale * math.sqrt(2 * KV_HEADS * HEAD)
    factor = jnp.minimum(1.0, radius / jnp.sqrt(size_sq + 1e-06))[:, None]
    return (
        attn[None],
        ((ks + a * grad_key) * factor)[None],
        ((vs + a * grad_val) * factor)[None],
    )


def solution(mesh):
    sizes = mesh.devices.shape
    inner = Mesh(
        mesh.devices.reshape(sizes[0], sizes[1] // 4, 4, sizes[2]), ("dp", "cz", "cx", "tp")
    )
    whole = P("dp", ("cz", "cx"), "tp")
    in_specs = (whole,) * 5 + (P("dp", ("cz", "cx")), whole)
    return jax.shard_map(
        per_device, mesh=inner, in_specs=in_specs, out_specs=(whole,) * 3, check_vma=False
    )
```

time: 208 us -> 184 us (0.88)
  waiting for transfers between devices: 90.1 us -> 53.2 us
  starting transfers between devices: 60.4 us -> 67.4 us
  blocking collectives: 15 us -> 18.9 us
    ppermute x6 -> x0, waiting for transfers between devices: 35.8 us -> none  [along_x(): return lax.ppermute(x, 'cx', [((i - d) % n, i) for i in range(n)])]
    ppermute x8 -> x12, waiting for transfers between devices: 43.1 us -> 21.3 us  [along_z(): lax.ppermute(x, 'cz', [(i - d, i) for i in range(n) if 0 <= i - d < n])]
    all_to_all x0 -> x4, waiting for transfers between devices: none -> 20.7 us  [swap_x(): return lax.all_to_all(x, 'cx', 0, 0)]
    ppermute x6 -> x0, starting transfers between devices: 18.1 us -> none  [along_x(): return lax.ppermute(x, 'cx', [((i - d) % n, i) for i in range(n)])]
    all_to_all x0 -> x4, starting transfers between devices: none -> 16.1 us  [swap_x(): return lax.all_to_all(x, 'cx', 0, 0)]
    ppermute x8 -> x12, starting transfers between devices: 29.1 us -> 36 us  [along_z(): lax.ppermute(x, 'cz', [(i - d, i) for i in range(n) if 0 <= i - d < n])]
    all_to_all x1, blocking collectives: 15 us -> 18.9 us  [sum_among(): return lax.all_to_all(jnp.broadcast_to(x[None], (n,) + x.shape), axes, 0, 0)]
    unnamed x10 -> x14, local copies, waits for them, and re-layouts: 0.89 us -> 4.33 us
  transfers between devices with their start and end apart: 15 -> 17, of which waited for: 9 -> 8; matrix products, arithmetic and copies ran while one was open for 2% -> 1% of each run, Pallas kernels for 0% -> 14%
where the time goes in v2:
time: 184 us; the launch traced here: 183 us
  starting transfers between devices  67.4 us (37%)
  waiting for transfers between devices  53.2 us (29%)
  Pallas kernels  25.1 us (14%)
  blocking collectives  18.9 us (10%)
  other arithmetic  9.37 us (5%)
  local copies, waits for them, and re-layouts  6.92 us (4%)
  between operations  1.84 us (1%)
    ppermute x12, starting transfers between devices, along_z(): lax.ppermute(x, 'cz', [(i - d, i) for i in range(n) if 0 <= i - d < n])  36 us
    pallas_call x2, Pallas kernels, attention(): pl.pallas_call(attn_kernel, grid=(heads,), in_specs=[wide, wide, many(win...  25.1 us
    ppermute x12, waiting for transfers between devices, along_z(): lax.ppermute(x, 'cz', [(i - d, i) for i in range(n) if 0 <= i - d < n])  21.3 us
    all_to_all x4, waiting for transfers between devices, swap_x(): return lax.all_to_all(x, 'cx', 0, 0)  20.7 us
    all_to_all x1, blocking collectives, sum_among(): return lax.all_to_all(jnp.broadcast_to(x[None], (n,) + x.shape), axes, 0, 0)  18.9 us
    all_to_all x4, starting transfers between devices, swap_x(): return lax.all_to_all(x, 'cx', 0, 0)  16.1 us
    all_to_all x1, starting transfers between devices, sum_among(): return lax.all_to_all(jnp.broadcast_to(x[None], (n,) + x.shape), axes, 0, 0)  15.2 us
    all_to_all x1, waiting for transfers between devices, sum_among(): return lax.all_to_all(jnp.broadcast_to(x[None], (n,) + x.shape), axes, 0, 0)  11.2 us
  transfers between devices with their start and end apart: 17, of which 8 were waited for; matrix products, arithmetic and copies ran while one was open for 1% of the time, Pallas kernels for 14%

profile of v2, /device:TPU:1, one launch (start us, length us, event | category | flops | bytes accessed | tf_op | source)
XLA Modules:
  0.0 182.7 jit_solution(3303018657789956188)
XLA Ops:
  0.6 0.9 fusion.13
  1.6 0.9 fusion.12
  2.5 0.7 add_convert_fusion
  3.2 4.4 %collective-permute-start = (bf16[136,256]{1,0:T(8,128)(2,1)S(1)}, bf16[136,256]{1,0:T(8,128)(2,1)S(1)}, u32[]{:S(2)}, u32[]{:S(2)}) collective-permute-start(bf16[136,256]{1,0:T(8,128)(2,1)S(1)} %get-tuple-element.60.own_ref), channel_id=1, source_target_pairs={{0,16},{16,32},{32,48},{48,64},{64,80},{80,96},{96,112},{112,128},... | collective-permute-start | bytes 208904 | tf_op jit(solution)/shard_map/ppermute | solution.py:157
  7.6 4.9 %collective-permute-start.1 = (bf16[136,256]{1,0:T(8,128)(2,1)S(1)}, bf16[136,256]{1,0:T(8,128)(2,1)S(1)}, u32[]{:S(2)}, u32[]{:S(2)}) collective-permute-start(bf16[136,256]{1,0:T(8,128)(2,1)S(1)} %get-tuple-element.60.own_ref), channel_id=1, source_target_pairs={{0,32},{16,48},{32,64},{48,80},{64,96},{80,112},{96,128},{112,144}... | collective-permute-start | bytes 208904 | tf_op jit(solution)/shard_map/ppermute | solution.py:157
  12.5 4.8 %collective-permute-start.3 = (bf16[136,256]{1,0:T(8,128)(2,1)S(1)}, bf16[136,256]{1,0:T(8,128)(2,1)S(1)}, u32[]{:S(2)}, u32[]{:S(2)}) collective-permute-start(bf16[136,256]{1,0:T(8,128)(2,1)S(1)} %get-tuple-element.59.own_ref), channel_id=1, source_target_pairs={{0,16},{16,32},{32,48},{48,64},{64,80},{80,96},{96,112},{112,128},... | collective-permute-start | bytes 208904 | tf_op jit(solution)/shard_map/ppermute | solution.py:157
  17.3 4.9 %collective-permute-start.4 = (bf16[136,256]{1,0:T(8,128)(2,1)S(1)}, bf16[136,256]{1,0:T(8,128)(2,1)S(1)}, u32[]{:S(2)}, u32[]{:S(2)}) collective-permute-start(bf16[136,256]{1,0:T(8,128)(2,1)S(1)} %get-tuple-element.59.own_ref), channel_id=1, source_target_pairs={{0,32},{16,48},{32,64},{48,80},{64,96},{80,112},{96,128},{112,144}... | collective-permute-start | bytes 208904 | tf_op jit(solution)/shard_map/ppermute | solution.py:157
  22.2 0.0 collective-permute-done
  22.2 0.0 collective-permute-done.1
  22.3 6.1 %collective-permute-start.2 = (bf16[272,256]{1,0:T(8,128)(2,1)S(1)}, bf16[272,256]{1,0:T(8,128)(2,1)S(1)}, u32[]{:S(2)}, u32[]{:S(2)}) collective-permute-start(bf16[272,256]{1,0:T(8,128)(2,1)S(1)} %pad_maximum_fusion), channel_id=1, source_target_pairs={{0,32},{16,48},{32,64},{48,80},{64,96},{80,112},{96,128},{112,144}... | collective-permute-start | bytes 417800 | tf_op jit(solution)/shard_map/ppermute | solution.py:157
  28.4 0.0 collective-permute-done.3
  28.5 0.0 collective-permute-done.4
  28.5 3.1 %collective-permute-start.5 = (bf16[272,256]{1,0:T(8,128)(2,1)S(1)}, bf16[272,256]{1,0:T(8,128)(2,1)S(1)}, u32[]{:S(2)}, u32[]{:S(2)}) collective-permute-start(bf16[272,256]{1,0:T(8,128)(2,1)S(1)} %pad_maximum_fusion.1), channel_id=1, source_target_pairs={{0,32},{16,48},{32,64},{48,80},{64,96},{80,112},{96,128},{112,144}... | collective-permute-start | bytes 417800 | tf_op jit(solution)/shard_map/ppermute | solution.py:157
  31.7 0.0 collective-permute-done.2
  31.7 2.5 %collective-permute-done.5 = bf16[272,256]{1,0:T(8,128)(2,1)S(1)} collective-permute-done((bf16[272,256]{1,0:T(8,128)(2,1)S(1)}, bf16[272,256]{1,0:T(8,128)(2,1)S(1)}, u32[]{:S(2)}, u32[]{:S(2)}) %collective-permute-start.5) | collective-permute-done | bytes 139296 | tf_op jit(solution)/shard_map/ppermute | solution.py:157
  34.2 1.0 select_dynamic-update-slice_fusion
  35.2 0.8 broadcast_dynamic-update-slice_fusion.1
  36.0 0.7 broadcast_dynamic-update-slice_fusion.3
  36.7 0.8 broadcast_dynamic-update-slice_fusion
  37.5 0.7 broadcast_dynamic-update-slice_fusion.2
  38.2 0.7 constant_dynamic-update-slice_fusion.5
  38.9 0.6 constant_dynamic-update-slice_fusion.4
  39.5 0.6 constant_dynamic-update-slice_fusion.3
  40.1 4.0 %all-to-all-start.1 = ((bf16[4,544,256]{2,1,0:T(8,128)(2,1)}), bf16[4,544,256]{2,1,0:T(8,128)(2,1)S(1)}, u32[]{:S(2)}, u32[]{:S(2)}) async-start(bf16[4,544,256]{2,1,0:T(8,128)(2,1)} %constant_dynamic-update-slice_fusion.3), calls=%async_computation.1 | async-start | bytes 2228224 | tf_op jit(solution)/shard_map/all_to_all | solution.py:161
  44.2 0.6 constant_dynamic-update-slice_fusion.1
  44.8 0.6 constant_dynamic-update-slice_fusion
  45.4 11.7 %all-to-all-done.1.win_ref = bf16[4,544,256]{2,1,0:T(8,128)(2,1)S(1)} async-done(((bf16[4,544,256]{2,1,0:T(8,128)(2,1)}), bf16[4,544,256]{2,1,0:T(8,128)(2,1)S(1)}, u32[]{:S(2)}, u32[]{:S(2)}) %all-to-all-start.1) | async-done | bytes 1114144 | tf_op jit(solution)/shard_map/all_to_all | solution.py:161
  57.0 3.5 %all-to-all-start = ((bf16[4,544,256]{2,1,0:T(8,128)(2,1)}), bf16[4,544,256]{2,1,0:T(8,128)(2,1)S(1)}, u32[]{:S(2)}, u32[]{:S(2)}) async-start(bf16[4,544,256]{2,1,0:T(8,128)(2,1)} %constant_dynamic-update-slice_fusion), calls=%async_computation | async-start | bytes 2228224 | tf_op jit(solution)/shard_map/all_to_all | solution.py:161
  60.6 0.0 copy-done
  60.6 0.0 copy-done.1
  60.6 12.6 %shard_map.94 = (bf16[128,2048]{1,0:T(8,128)(2,1)}, bf16[4,512,256]{2,1,0:T(8,128)(2,1)}, f32[128,256]{1,0:T(8,128)S(1)}) custom-call(bf16[128,2048]{1,0:T(8,128)(2,1)S(1)} %bitcast.42, bf16[128,2048]{1,0:T(8,128)(2,1)S(1)} %bitcast.45, bf16[4,544,256]{2,1,0:T(8,128)(2,1)S(1)} %all-to-all-done.1.win_ref, bf16[136,256]{1,0:T(8,128)(2,1)S(1)} %get-tuple-element.59.own_ref, ...), custom_call_target="tpu_custom_call" | custom-call | flops 2852126720 | bytes 4194304 | tf_op jit(solution)/shard_map/pallas_call | solution.py:126
  73.1 0.0 all-to-all-done.win_ref
  73.2 4.4 %all-to-all-start.2 = ((bf16[4,512,256]{2,1,0:T(8,128)(2,1)}), bf16[4,512,256]{2,1,0:T(8,128)(2,1)}, u32[]{:S(2)}, u32[]{:S(2)}) async-start(bf16[4,512,256]{2,1,0:T(8,128)(2,1)} %get-tuple-element.12), calls=%async_computation.2 | async-start | bytes 2097152 | tf_op jit(solution)/shard_map/all_to_all | solution.py:161
  77.6 12.5 %shard_map.95 = (bf16[128,2048]{1,0:T(8,128)(2,1)}, bf16[4,512,256]{2,1,0:T(8,128)(2,1)}, f32[128,256]{1,0:T(8,128)S(1)}) custom-call(bf16[128,2048]{1,0:T(8,128)(2,1)S(1)} %bitcast.44, bf16[128,2048]{1,0:T(8,128)(2,1)S(1)} %bitcast.46, bf16[4,544,256]{2,1,0:T(8,128)(2,1)S(1)} %all-to-all-done.win_ref, ...), custom_call_target="tpu_custom_call", output_to_operand_aliasing={{0}: (4, {})} | custom-call | flops 2852126720 | bytes 4194304 | tf_op jit(solution)/shard_map/pallas_call | solution.py:126
  90.1 0.0 all-to-all-done.2
  90.1 4.2 %all-to-all-start.3 = ((bf16[4,512,256]{2,1,0:T(8,128)(2,1)}), bf16[4,512,256]{2,1,0:T(8,128)(2,1)S(1)}, u32[]{:S(2)}, u32[]{:S(2)}) async-start(bf16[4,512,256]{2,1,0:T(8,128)(2,1)} %get-tuple-element.14), calls=%async_computation.3 | async-start | bytes 2097152 | tf_op jit(solution)/shard_map/all_to_all | solution.py:161
  94.3 1.0 slice_reduce_fusion.1
  95.3 9.0 %all-to-all-done.3 = bf16[4,512,256]{2,1,0:T(8,128)(2,1)S(1)} async-done(((bf16[4,512,256]{2,1,0:T(8,128)(2,1)}), bf16[4,512,256]{2,1,0:T(8,128)(2,1)S(1)}, u32[]{:S(2)}, u32[]{:S(2)}) %all-to-all-start.3) | async-done | bytes 1048608 | tf_op jit(solution)/shard_map/all_to_all | solution.py:161
  104.3 1.6 fusion
  105.9 1.3 collective-permute-start.6
  107.3 1.3 collective-permute-start.9
  108.6 3.9 %collective-permute-done.6 = bf16[256,256]{1,0:T(8,128)(2,1)S(1)} collective-permute-done((bf16[256,256]{1,0:T(8,128)(2,1)S(1)}, bf16[256,256]{1,0:T(8,128)(2,1)S(1)}, u32[]{:S(2)}, u32[]{:S(2)}) %collective-permute-start.6) | collective-permute-done | bytes 131104 | tf_op jit(solution)/shard_map/ppermute | solution.py:157
  112.6 1.3 collective-permute-start.7
  113.9 1.3 collective-permute-start.8
  115.2 0.0 collective-permute-done.9
  115.2 0.0 copy-start.2
  115.3 0.0 copy-start.3
  115.3 1.4 collective-permute-start.10
  116.7 1.3 collective-permute-start.11
  118.0 0.5 collective-permute-done.7
  118.5 9.3 %collective-permute-done.8 = bf16[128,256]{1,0:T(8,128)(2,1)S(1)} collective-permute-done((bf16[128,256]{1,0:T(8,128)(2,1)S(1)}, bf16[128,256]{1,0:T(8,128)(2,1)S(1)}, u32[]{:S(2)}, u32[]{:S(2)}) %collective-permute-start.8) | collective-permute-done | bytes 65568 | tf_op jit(solution)/shard_map/ppermute | solution.py:157
  127.8 5.1 %collective-permute-done.10 = bf16[128,256]{1,0:T(8,128)(2,1)S(1)} collective-permute-done((bf16[128,256]{1,0:T(8,128)(2,1)S(1)}, bf16[128,256]{1,0:T(8,128)(2,1)S(1)}, u32[]{:S(2)}, u32[]{:S(2)}) %collective-permute-start.10) | collective-permute-done | bytes 65568 | tf_op jit(solution)/shard_map/ppermute | solution.py:157
  132.9 0.0 collective-permute-done.11
  133.0 0.0 copy-done.2
  133.0 0.1 fusion.14
  133.1 0.0 copy-done.3
  133.2 0.1 fusion.16
  133.4 18.9 %all_to_all.30 = f32[32,3,128]{2,1,0:T(4,128)S(1)} all-to-all(f32[32,3,128]{2,1,0:T(4,128)S(1)} %broadcast_in_dim.187), channel_id=1, replica_groups=mesh['dp'=2,'cz'=16,'cx'=4,'tp'=4] {'dp','cx','tp'}, dimensions={0} | all-to-all | bytes 98304 | tf_op jit(solution)/shard_map/all_to_all | solution.py:166
  152.3 0.6 reduce_sum.187
  152.9 1.2 broadcast_in_dim_broadcast_in_dim_broadcast_in_dim.3
  154.2 15.2 %all-to-all-start.5 = ((f32[16,1,128]{2,1,0:T(1,128)}), f32[16,1,128]{2,1,0:T(1,128)S(1)}, u32[]{:S(2)}, u32[]{:S(2)}) async-start(f32[16,1,128]{2,1,0:T(1,128)} %broadcast_in_dim_broadcast_in_dim_broadcast_in_dim.3), calls=%async_computation.5 | async-start | bytes 16384 | tf_op jit(solution)/shard_map/all_to_all | solution.py:166
  169.4 11.2 %all-to-all-done.5 = f32[16,1,128]{2,1,0:T(1,128)S(1)} async-done(((f32[16,1,128]{2,1,0:T(1,128)}), f32[16,1,128]{2,1,0:T(1,128)S(1)}, u32[]{:S(2)}, u32[]{:S(2)}) %all-to-all-start.5) | async-done | bytes 8224 | tf_op jit(solution)/shard_map/all_to_all | solution.py:166
  180.6 0.6 slice_reduce_fusion.2
  181.9 0.8 fusion.11
  (43 shorter events, 0.5 us)
Async XLA Ops:
  3.2 19.0 %collective-permute-start = (bf16[136,256]{1,0:T(8,128)(2,1)S(1)}, bf16[136,256]{1,0:T(8,128)(2,1)S(1)}, u32[]{:S(2)}, u32[]{:S(2)}) collective-permute-start(bf16[136,256]{1,0:T(8,128)(2,1)S(1)} %get-tuple-element.60.own_ref), channel_id=1, source_target_pairs={{0,16},{16,32},{32,48},{48,64},{64,80},{80,96},{96,112},{112,128},... | collective-permute-start | bytes 208904 | tf_op jit(solution)/shard_map/ppermute | solution.py:157
  7.6 14.7 %collective-permute-start.1 = (bf16[136,256]{1,0:T(8,128)(2,1)S(1)}, bf16[136,256]{1,0:T(8,128)(2,1)S(1)}, u32[]{:S(2)}, u32[]{:S(2)}) collective-permute-start(bf16[136,256]{1,0:T(8,128)(2,1)S(1)} %get-tuple-element.60.own_ref), channel_id=1, source_target_pairs={{0,32},{16,48},{32,64},{48,80},{64,96},{80,112},{96,128},{112,144}... | collective-permute-start | bytes 208904 | tf_op jit(solution)/shard_map/ppermute | solution.py:157
  12.5 15.9 %collective-permute-start.3 = (bf16[136,256]{1,0:T(8,128)(2,1)S(1)}, bf16[136,256]{1,0:T(8,128)(2,1)S(1)}, u32[]{:S(2)}, u32[]{:S(2)}) collective-permute-start(bf16[136,256]{1,0:T(8,128)(2,1)S(1)} %get-tuple-element.59.own_ref), channel_id=1, source_target_pairs={{0,16},{16,32},{32,48},{48,64},{64,80},{80,96},{96,112},{112,128},... | collective-permute-start | bytes 208904 | tf_op jit(solution)/shard_map/ppermute | solution.py:157
  17.3 11.2 %collective-permute-start.4 = (bf16[136,256]{1,0:T(8,128)(2,1)S(1)}, bf16[136,256]{1,0:T(8,128)(2,1)S(1)}, u32[]{:S(2)}, u32[]{:S(2)}) collective-permute-start(bf16[136,256]{1,0:T(8,128)(2,1)S(1)} %get-tuple-element.59.own_ref), channel_id=1, source_target_pairs={{0,32},{16,48},{32,64},{48,80},{64,96},{80,112},{96,128},{112,144}... | collective-permute-start | bytes 208904 | tf_op jit(solution)/shard_map/ppermute | solution.py:157
  22.3 9.4 %collective-permute-start.2 = (bf16[272,256]{1,0:T(8,128)(2,1)S(1)}, bf16[272,256]{1,0:T(8,128)(2,1)S(1)}, u32[]{:S(2)}, u32[]{:S(2)}) collective-permute-start(bf16[272,256]{1,0:T(8,128)(2,1)S(1)} %pad_maximum_fusion), channel_id=1, source_target_pairs={{0,32},{16,48},{32,64},{48,80},{64,96},{80,112},{96,128},{112,144}... | collective-permute-start | bytes 417800 | tf_op jit(solution)/shard_map/ppermute | solution.py:157
  28.5 5.7 %collective-permute-start.5 = (bf16[272,256]{1,0:T(8,128)(2,1)S(1)}, bf16[272,256]{1,0:T(8,128)(2,1)S(1)}, u32[]{:S(2)}, u32[]{:S(2)}) collective-permute-start(bf16[272,256]{1,0:T(8,128)(2,1)S(1)} %pad_maximum_fusion.1), channel_id=1, source_target_pairs={{0,32},{16,48},{32,64},{48,80},{64,96},{80,112},{96,128},{112,144}... | collective-permute-start | bytes 417800 | tf_op jit(solution)/shard_map/ppermute | solution.py:157
  40.1 16.9 %all-to-all-start.1 = ((bf16[4,544,256]{2,1,0:T(8,128)(2,1)}), bf16[4,544,256]{2,1,0:T(8,128)(2,1)S(1)}, u32[]{:S(2)}, u32[]{:S(2)}) async-start(bf16[4,544,256]{2,1,0:T(8,128)(2,1)} %constant_dynamic-update-slice_fusion.3), calls=%async_computation.1 | async-start | bytes 2228224 | tf_op jit(solution)/shard_map/all_to_all | solution.py:161
  45.4 15.2 %copy-start = (bf16[1,128,2048]{2,1,0:T(8,128)(2,1)S(1)}, bf16[1,128,2048]{2,1,0:T(8,128)(2,1)}, u32[]{:S(2)}) copy-start(bf16[1,128,2048]{2,1,0:T(8,128)(2,1)} %param.7) | copy-start | bytes 1572868
  45.4 15.2 %copy-start.1 = (bf16[1,128,2048]{2,1,0:T(8,128)(2,1)S(1)}, bf16[1,128,2048]{2,1,0:T(8,128)(2,1)}, u32[]{:S(2)}) copy-start(bf16[1,128,2048]{2,1,0:T(8,128)(2,1)} %param.13) | copy-start | bytes 1572868
  57.0 16.1 %all-to-all-start = ((bf16[4,544,256]{2,1,0:T(8,128)(2,1)}), bf16[4,544,256]{2,1,0:T(8,128)(2,1)S(1)}, u32[]{:S(2)}, u32[]{:S(2)}) async-start(bf16[4,544,256]{2,1,0:T(8,128)(2,1)} %constant_dynamic-update-slice_fusion), calls=%async_computation | async-start | bytes 2228224 | tf_op jit(solution)/shard_map/all_to_all | solution.py:161
  73.2 17.0 %all-to-all-start.2 = ((bf16[4,512,256]{2,1,0:T(8,128)(2,1)}), bf16[4,512,256]{2,1,0:T(8,128)(2,1)}, u32[]{:S(2)}, u32[]{:S(2)}) async-start(bf16[4,512,256]{2,1,0:T(8,128)(2,1)} %get-tuple-element.12), calls=%async_computation.2 | async-start | bytes 2097152 | tf_op jit(solution)/shard_map/all_to_all | solution.py:161
  90.1 14.2 %all-to-all-start.3 = ((bf16[4,512,256]{2,1,0:T(8,128)(2,1)}), bf16[4,512,256]{2,1,0:T(8,128)(2,1)S(1)}, u32[]{:S(2)}, u32[]{:S(2)}) async-start(bf16[4,512,256]{2,1,0:T(8,128)(2,1)} %get-tuple-element.14), calls=%async_computation.3 | async-start | bytes 2097152 | tf_op jit(solution)/shard_map/all_to_all | solution.py:161
  105.9 6.6 %collective-permute-start.6 = (bf16[256,256]{1,0:T(8,128)(2,1)S(1)}, bf16[256,256]{1,0:T(8,128)(2,1)S(1)}, u32[]{:S(2)}, u32[]{:S(2)}) collective-permute-start(bf16[256,256]{1,0:T(8,128)(2,1)S(1)} %pad_maximum_fusion.4), channel_id=1, source_target_pairs={{32,0},{48,16},{64,32},{80,48},{96,64},{112,80},{128,96},{144,112}... | collective-permute-start | bytes 393224 | tf_op jit(solution)/shard_map/ppermute | solution.py:157
  107.3 7.9 %collective-permute-start.9 = (bf16[256,256]{1,0:T(8,128)(2,1)S(1)}, bf16[256,256]{1,0:T(8,128)(2,1)S(1)}, u32[]{:S(2)}, u32[]{:S(2)}) collective-permute-start(bf16[256,256]{1,0:T(8,128)(2,1)S(1)} %pad_maximum_fusion.5), channel_id=1, source_target_pairs={{32,0},{48,16},{64,32},{80,48},{96,64},{112,80},{128,96},{144,112}... | collective-permute-start | bytes 393224 | tf_op jit(solution)/shard_map/ppermute | solution.py:157
  112.6 5.9 %collective-permute-start.7 = (bf16[128,256]{1,0:T(8,128)(2,1)S(1)}, bf16[128,256]{1,0:T(8,128)(2,1)S(1)}, u32[]{:S(2)}, u32[]{:S(2)}) collective-permute-start(bf16[128,256]{1,0:T(8,128)(2,1)S(1)} %get-tuple-element.33), channel_id=1, source_target_pairs={{32,0},{48,16},{64,32},{80,48},{96,64},{112,80},{128,96},{144,112}... | collective-permute-start | bytes 196616 | tf_op jit(solution)/shard_map/ppermute | solution.py:157
  113.9 13.9 %collective-permute-start.8 = (bf16[128,256]{1,0:T(8,128)(2,1)S(1)}, bf16[128,256]{1,0:T(8,128)(2,1)S(1)}, u32[]{:S(2)}, u32[]{:S(2)}) collective-permute-start(bf16[128,256]{1,0:T(8,128)(2,1)S(1)} %get-tuple-element.34), channel_id=1, source_target_pairs={{16,0},{32,16},{48,32},{64,48},{80,64},{96,80},{112,96},{128,112},... | collective-permute-start | bytes 196616 | tf_op jit(solution)/shard_map/ppermute | solution.py:157
  115.2 17.8 %copy-start.2 = (f32[1,128,256]{2,1,0:T(8,128)S(1)}, f32[1,128,256]{2,1,0:T(8,128)}, u32[]{:S(2)}) copy-start(f32[1,128,256]{2,1,0:T(8,128)} %param.11) | copy-start | bytes 393220
  115.3 17.9 %copy-start.3 = (f32[1,128,256]{2,1,0:T(8,128)S(1)}, f32[1,128,256]{2,1,0:T(8,128)}, u32[]{:S(2)}) copy-start(f32[1,128,256]{2,1,0:T(8,128)} %param.10) | copy-start | bytes 393220
  115.3 17.6 %collective-permute-start.10 = (bf16[128,256]{1,0:T(8,128)(2,1)S(1)}, bf16[128,256]{1,0:T(8,128)(2,1)S(1)}, u32[]{:S(2)}, u32[]{:S(2)}) collective-permute-start(bf16[128,256]{1,0:T(8,128)(2,1)S(1)} %get-tuple-element.35), channel_id=1, source_target_pairs={{32,0},{48,16},{64,32},{80,48},{96,64},{112,80},{128,96},{144,112}... | collective-permute-start | bytes 196616 | tf_op jit(solution)/shard_map/ppermute | solution.py:157
  116.7 16.2 %collective-permute-start.11 = (bf16[128,256]{1,0:T(8,128)(2,1)S(1)}, bf16[128,256]{1,0:T(8,128)(2,1)S(1)}, u32[]{:S(2)}, u32[]{:S(2)}) collective-permute-start(bf16[128,256]{1,0:T(8,128)(2,1)S(1)} %get-tuple-element.36), channel_id=1, source_target_pairs={{16,0},{32,16},{48,32},{64,48},{80,64},{96,80},{112,96},{128,112},... | collective-permute-start | bytes 196616 | tf_op jit(solution)/shard_map/ppermute | solution.py:157
  154.2 26.4 %all-to-all-start.5 = ((f32[16,1,128]{2,1,0:T(1,128)}), f32[16,1,128]{2,1,0:T(1,128)S(1)}, u32[]{:S(2)}, u32[]{:S(2)}) async-start(f32[16,1,128]{2,1,0:T(1,128)} %broadcast_in_dim_broadcast_in_dim_broadcast_in_dim.3), calls=%async_computation.5 | async-start | bytes 16384 | tf_op jit(solution)/shard_map/all_to_all | solution.py:166

commit v3 on v2

--- a/solution.py
+++ b/solution.py
@@ -24,7 +24,7 @@
 NN = (((1,), (0,)), ((), ()))
 FAR = -1e30
 ROWS = 4
-HEADS_AT_ONCE = 1
+TAIL = 8
 
 
 def mm(a, b, dims=NN):
@@ -40,19 +40,22 @@
     blocks = []
     for x in range(win_ref.shape[0]):
         for b in range(ROWS):
-            blocks.append((win_ref.at[x], gwin_ref.at[x], b * tokens, ROWS * tokens + 8 * b))
-    blocks.append((own_ref, gown_ref, 0, tokens))
-    docs = jnp.concatenate([src[d : d + 1, 0:tokens] for src, _, _, d in blocks], 0).astype(F32)
+            blocks.append((win_ref.at[x], gwin_ref.at[x], b))
+    blocks.append((own_ref, gown_ref, 0))
+    step = tokens + TAIL
+    docs = jnp.concatenate(
+        [src[b * step + tokens : b * step + tokens + 1, 0:tokens].astype(F32) for src, _, b in blocks], 0
+    )
     docs_sq = jnp.concatenate([docs, jnp.zeros((tokens - docs.shape[0], tokens), F32)], 0)
     doc_cols = docs_sq.T
     doc_row = docs[len(blocks) - 1 :, :]
     i_key = lax.broadcasted_iota(jnp.int32, (tokens, tokens), 0)
     i_qry = lax.broadcasted_iota(jnp.int32, (tokens, tokens), 1)
     one = jnp.ones((tokens, HEAD), BF)
-    for j, (src, _, b, _) in enumerate(blocks):
+    for j, (src, _, b) in enumerate(blocks):
         rows = slice(j * tokens, (j + 1) * tokens)
-        kaug[rows, 0:HEAD] = src[b : b + tokens, 0:HEAD]
-        v = src[b : b + tokens, HEAD : 2 * HEAD]
+        kaug[rows, 0:HEAD] = src[b * step : b * step + tokens, 0:HEAD]
+        v = src[b * step : b * step + tokens, HEAD : 2 * HEAD]
         vaug[rows, 0:HEAD] = v
         vaug[rows, HEAD : 2 * HEAD] = one
         vat[0:HEAD, rows] = v.T
@@ -99,9 +102,9 @@
             taug[h * tokens : (h + 1) * tokens, 0:HEAD] = tp
             taug[h * tokens : (h + 1) * tokens, HEAD : 2 * HEAD] = ext.astype(BF)
     scale = 1.0 / math.sqrt(HEAD)
-    for j, (_, g, b, _) in enumerate(blocks):
+    for j, (_, g, b) in enumerate(blocks):
         rows = slice(j * tokens, (j + 1) * tokens)
-        out_rows = slice(b, b + tokens)
+        out_rows = slice(b * tokens, (b + 1) * tokens)
         x = mm(vaug[rows, :], taug[...], NT)
         ds = (s_ref[rows, :] * x).astype(BF)
         dk = mm(ds, qaug[:, 0:HEAD]) * scale
@@ -110,30 +113,30 @@
         g[out_rows, HEAD : 2 * HEAD] = dv.astype(g.dtype)
 
 
-def attention(q, t, win, own, attn, first, heads):
+def attention(q, t, win, own, attn, head):
     tokens = q.shape[0]
     n = win.shape[0]
     keys = (ROWS * n + 1) * tokens
     rows_all = GROUP * tokens
-    wide = pl.BlockSpec((tokens, rows_all), lambda g: (0, g + first))
-
-    def many(rows):
-        return pl.BlockSpec((n, rows, 2 * HEAD), lambda g: (0, 0, g))
-
-    def one(rows):
-        return pl.BlockSpec((rows, 2 * HEAD), lambda g: (0, g))
-
+    wide = pl.BlockSpec((tokens, rows_all), lambda g: (0, head))
+    whole = pl.BlockSpec(memory_space=pltpu.VMEM)
     return pl.pallas_call(
         attn_kernel,
-        grid=(heads,),
-        in_specs=[wide, wide, many(win.shape[1]), one(own.shape[0]), pl.BlockSpec(memory_space=pl.ANY)],
-        out_specs=[wide, many(ROWS * tokens), one(tokens)],
+        grid=(1,),
+        in_specs=[
+            wide,
+            wide,
+            whole,
+            pl.BlockSpec((own.shape[0], 2 * HEAD), lambda g: (0, head)),
+            pl.BlockSpec(memory_space=pl.ANY),
+        ],
+        out_specs=[wide, whole, whole],
         out_shape=[
             jax.ShapeDtypeStruct(q.shape, BF),
-            jax.ShapeDtypeStruct((n, ROWS * tokens, heads * 2 * HEAD), BF),
-            jax.ShapeDtypeStruct((tokens, heads * 2 * HEAD), F32),
+            jax.ShapeDtypeStruct((n, ROWS * tokens, 2 * HEAD), BF),
+            jax.ShapeDtypeStruct((tokens, 2 * HEAD), F32),
         ],
-        input_output_aliases={4: 0} if first else {},
+        input_output_aliases={4: 0} if head else {},
         scratch_shapes=[
             pltpu.VMEM((keys, 2 * HEAD), BF),
             pltpu.VMEM((keys, 2 * HEAD), BF),
@@ -143,13 +146,110 @@
             pltpu.VMEM((keys, rows_all), F32),
             pltpu.VMEM((keys, rows_all), BF),
         ],
-        compiler_params=pltpu.CompilerParams(vmem_limit_bytes=40 << 20),
+        compiler_params=pltpu.CompilerParams(vmem_limit_bytes=32 << 20),
         cost_estimate=pl.CostEstimate(
-            flops=heads * keys * rows_all * HEAD * 10,
-            bytes_accessed=heads * 4 << 20,
-            transcendentals=heads * keys * rows_all,
+            flops=keys * rows_all * HEAD * 10,
+            bytes_accessed=4 << 20,
+            transcendentals=keys * rows_all,
         ),
     )(q, t, win, own, attn)
+
+
+def prepare_kernel(k_ref, v_ref, ks_ref, vs_ref, docs_ref, row_ref):
+    tokens = k_ref.shape[0]
+    k = (k_ref[...].astype(F32) + ks_ref[...]).astype(BF)
+    v = (v_ref[...].astype(F32) + vs_ref[...]).astype(BF)
+    docs = (docs_ref[...] + 1).astype(F32)
+    docs = jnp.broadcast_to(docs, (TAIL, docs.shape[1])).astype(BF)
+    for h in range(k.shape[1] // HEAD):
+        at = 2 * h * HEAD
+        row_ref[0:tokens, at : at + HEAD] = k[:, h * HEAD : (h + 1) * HEAD]
+        row_ref[0:tokens, at + HEAD : at + 2 * HEAD] = v[:, h * HEAD : (h + 1) * HEAD]
+        row_ref[tokens:, at : at + tokens] = docs
+        row_ref[tokens:, at + HEAD : at + HEAD + tokens] = docs
+
+
+def prepare(k, v, ks, vs, docs):
+    tokens, width = k.shape
+    return pl.pallas_call(
+        prepare_kernel,
+        out_shape=jax.ShapeDtypeStruct((tokens + TAIL, 2 * width), BF),
+        compiler_params=pltpu.CompilerParams(vmem_limit_bytes=4 << 20),
+        cost_estimate=pl.CostEstimate(flops=1 << 17, bytes_accessed=1 << 19, transcendentals=0),
+    )(k, v, ks, vs, docs)
+
+
+def spread_kernel(x_ref, row_ref, near_ref, far_ref, out_ref):
+    rows = row_ref.shape[0]
+    target = pl.program_id(0)
+
+    @pl.when(target > x_ref[0])
+    def _():
+        out_ref[0, 0:rows, :] = row_ref[...]
+
+    @pl.when(target <= x_ref[0])
+    def _():
+        out_ref[0, 0:rows, :] = far_ref[rows:, :]
+
+    out_ref[0, rows : 3 * rows, :] = near_ref[...]
+    out_ref[0, 3 * rows :, :] = far_ref[0:rows, :]
+
+
+def spread(where_x, row, near, far, head, n):
+    rows, width = near.shape
+    return pl.pallas_call(
+        spread_kernel,
+        grid_spec=pltpu.PrefetchScalarGridSpec(
+            num_scalar_prefetch=1,
+            grid=(n,),
+            in_specs=[
+                pl.BlockSpec((rows // 2, width), lambda g, x: (0, head)),
+                pl.BlockSpec((rows, width), lambda g, x: (0, 0)),
+                pl.BlockSpec((rows, width), lambda g, x: (0, 0)),
+            ],
+            out_specs=pl.BlockSpec((1, 2 * rows, width), lambda g, x: (g, 0, 0)),
+        ),
+        out_shape=jax.ShapeDtypeStruct((n, 2 * rows, width), BF),
+        compiler_params=pltpu.CompilerParams(vmem_limit_bytes=8 << 20),
+        cost_estimate=pl.CostEstimate(flops=0, bytes_accessed=2 << 20, transcendentals=0),
+    )(where_x, row, near, far)
+
+
+def fold_kernel(x_ref, back_ref, gown_ref, sent_ref, kept_ref):
+    tokens = gown_ref.shape[0]
+    n = back_ref.shape[0]
+
+    def part(i, b):
+        return back_ref[i, b * tokens : (b + 1) * tokens, :].astype(F32)
+
+    own = gown_ref[...]
+    last = jnp.zeros_like(own)
+    for i in range(n):
+        later = i > x_ref[0]
+        p = part(i, 0)
+        own = own + jnp.where(later, p, 0.0)
+        last = last + jnp.where(later, 0.0, p)
+    kept_ref[0:tokens, :] = own
+    for b in (1, 2):
+        kept_ref[b * tokens : (b + 1) * tokens, :] = sum(part(i, b) for i in range(n))
+    sent_ref[0:tokens, :] = sum(part(i, 3) for i in range(n)).astype(BF)
+    sent_ref[tokens:, :] = last.astype(BF)
+
+
+def fold(where_x, back, gown):
+    tokens, width = gown.shape
+    vmem = pl.BlockSpec(memory_space=pltpu.VMEM)
+    return pl.pallas_call(
+        fold_kernel,
+        in_specs=[pl.BlockSpec(memory_space=pltpu.SMEM), vmem, vmem],
+        out_specs=[vmem, vmem],
+        out_shape=[
+            jax.ShapeDtypeStruct((2 * tokens, width), BF),
+            jax.ShapeDtypeStruct((3 * tokens, width), F32),
+        ],
+        compiler_params=pltpu.CompilerParams(vmem_limit_bytes=8 << 20),
+        cost_estimate=pl.CostEstimate(flops=1 << 19, bytes_accessed=2 << 20, transcendentals=0),
+    )(where_x, back, gown)
 
 
 def along_z(x, d):
@@ -171,53 +271,33 @@
     kv_local = key.shape[2] // HEAD
     where_x = lax.axis_index("cx")
     n_x = lax.axis_size("cx")
-    key_new = (key[0].astype(F32) + key_shift[0]).astype(BF)
-    val_new = (value[0].astype(F32) + value_shift[0]).astype(BF)
-    docs = (doc_ids[0] + 1).astype(BF)[None, :]
-    later = jnp.arange(n_x)[:, None, None] > where_x
-    own, wins = [], []
-    for h in range(0, kv_local, HEADS_AT_ONCE):
-        lanes = []
-        for i in range(h, h + HEADS_AT_ONCE):
-            part = slice(i * HEAD, (i + 1) * HEAD)
-            lanes += [key_new[:, part], val_new[:, part]]
-        kv = jnp.concatenate(lanes, 1)
-        tail = jnp.pad(docs, ((0, 7), (0, kv.shape[1] - tokens)))
-        row = jnp.concatenate([kv, tail], 0)
-        one, two = along_z(row, 1), along_z(row, 2)
-        near = jnp.concatenate([one[:tokens], two[:tokens], one[tokens:], two[tokens:]], 0)
+    at_x = where_x.astype(jnp.int32)[None]
+    row = prepare(key[0], value[0], key_shift[0], value_shift[0], doc_ids)
+    one, two = along_z(row, 1), along_z(row, 2)
+    wins = []
+    for h in range(kv_local):
+        part = slice(2 * h * HEAD, 2 * (h + 1) * HEAD)
+        near = jnp.concatenate([one[:, part], two[:, part]], 0)
         far = along_z(near, 2)
-        keep = 2 * tokens
-        mixed = jnp.where(later, row[None, :tokens], far[None, tokens:keep])
-        mixed_docs = jnp.where(later, row[None, tokens:], far[None, keep + 8 :])
-
-        def each(x):
-            return jnp.broadcast_to(x[None], (n_x,) + x.shape)
-
-        sent = jnp.concatenate(
-            [mixed, each(near[:keep]), each(far[:tokens]), mixed_docs, each(near[keep:]), each(far[keep : keep + 8])], 1
+        wins.append(swap_x(spread(at_x, row, near, far, h, n_x)))
+    attn = query[0]
+    kept = []
+    for h in range(kv_local):
+        attn, gwin, gown = attention(query[0], target[0], wins[h], row, attn, h)
+        sent, mine = fold(at_x, swap_x(gwin), gown)
+        kept.append((along_z(sent, -2), mine))
+    near = [
+        jnp.concatenate(
+            [
+                (mine[(b + 1) * tokens : (b + 2) * tokens] + far[b * tokens : (b + 1) * tokens]).astype(BF)
+                for far, mine in kept
+            ],
+            1,
         )
-        own.append(row)
-        wins.append(swap_x(sent))
-    attn = query[0]
-    grads = []
-    for i, h in enumerate(range(0, kv_local, HEADS_AT_ONCE)):
-        attn, gwin, gown = attention(query[0], target[0], wins[i], own[i], attn, h, HEADS_AT_ONCE)
-        back = swap_x(gwin)
-
-        def piece(b):
-            return back[:, b * tokens : (b + 1) * tokens].astype(F32)
-
-        part0 = gown + jnp.sum(jnp.where(later, piece(0), 0.0), 0)
-        part4 = jnp.sum(jnp.where(later, 0.0, piece(0)), 0)
-        part3 = jnp.sum(piece(3), 0)
-        far = along_z(jnp.concatenate([part3, part4], 0).astype(BF), -2).astype(F32)
-        part1 = jnp.sum(piece(1), 0) + far[:tokens]
-        part2 = jnp.sum(piece(2), 0) + far[tokens:]
-        two = along_z(part2.astype(BF), -2)
-        one = along_z(part1.astype(BF), -1)
-        grads.append(part0 + two.astype(F32) + one.astype(F32))
-    grad = jnp.concatenate(grads, 1)
+        for b in range(2)
+    ]
+    two, one = along_z(near[1], -2), along_z(near[0], -1)
+    grad = jnp.concatenate([mine[:tokens] for _, mine in kept], 1) + one.astype(F32) + two.astype(F32)
     grad_key = jnp.concatenate(
         [grad[:, 2 * h * HEAD : (2 * h + 1) * HEAD] for h in range(kv_local)], 1
     )

time: 184 us -> 172 us (0.935)
  other arithmetic: 9.37 us -> 2.43 us
  waiting for transfers between devices: 53.2 us -> 46.9 us
  starting transfers between devices: 67.4 us -> 63.7 us
  Pallas kernels: 25.1 us -> 28.8 us
    all_to_all x4, waiting for transfers between devices: 20.7 us -> 9.89 us  [swap_x(): return lax.all_to_all(x, 'cx', 0, 0)]
    ppermute x12 -> x8, waiting for transfers between devices: 21.3 us -> 25.8 us  [along_z(): lax.ppermute(x, 'cz', [(i - d, i) for i in range(n) if 0 <= i - d < n])]
    pallas_call x2 -> x7, Pallas kernels: 25.1 us -> 28.8 us  [the longest x2 25.2 us: attention(): pl.pallas_call(attn_kernel, grid=(1,), in_specs=[wide, wide, whole, pl.Bl...]
    reduce_sum x4 -> x0, other arithmetic: 2.74 us -> none  [the longest x1 1.57 us: per_device(): part0 = gown + jnp.sum(jnp.where(later, piece(0), 0.0), 0)]
    ppermute x12 -> x8, starting transfers between devices: 36 us -> 33.3 us  [along_z(): lax.ppermute(x, 'cz', [(i - d, i) for i in range(n) if 0 <= i - d < n])]
    convert_element_type x7 -> x2, other arithmetic: 2.62 us -> 0.07 us  [per_device(): (mine[(b + 1) * tokens:(b + 2) * tokens] + far[b * tokens:(b + 1) * token...]
    unnamed x14 -> x20, local copies, waits for them, and re-layouts: 4.33 us -> 6.23 us
  transfers between devices with their start and end apart: 17 -> 13, of which waited for: 8 -> 8; matrix products, arithmetic and copies ran while one was open for 1% -> 0% of each run, Pallas kernels for 14% -> 16%
where the time goes in v3:
time: 172 us; the launch traced here: 171 us
  starting transfers between devices  63.7 us (37%)
  waiting for transfers between devices  46.9 us (27%)
  Pallas kernels  28.8 us (17%)
  blocking collectives  19.7 us (11%)
  local copies, waits for them, and re-layouts  7.56 us (4%)
  other arithmetic  2.43 us (1%)
    ppermute x8, starting transfers between devices, along_z(): lax.ppermute(x, 'cz', [(i - d, i) for i in range(n) if 0 <= i - d < n])  33.3 us
    ppermute x8, waiting for transfers between devices, along_z(): lax.ppermute(x, 'cz', [(i - d, i) for i in range(n) if 0 <= i - d < n])  25.8 us
    pallas_call x2, Pallas kernels, attention(): pl.pallas_call(attn_kernel, grid=(1,), in_specs=[wide, wide, whole, pl.Bl...  25.2 us
    all_to_all x1, blocking collectives, sum_among(): return lax.all_to_all(jnp.broadcast_to(x[None], (n,) + x.shape), axes, 0, 0)  19.7 us
    all_to_all x4, starting transfers between devices, swap_x(): return lax.all_to_all(x, 'cx', 0, 0)  16.8 us
    all_to_all x1, starting transfers between devices, sum_among(): return lax.all_to_all(jnp.broadcast_to(x[None], (n,) + x.shape), axes, 0, 0)  13.5 us
    all_to_all x1, waiting for transfers between devices, sum_among(): return lax.all_to_all(jnp.broadcast_to(x[None], (n,) + x.shape), axes, 0, 0)  11.2 us
    all_to_all x4, waiting for transfers between devices, swap_x(): return lax.all_to_all(x, 'cx', 0, 0)  9.89 us
  transfers between devices with their start and end apart: 13, of which 8 were waited for; matrix products, arithmetic and copies ran while one was open for 0% of the time, Pallas kernels for 16%

profile of v3, /device:TPU:1, one launch (start us, length us, event | category | flops | bytes accessed | tf_op | source)
XLA Modules:
  0.0 170.6 jit_solution(1601380723002778766)
XLA Ops:
  0.6 0.0 copy-start
  0.6 0.9 copy-done
  1.5 0.0 copy-start.2
  1.5 0.9 copy-done.2
  2.4 0.0 copy-start.4
  2.4 0.8 copy-done.4
  3.3 0.0 copy-start.5
  3.3 0.8 copy-done.5
  4.1 0.0 copy-start.6
  4.1 0.7 copy-done.6
  4.8 5.7 %collective-permute-start.1 = (bf16[136,512]{1,0:T(8,128)(2,1)S(1)}, bf16[136,512]{1,0:T(8,128)(2,1)S(1)}, u32[]{:S(2)}, u32[]{:S(2)}) collective-permute-start(bf16[136,512]{1,0:T(8,128)(2,1)S(1)} %shard_map.94.row_ref.own_ref), channel_id=1, source_target_pairs={{0,32},{16,48},{32,64},{48,80},{64,96},{80,112},{96,128},{112,144}... | collective-permute-start | bytes 417800 | tf_op jit(solution)/shard_map/ppermute | solution.py:257
  10.6 3.5 %collective-permute-start = (bf16[136,512]{1,0:T(8,128)(2,1)S(1)}, bf16[136,512]{1,0:T(8,128)(2,1)S(1)}, u32[]{:S(2)}, u32[]{:S(2)}) collective-permute-start(bf16[136,512]{1,0:T(8,128)(2,1)S(1)} %shard_map.94.row_ref.own_ref), channel_id=1, source_target_pairs={{0,16},{16,32},{32,48},{48,64},{64,80},{80,96},{96,112},{112,128},... | collective-permute-start | bytes 417800 | tf_op jit(solution)/shard_map/ppermute | solution.py:257
  14.1 0.0 collective-permute-done.1
  14.1 3.1 %collective-permute-done = bf16[136,512]{1,0:T(8,128)(2,1)S(1)} collective-permute-done((bf16[136,512]{1,0:T(8,128)(2,1)S(1)}, bf16[136,512]{1,0:T(8,128)(2,1)S(1)}, u32[]{:S(2)}, u32[]{:S(2)}) %collective-permute-start) | collective-permute-done | bytes 139296 | tf_op jit(solution)/shard_map/ppermute | solution.py:257
  17.3 7.7 %collective-permute-start.3 = (bf16[272,256]{1,0:T(8,128)(2,1)S(1)}, bf16[272,256]{1,0:T(8,128)(2,1)S(1)}, u32[]{:S(2)}, u32[]{:S(2)}) collective-permute-start(bf16[272,256]{1,0:T(8,128)(2,1)S(1)} %pad_maximum_fusion.1.near_ref), channel_id=1, source_target_pairs={{0,32},{16,48},{32,64},{48,80},{64,96},{80,112},{96,128},{112,144}... | collective-permute-start | bytes 417800 | tf_op jit(solution)/shard_map/ppermute | solution.py:257
  25.0 2.0 %collective-permute-done.3.far_ref = bf16[272,256]{1,0:T(8,128)(2,1)S(1)} collective-permute-done((bf16[272,256]{1,0:T(8,128)(2,1)S(1)}, bf16[272,256]{1,0:T(8,128)(2,1)S(1)}, u32[]{:S(2)}, u32[]{:S(2)}) %collective-permute-start.3) | collective-permute-done | bytes 139296 | tf_op jit(solution)/shard_map/ppermute | solution.py:257
  27.0 1.6 shard_map.96
  28.6 4.0 %all-to-all-start.1 = ((bf16[4,544,256]{2,1,0:T(8,128)(2,1)}), bf16[4,544,256]{2,1,0:T(8,128)(2,1)S(1)}, u32[]{:S(2)}, u32[]{:S(2)}) async-start(bf16[4,544,256]{2,1,0:T(8,128)(2,1)} %shard_map.96), calls=%async_computation.1 | async-start | bytes 2228224 | tf_op jit(solution)/shard_map/all_to_all | solution.py:261
  32.6 11.0 %collective-permute-start.2 = (bf16[272,256]{1,0:T(8,128)(2,1)S(1)}, bf16[272,256]{1,0:T(8,128)(2,1)S(1)}, u32[]{:S(2)}, u32[]{:S(2)}) collective-permute-start(bf16[272,256]{1,0:T(8,128)(2,1)S(1)} %pad_maximum_fusion.near_ref), channel_id=1, source_target_pairs={{0,32},{16,48},{32,64},{48,80},{64,96},{80,112},{96,128},{112,144}... | collective-permute-start | bytes 417800 | tf_op jit(solution)/shard_map/ppermute | solution.py:257
  43.6 2.0 %collective-permute-done.2.far_ref = bf16[272,256]{1,0:T(8,128)(2,1)S(1)} collective-permute-done((bf16[272,256]{1,0:T(8,128)(2,1)S(1)}, bf16[272,256]{1,0:T(8,128)(2,1)S(1)}, u32[]{:S(2)}, u32[]{:S(2)}) %collective-permute-start.2) | collective-permute-done | bytes 139296 | tf_op jit(solution)/shard_map/ppermute | solution.py:257
  45.6 1.6 shard_map.95
  47.2 0.0 copy-start.7
  47.2 0.0 all-to-all-done.1.win_ref
  47.2 4.4 %all-to-all-start = ((bf16[4,544,256]{2,1,0:T(8,128)(2,1)}), bf16[4,544,256]{2,1,0:T(8,128)(2,1)S(1)}, u32[]{:S(2)}, u32[]{:S(2)}) async-start(bf16[4,544,256]{2,1,0:T(8,128)(2,1)} %shard_map.95), calls=%async_computation | async-start | bytes 2228224 | tf_op jit(solution)/shard_map/all_to_all | solution.py:261
  51.6 0.0 copy-done.7
  51.6 0.0 copy-start.8
  51.6 1.0 copy-done.8
  52.6 12.6 %shard_map.97 = (bf16[128,2048]{1,0:T(8,128)(2,1)}, bf16[4,512,256]{2,1,0:T(8,128)(2,1)}, f32[128,256]{1,0:T(8,128)S(1)}) custom-call(bf16[128,2048]{1,0:T(8,128)(2,1)S(1)} %bitcast.33, bf16[128,2048]{1,0:T(8,128)(2,1)S(1)} %bitcast.36, bf16[4,544,256]{2,1,0:T(8,128)(2,1)S(1)} %all-to-all-done.1.win_ref, bf16[136,512]{1,0:T(8,128)(2,1)S(1)} %shard_map.94.row_ref.own_ref, ...), custom_call_target="tpu_custom_call" | custom-call | flops 2852126720 | bytes 4194304 | tf_op jit(solution)/shard_map/pallas_call | solution.py:123
  65.2 0.0 all-to-all-done.win_ref
  65.2 4.2 %all-to-all-start.2 = ((bf16[4,512,256]{2,1,0:T(8,128)(2,1)}), bf16[4,512,256]{2,1,0:T(8,128)(2,1)S(1)}, u32[]{:S(2)}, u32[]{:S(2)}) async-start(bf16[4,512,256]{2,1,0:T(8,128)(2,1)} %get-tuple-element.15), calls=%async_computation.2 | async-start | bytes 2097152 | tf_op jit(solution)/shard_map/all_to_all | solution.py:261
  69.5 0.0 copy-start.9
  69.5 1.0 copy-done.9
  70.5 12.6 %shard_map.98 = (bf16[128,2048]{1,0:T(8,128)(2,1)}, bf16[4,512,256]{2,1,0:T(8,128)(2,1)}, f32[128,256]{1,0:T(8,128)S(1)}) custom-call(bf16[128,2048]{1,0:T(8,128)(2,1)S(1)} %bitcast.35, bf16[128,2048]{1,0:T(8,128)(2,1)S(1)} %bitcast.37, bf16[4,544,256]{2,1,0:T(8,128)(2,1)S(1)} %all-to-all-done.win_ref, ...), custom_call_target="tpu_custom_call", output_to_operand_aliasing={{0}: (4, {})} | custom-call | flops 2852126720 | bytes 4194304 | tf_op jit(solution)/shard_map/pallas_call | solution.py:123
  83.1 0.0 all-to-all-done.2.back_ref
  83.1 4.2 %all-to-all-start.3 = ((bf16[4,512,256]{2,1,0:T(8,128)(2,1)}), bf16[4,512,256]{2,1,0:T(8,128)(2,1)S(1)}, u32[]{:S(2)}, u32[]{:S(2)}) async-start(bf16[4,512,256]{2,1,0:T(8,128)(2,1)} %get-tuple-element.18), calls=%async_computation.3 | async-start | bytes 2097152 | tf_op jit(solution)/shard_map/all_to_all | solution.py:261
  87.3 0.2 shard_map.99
  87.5 1.3 collective-permute-start.4
  88.8 9.9 %all-to-all-done.3.back_ref = bf16[4,512,256]{2,1,0:T(8,128)(2,1)S(1)} async-done(((bf16[4,512,256]{2,1,0:T(8,128)(2,1)}), bf16[4,512,256]{2,1,0:T(8,128)(2,1)S(1)}, u32[]{:S(2)}, u32[]{:S(2)}) %all-to-all-start.3) | async-done | bytes 1048608 | tf_op jit(solution)/shard_map/all_to_all | solution.py:261
  98.7 0.2 shard_map.100
  98.9 1.3 collective-permute-start.5
  100.2 0.4 collective-permute-done.4
  100.6 11.8 %collective-permute-done.5 = bf16[256,256]{1,0:T(8,128)(2,1)S(1)} collective-permute-done((bf16[256,256]{1,0:T(8,128)(2,1)S(1)}, bf16[256,256]{1,0:T(8,128)(2,1)S(1)}, u32[]{:S(2)}, u32[]{:S(2)}) %collective-permute-start.5) | collective-permute-done | bytes 131104 | tf_op jit(solution)/shard_map/ppermute | solution.py:257
  112.5 0.0 copy-start.1
  112.5 0.0 copy-start.3
  112.5 1.4 collective-permute-start.7
  114.0 1.3 collective-permute-start.6
  115.3 6.5 %collective-permute-done.7 = bf16[128,512]{1,0:T(8,128)(2,1)S(1)} collective-permute-done((bf16[128,512]{1,0:T(8,128)(2,1)S(1)}, bf16[128,512]{1,0:T(8,128)(2,1)S(1)}, u32[]{:S(2)}, u32[]{:S(2)}) %collective-permute-start.7) | collective-permute-done | bytes 131104 | tf_op jit(solution)/shard_map/ppermute | solution.py:257
  121.8 0.0 collective-permute-done.6
  121.9 0.0 copy-done.1
  121.9 0.0 copy-done.3
  121.9 0.2 multiply_reduce_fusion.4
  122.1 19.7 %all_to_all.30 = f32[32,3,128]{2,1,0:T(4,128)S(1)} all-to-all(f32[32,3,128]{2,1,0:T(4,128)S(1)} %broadcast_in_dim.8), channel_id=1, replica_groups=mesh['dp'=2,'cz'=16,'cx'=4,'tp'=4] {'dp','cx','tp'}, dimensions={0} | all-to-all | bytes 98304 | tf_op jit(solution)/shard_map/all_to_all | solution.py:266
  141.9 0.6 reduce_sum.87
  142.5 1.2 broadcast_in_dim_broadcast_in_dim_broadcast_in_dim.3
  143.7 13.5 %all-to-all-start.5 = ((f32[16,1,128]{2,1,0:T(1,128)}), f32[16,1,128]{2,1,0:T(1,128)S(1)}, u32[]{:S(2)}, u32[]{:S(2)}) async-start(f32[16,1,128]{2,1,0:T(1,128)} %broadcast_in_dim_broadcast_in_dim_broadcast_in_dim.3), calls=%async_computation.5 | async-start | bytes 16384 | tf_op jit(solution)/shard_map/all_to_all | solution.py:266
  157.3 11.2 %all-to-all-done.5 = f32[16,1,128]{2,1,0:T(1,128)S(1)} async-done(((f32[16,1,128]{2,1,0:T(1,128)}), f32[16,1,128]{2,1,0:T(1,128)S(1)}, u32[]{:S(2)}, u32[]{:S(2)}) %all-to-all-start.5) | async-done | bytes 8224 | tf_op jit(solution)/shard_map/all_to_all | solution.py:266
  168.5 0.6 slice_reduce_fusion
  169.9 0.8 fusion.4
  (19 shorter events, 0.3 us)
Async XLA Ops:
  0.6 0.9 copy-start
  1.5 0.9 copy-start.2
  2.4 0.8 copy-start.4
  3.3 0.8 copy-start.5
  4.1 0.7 copy-start.6
  4.8 9.3 %collective-permute-start.1 = (bf16[136,512]{1,0:T(8,128)(2,1)S(1)}, bf16[136,512]{1,0:T(8,128)(2,1)S(1)}, u32[]{:S(2)}, u32[]{:S(2)}) collective-permute-start(bf16[136,512]{1,0:T(8,128)(2,1)S(1)} %shard_map.94.row_ref.own_ref), channel_id=1, source_target_pairs={{0,32},{16,48},{32,64},{48,80},{64,96},{80,112},{96,128},{112,144}... | collective-permute-start | bytes 417800 | tf_op jit(solution)/shard_map/ppermute | solution.py:257
  10.6 6.7 %collective-permute-start = (bf16[136,512]{1,0:T(8,128)(2,1)S(1)}, bf16[136,512]{1,0:T(8,128)(2,1)S(1)}, u32[]{:S(2)}, u32[]{:S(2)}) collective-permute-start(bf16[136,512]{1,0:T(8,128)(2,1)S(1)} %shard_map.94.row_ref.own_ref), channel_id=1, source_target_pairs={{0,16},{16,32},{32,48},{48,64},{64,80},{80,96},{96,112},{112,128},... | collective-permute-start | bytes 417800 | tf_op jit(solution)/shard_map/ppermute | solution.py:257
  17.3 9.7 %collective-permute-start.3 = (bf16[272,256]{1,0:T(8,128)(2,1)S(1)}, bf16[272,256]{1,0:T(8,128)(2,1)S(1)}, u32[]{:S(2)}, u32[]{:S(2)}) collective-permute-start(bf16[272,256]{1,0:T(8,128)(2,1)S(1)} %pad_maximum_fusion.1.near_ref), channel_id=1, source_target_pairs={{0,32},{16,48},{32,64},{48,80},{64,96},{80,112},{96,128},{112,144}... | collective-permute-start | bytes 417800 | tf_op jit(solution)/shard_map/ppermute | solution.py:257
  28.6 18.6 %all-to-all-start.1 = ((bf16[4,544,256]{2,1,0:T(8,128)(2,1)}), bf16[4,544,256]{2,1,0:T(8,128)(2,1)S(1)}, u32[]{:S(2)}, u32[]{:S(2)}) async-start(bf16[4,544,256]{2,1,0:T(8,128)(2,1)} %shard_map.96), calls=%async_computation.1 | async-start | bytes 2228224 | tf_op jit(solution)/shard_map/all_to_all | solution.py:261
  32.6 13.0 %collective-permute-start.2 = (bf16[272,256]{1,0:T(8,128)(2,1)S(1)}, bf16[272,256]{1,0:T(8,128)(2,1)S(1)}, u32[]{:S(2)}, u32[]{:S(2)}) collective-permute-start(bf16[272,256]{1,0:T(8,128)(2,1)S(1)} %pad_maximum_fusion.near_ref), channel_id=1, source_target_pairs={{0,32},{16,48},{32,64},{48,80},{64,96},{80,112},{96,128},{112,144}... | collective-permute-start | bytes 417800 | tf_op jit(solution)/shard_map/ppermute | solution.py:257
  47.2 4.4 %copy-start.7 = (bf16[1,128,2048]{2,1,0:T(8,128)(2,1)S(1)}, bf16[1,128,2048]{2,1,0:T(8,128)(2,1)}, u32[]{:S(2)}) copy-start(bf16[1,128,2048]{2,1,0:T(8,128)(2,1)} %param.7) | copy-start | bytes 1572868
  47.2 18.0 %all-to-all-start = ((bf16[4,544,256]{2,1,0:T(8,128)(2,1)}), bf16[4,544,256]{2,1,0:T(8,128)(2,1)S(1)}, u32[]{:S(2)}, u32[]{:S(2)}) async-start(bf16[4,544,256]{2,1,0:T(8,128)(2,1)} %shard_map.95), calls=%async_computation | async-start | bytes 2228224 | tf_op jit(solution)/shard_map/all_to_all | solution.py:261
  51.6 1.0 copy-start.8
  65.2 17.9 %all-to-all-start.2 = ((bf16[4,512,256]{2,1,0:T(8,128)(2,1)}), bf16[4,512,256]{2,1,0:T(8,128)(2,1)S(1)}, u32[]{:S(2)}, u32[]{:S(2)}) async-start(bf16[4,512,256]{2,1,0:T(8,128)(2,1)} %get-tuple-element.15), calls=%async_computation.2 | async-start | bytes 2097152 | tf_op jit(solution)/shard_map/all_to_all | solution.py:261
  69.5 1.0 copy-start.9
  83.1 15.6 %all-to-all-start.3 = ((bf16[4,512,256]{2,1,0:T(8,128)(2,1)}), bf16[4,512,256]{2,1,0:T(8,128)(2,1)S(1)}, u32[]{:S(2)}, u32[]{:S(2)}) async-start(bf16[4,512,256]{2,1,0:T(8,128)(2,1)} %get-tuple-element.18), calls=%async_computation.3 | async-start | bytes 2097152 | tf_op jit(solution)/shard_map/all_to_all | solution.py:261
  87.5 13.1 %collective-permute-start.4 = (bf16[256,256]{1,0:T(8,128)(2,1)S(1)}, bf16[256,256]{1,0:T(8,128)(2,1)S(1)}, u32[]{:S(2)}, u32[]{:S(2)}) collective-permute-start(bf16[256,256]{1,0:T(8,128)(2,1)S(1)} %get-tuple-element.21), channel_id=1, source_target_pairs={{32,0},{48,16},{64,32},{80,48},{96,64},{112,80},{128,96},{144,112}... | collective-permute-start | bytes 393224 | tf_op jit(solution)/shard_map/ppermute | solution.py:257
  98.9 13.5 %collective-permute-start.5 = (bf16[256,256]{1,0:T(8,128)(2,1)S(1)}, bf16[256,256]{1,0:T(8,128)(2,1)S(1)}, u32[]{:S(2)}, u32[]{:S(2)}) collective-permute-start(bf16[256,256]{1,0:T(8,128)(2,1)S(1)} %get-tuple-element.22), channel_id=1, source_target_pairs={{32,0},{48,16},{64,32},{80,48},{96,64},{112,80},{128,96},{144,112}... | collective-permute-start | bytes 393224 | tf_op jit(solution)/shard_map/ppermute | solution.py:257
  112.5 9.4 %copy-start.1 = (f32[1,128,256]{2,1,0:T(8,128)S(1)}, f32[1,128,256]{2,1,0:T(8,128)}, u32[]{:S(2)}) copy-start(f32[1,128,256]{2,1,0:T(8,128)} %param.10) | copy-start | bytes 393220
  112.5 9.4 %copy-start.3 = (f32[1,128,256]{2,1,0:T(8,128)S(1)}, f32[1,128,256]{2,1,0:T(8,128)}, u32[]{:S(2)}) copy-start(f32[1,128,256]{2,1,0:T(8,128)} %param.11) | copy-start | bytes 393220
  112.5 9.2 %collective-permute-start.7 = (bf16[128,512]{1,0:T(8,128)(2,1)S(1)}, bf16[128,512]{1,0:T(8,128)(2,1)S(1)}, u32[]{:S(2)}, u32[]{:S(2)}) collective-permute-start(bf16[128,512]{1,0:T(8,128)(2,1)S(1)} %pad_maximum_fusion.3), channel_id=1, source_target_pairs={{32,0},{48,16},{64,32},{80,48},{96,64},{112,80},{128,96},{144,112}... | collective-permute-start | bytes 393224 | tf_op jit(solution)/shard_map/ppermute | solution.py:257
  114.0 7.8 %collective-permute-start.6 = (bf16[128,512]{1,0:T(8,128)(2,1)S(1)}, bf16[128,512]{1,0:T(8,128)(2,1)S(1)}, u32[]{:S(2)}, u32[]{:S(2)}) collective-permute-start(bf16[128,512]{1,0:T(8,128)(2,1)S(1)} %pad_maximum_fusion.2), channel_id=1, source_target_pairs={{16,0},{32,16},{48,32},{64,48},{80,64},{96,80},{112,96},{128,112},... | collective-permute-start | bytes 393224 | tf_op jit(solution)/shard_map/ppermute | solution.py:257
  143.7 24.8 %all-to-all-start.5 = ((f32[16,1,128]{2,1,0:T(1,128)}), f32[16,1,128]{2,1,0:T(1,128)S(1)}, u32[]{:S(2)}, u32[]{:S(2)}) async-start(f32[16,1,128]{2,1,0:T(1,128)} %broadcast_in_dim_broadcast_in_dim_broadcast_in_dim.3), calls=%async_computation.5 | async-start | bytes 16384 | tf_op jit(solution)/shard_map/all_to_all | solution.py:266

commit v4 on v3

--- a/solution.py
+++ b/solution.py
@@ -68,19 +68,14 @@
     for h in range(GROUP):
         qaug[h * tokens : (h + 1) * tokens, 0:HEAD] = q_ref[:, h * HEAD : (h + 1) * HEAD]
         qaug[h * tokens : (h + 1) * tokens, HEAD : HEAD + tokens] = eye
-    top = jnp.full((8, rows_all), -3e38, F32)
-    for j in range(len(blocks)):
-        rows = slice(j * tokens, (j + 1) * tokens)
-        s = mm(kaug[rows, :], qaug[...], NT)
-        s_ref[rows, :] = s
-        top = jnp.maximum(top, jnp.max(s.reshape(tokens // 8, 8, rows_all), 0))
+    scores = mm(kaug[...], qaug[...], NT)
+    s_ref[...] = scores
+    top = jnp.max(scores.reshape(scores.shape[0] // 8, 8, rows_all), 0)
     top = jnp.max(top, 0, keepdims=True)
     c = math.log2(math.e) / math.sqrt(HEAD)
     for j in range(len(blocks)):
         rows = slice(j * tokens, (j + 1) * tokens)
-        p = jnp.exp2((s_ref[rows, :] - top) * c)
-        s_ref[rows, :] = p
-        p_ref[rows, :] = p.astype(BF)
+        p_ref[rows, :] = jnp.exp2((s_ref[rows, :] - top) * c).astype(BF)
     lane = lax.broadcasted_iota(jnp.int32, (tokens, HEAD), 1)
     for pair in range(GROUP // 2):
         ot = mm(vat[...], p_ref[:, pair * 2 * tokens : (pair + 1) * 2 * tokens])
@@ -102,15 +97,14 @@
             taug[h * tokens : (h + 1) * tokens, 0:HEAD] = tp
             taug[h * tokens : (h + 1) * tokens, HEAD : 2 * HEAD] = ext.astype(BF)
     scale = 1.0 / math.sqrt(HEAD)
+    ds = (p_ref[...].astype(F32) * mm(vaug[...], taug[...], NT)).astype(BF)
+    dk = mm(ds, qaug[:, 0:HEAD]) * scale
+    dv = mm(p_ref[...], taug[:, 0:HEAD])
     for j, (_, g, b) in enumerate(blocks):
         rows = slice(j * tokens, (j + 1) * tokens)
         out_rows = slice(b * tokens, (b + 1) * tokens)
-        x = mm(vaug[rows, :], taug[...], NT)
-        ds = (s_ref[rows, :] * x).astype(BF)
-        dk = mm(ds, qaug[:, 0:HEAD]) * scale
-        dv = mm(p_ref[rows, :], taug[:, 0:HEAD])
-        g[out_rows, 0:HEAD] = dk.astype(g.dtype)
-        g[out_rows, HEAD : 2 * HEAD] = dv.astype(g.dtype)
+        g[out_rows, 0:HEAD] = dk[rows].astype(g.dtype)
+        g[out_rows, HEAD : 2 * HEAD] = dv[rows].astype(g.dtype)
 
 
 def attention(q, t, win, own, attn, head):
@@ -152,7 +146,13 @@
             bytes_accessed=4 << 20,
             transcendentals=keys * rows_all,
         ),
-    )(q, t, win, own, attn)
+    )(
+        pltpu.with_memory_space_constraint(q, pltpu.HBM),
+        pltpu.with_memory_space_constraint(t, pltpu.HBM),
+        win,
+        own,
+        attn,
+    )
 
 
 def prepare_kernel(k_ref, v_ref, ks_ref, vs_ref, docs_ref, row_ref):
@@ -174,41 +174,38 @@
     return pl.pallas_call(
         prepare_kernel,
         out_shape=jax.ShapeDtypeStruct((tokens + TAIL, 2 * width), BF),
-        compiler_params=pltpu.CompilerParams(vmem_limit_bytes=4 << 20),
         cost_estimate=pl.CostEstimate(flops=1 << 17, bytes_accessed=1 << 19, transcendentals=0),
     )(k, v, ks, vs, docs)
 
 
 def spread_kernel(x_ref, row_ref, near_ref, far_ref, out_ref):
     rows = row_ref.shape[0]
-    target = pl.program_id(0)
-
-    @pl.when(target > x_ref[0])
-    def _():
-        out_ref[0, 0:rows, :] = row_ref[...]
-
-    @pl.when(target <= x_ref[0])
-    def _():
-        out_ref[0, 0:rows, :] = far_ref[rows:, :]
-
-    out_ref[0, rows : 3 * rows, :] = near_ref[...]
-    out_ref[0, 3 * rows :, :] = far_ref[0:rows, :]
+    for i in range(out_ref.shape[0]):
+        @pl.when(i > x_ref[0])
+        def _():
+            out_ref[i, 0:rows, :] = row_ref[...]
+
+        @pl.when(i <= x_ref[0])
+        def _():
+            out_ref[i, 0:rows, :] = far_ref[rows:, :]
+
+        out_ref[i, rows : 3 * rows, :] = near_ref[...]
+        out_ref[i, 3 * rows :, :] = far_ref[0:rows, :]
 
 
 def spread(where_x, row, near, far, head, n):
     rows, width = near.shape
+    whole = pl.BlockSpec(memory_space=pltpu.VMEM)
     return pl.pallas_call(
         spread_kernel,
-        grid_spec=pltpu.PrefetchScalarGridSpec(
-            num_scalar_prefetch=1,
-            grid=(n,),
-            in_specs=[
-                pl.BlockSpec((rows // 2, width), lambda g, x: (0, head)),
-                pl.BlockSpec((rows, width), lambda g, x: (0, 0)),
-                pl.BlockSpec((rows, width), lambda g, x: (0, 0)),
-            ],
-            out_specs=pl.BlockSpec((1, 2 * rows, width), lambda g, x: (g, 0, 0)),
-        ),
+        grid=(1,),
+        in_specs=[
+            pl.BlockSpec(memory_space=pltpu.SMEM),
+            pl.BlockSpec((rows // 2, width), lambda g: (0, head)),
+            whole,
+            whole,
+        ],
+        out_specs=whole,
         out_shape=jax.ShapeDtypeStruct((n, 2 * rows, width), BF),
         compiler_params=pltpu.CompilerParams(vmem_limit_bytes=8 << 20),
         cost_estimate=pl.CostEstimate(flops=0, bytes_accessed=2 << 20, transcendentals=0),
@@ -250,6 +247,51 @@
         compiler_params=pltpu.CompilerParams(vmem_limit_bytes=8 << 20),
         cost_estimate=pl.CostEstimate(flops=1 << 19, bytes_accessed=2 << 20, transcendentals=0),
     )(where_x, back, gown)
+
+
+def gather_kernel(n_tp, first_ref, plane_ref, near_ref, out_ref):
+    square = jnp.sum(plane_ref[:, 2, :])
+    out_ref[...] = jnp.full(out_ref.shape, square, F32)
+    near_ref[...] = jnp.sum(plane_ref[pl.ds(first_ref[0], n_tp)], 0)
+
+
+def gather(first, plane, n, n_tp):
+    vmem = pl.BlockSpec(memory_space=pltpu.VMEM)
+    return pl.pallas_call(
+        functools.partial(gather_kernel, n_tp),
+        in_specs=[pl.BlockSpec(memory_space=pltpu.SMEM), vmem],
+        out_specs=[vmem, vmem],
+        out_shape=[
+            jax.ShapeDtypeStruct(plane.shape[1:], F32),
+            jax.ShapeDtypeStruct((n, 1, plane.shape[2]), F32),
+        ],
+        compiler_params=pltpu.CompilerParams(vmem_limit_bytes=4 << 20),
+        cost_estimate=pl.CostEstimate(flops=1 << 14, bytes_accessed=1 << 16, transcendentals=0),
+    )(first, plane)
+
+
+def update_kernel(count, all_ref, near_ref, ks_ref, vs_ref, grad_ref, nk_ref, nv_ref):
+    tokens = ks_ref.shape[0]
+    overall = jnp.sum(all_ref[...], 0)
+    a = step_size / jnp.sqrt(overall / count + 1e-05)
+    near = near_ref[...]
+    size_sq = jnp.maximum(near[0:1] + 2.0 * a * near[1:2] + a * a * near[2:3], 0.0)
+    radius = radius_scale * math.sqrt(2 * KV_HEADS * HEAD)
+    factor = jnp.minimum(1.0, radius / jnp.sqrt(size_sq + 1e-06))
+    factor = jnp.broadcast_to(factor, (tokens, tokens)).T
+    for h in range(ks_ref.shape[1] // HEAD):
+        part = slice(h * HEAD, (h + 1) * HEAD)
+        nk_ref[:, part] = (ks_ref[:, part] + a * grad_ref[:, 2 * h * HEAD : (2 * h + 1) * HEAD]) * factor
+        nv_ref[:, part] = (vs_ref[:, part] + a * grad_ref[:, (2 * h + 1) * HEAD : (2 * h + 2) * HEAD]) * factor
+
+
+def update(count, everything, near, ks, vs, grad):
+    return pl.pallas_call(
+        functools.partial(update_kernel, count),
+        out_shape=[jax.ShapeDtypeStruct(ks.shape, F32)] * 2,
+        compiler_params=pltpu.CompilerParams(vmem_limit_bytes=4 << 20),
+        cost_estimate=pl.CostEstimate(flops=1 << 17, bytes_accessed=1 << 20, transcendentals=256),
+    )(everything, near, ks, vs, grad)
 
 
 def along_z(x, d):
@@ -314,25 +356,12 @@
     )
     n_dp, n_tp = lax.axis_size("dp"), lax.axis_size("tp")
     plane = sum_among(sums, ("dp", "cx", "tp"))
-    near = jnp.sum(
-        lax.dynamic_slice_in_dim(
-            plane, (lax.axis_index("dp") * n_x + where_x) * n_tp, n_tp, 0
-        ),
-        0,
-    )
-    square = jnp.sum(plane[:, 2])
-    overall = jnp.sum(sum_among(jnp.full((1, 128), square), ("cz",))[:, 0, 0])
+    first = ((lax.axis_index("dp") * n_x + where_x) * n_tp).astype(jnp.int32)[None]
+    near, square = gather(first, plane, lax.axis_size("cz"), n_tp)
+    everything = lax.all_to_all(square, "cz", 0, 0)
     count = n_dp * tokens * n_x * lax.axis_size("cz") * 2 * KV_HEADS * HEAD
-    rms = jnp.sqrt(overall / count + 1e-05)
-    a = step_size / rms
-    size_sq = jnp.maximum(near[0] + 2.0 * a * near[1] + a * a * near[2], 0.0)
-    radius = radius_scale * math.sqrt(2 * KV_HEADS * HEAD)
-    factor = jnp.minimum(1.0, radius / jnp.sqrt(size_sq + 1e-06))[:, None]
-    return (
-        attn[None],
-        ((ks + a * grad_key) * factor)[None],
-        ((vs + a * grad_val) * factor)[None],
-    )
+    new_ks, new_vs = update(count, everything, near, ks, vs, grad)
+    return attn[None], new_ks[None], new_vs[None]
 
 
 def solution(mesh):

time: 172 us -> 165 us (0.959)
  local copies, waits for them, and re-layouts: 7.56 us -> 1.6 us
  blocking collectives: 19.7 us -> 25 us
  Pallas kernels: 28.8 us -> 23.6 us
  waiting for transfers between devices: 46.9 us -> 49.9 us
  other arithmetic: 2.43 us -> 0.37 us
    pallas_call x2, Pallas kernels: 25.2 us -> 18.3 us  [attention(): pl.pallas_call(attn_kernel, grid=(1,), in_specs=[wide, wide, whole, pl.Bl...]
    unnamed x20 -> x8, local copies, waits for them, and re-layouts: 6.23 us -> 0.92 us
    all_to_all x1, blocking collectives: 19.7 us -> 25 us  [per_device(): everything = lax.all_to_all(square, 'cz', 0, 0)]
    all_to_all x4, waiting for transfers between devices: 9.89 us -> 15.1 us  [swap_x(): return lax.all_to_all(x, 'cx', 0, 0)]
    all_to_all x1, waiting for transfers between devices: 11.2 us -> 7.13 us  [sum_among(): return lax.all_to_all(jnp.broadcast_to(x[None], (n,) + x.shape), axes, 0, 0)]
    ppermute x8, waiting for transfers between devices: 25.8 us -> 27.6 us  [along_z(): lax.ppermute(x, 'cz', [(i - d, i) for i in range(n) if 0 <= i - d < n])]
  transfers between devices with their start and end apart: 13 -> 13, of which waited for: 8 -> 11; matrix products, arithmetic and copies ran while one was open for 0% -> 0% of each run, Pallas kernels for 16% -> 12%
where the time goes in v4:
time: 165 us; the launch traced here: 164 us
  starting transfers between devices  62.6 us (38%)
  waiting for transfers between devices  49.9 us (30%)
  blocking collectives  25 us (15%)
  Pallas kernels  23.6 us (14%)
    ppermute x8, starting transfers between devices, along_z(): lax.ppermute(x, 'cz', [(i - d, i) for i in range(n) if 0 <= i - d < n])  33.2 us
    ppermute x8, waiting for transfers between devices, along_z(): lax.ppermute(x, 'cz', [(i - d, i) for i in range(n) if 0 <= i - d < n])  27.6 us
    all_to_all x1, blocking collectives, per_device(): everything = lax.all_to_all(square, 'cz', 0, 0)  25 us
    pallas_call x2, Pallas kernels, attention(): pl.pallas_call(attn_kernel, grid=(1,), in_specs=[wide, wide, whole, pl.Bl...  18.3 us
    all_to_all x4, starting transfers between devices, swap_x(): return lax.all_to_all(x, 'cx', 0, 0)  15.5 us
    all_to_all x4, waiting for transfers between devices, swap_x(): return lax.all_to_all(x, 'cx', 0, 0)  15.1 us
    all_to_all x1, starting transfers between devices, sum_among(): return lax.all_to_all(jnp.broadcast_to(x[None], (n,) + x.shape), axes, 0, 0)  13.9 us
    all_to_all x1, waiting for transfers between devices, sum_among(): return lax.all_to_all(jnp.broadcast_to(x[None], (n,) + x.shape), axes, 0, 0)  7.13 us
  transfers between devices with their start and end apart: 13, of which 11 were waited for; matrix products, arithmetic and copies ran while one was open for 0% of the time, Pallas kernels for 12%

profile of v4, /device:TPU:1, one launch (start us, length us, event | category | flops | bytes accessed | tf_op | source)
XLA Modules:
  0.0 163.9 jit_solution(10662116683930873541)
XLA Ops:
  0.6 1.7 %shard_map.94.row_ref.own_ref = bf16[136,512]{1,0:T(8,128)(2,1)} custom-call(bf16[128,256]{1,0:T(8,128)(2,1)} %bitcast.25, bf16[128,256]{1,0:T(8,128)(2,1)} %bitcast.26, f32[128,256]{1,0:T(8,128)} %bitcast.21, f32[128,256]{1,0:T(8,128)} %bitcast.23, s32[1,128]{1,0:T(1,128)} %docs_ref.1), custom_call_target="tpu_custom_call" | custom-call | flops 131072 | bytes 524288 | tf_op jit(solution)/shard_map/pallas_call | solution.py:174
  2.4 5.7 %collective-permute-start.1 = (bf16[136,512]{1,0:T(8,128)(2,1)}, bf16[136,512]{1,0:T(8,128)(2,1)S(1)}, u32[]{:S(2)}, u32[]{:S(2)}) collective-permute-start(bf16[136,512]{1,0:T(8,128)(2,1)} %shard_map.94.row_ref.own_ref), channel_id=1, source_target_pairs={{0,32},{16,48},{32,64},{48,80},{64,96},{80,112},{96,128},{112,144}... | collective-permute-start | bytes 417800 | tf_op jit(solution)/shard_map/ppermute | solution.py:299
  8.1 3.5 %collective-permute-start = (bf16[136,512]{1,0:T(8,128)(2,1)}, bf16[136,512]{1,0:T(8,128)(2,1)S(1)}, u32[]{:S(2)}, u32[]{:S(2)}) collective-permute-start(bf16[136,512]{1,0:T(8,128)(2,1)} %shard_map.94.row_ref.own_ref), channel_id=1, source_target_pairs={{0,16},{16,32},{32,48},{48,64},{64,80},{80,96},{96,112},{112,128},... | collective-permute-start | bytes 417800 | tf_op jit(solution)/shard_map/ppermute | solution.py:299
  11.6 0.0 collective-permute-done.1
  11.7 3.4 %collective-permute-done = bf16[136,512]{1,0:T(8,128)(2,1)S(1)} collective-permute-done((bf16[136,512]{1,0:T(8,128)(2,1)}, bf16[136,512]{1,0:T(8,128)(2,1)S(1)}, u32[]{:S(2)}, u32[]{:S(2)}) %collective-permute-start) | collective-permute-done | bytes 139296 | tf_op jit(solution)/shard_map/ppermute | solution.py:299
  15.1 7.7 %collective-permute-start.3 = (bf16[272,256]{1,0:T(8,128)(2,1)S(1)}, bf16[272,256]{1,0:T(8,128)(2,1)S(1)}, u32[]{:S(2)}, u32[]{:S(2)}) collective-permute-start(bf16[272,256]{1,0:T(8,128)(2,1)S(1)} %pad_maximum_fusion.1.near_ref), channel_id=1, source_target_pairs={{0,32},{16,48},{32,64},{48,80},{64,96},{80,112},{96,128},{112,144}... | collective-permute-start | bytes 417800 | tf_op jit(solution)/shard_map/ppermute | solution.py:299
  22.8 2.0 %collective-permute-done.3.far_ref = bf16[272,256]{1,0:T(8,128)(2,1)S(1)} collective-permute-done((bf16[272,256]{1,0:T(8,128)(2,1)S(1)}, bf16[272,256]{1,0:T(8,128)(2,1)S(1)}, u32[]{:S(2)}, u32[]{:S(2)}) %collective-permute-start.3) | collective-permute-done | bytes 139296 | tf_op jit(solution)/shard_map/ppermute | solution.py:299
  24.8 0.0 copy-start
  24.8 0.9 copy-done
  25.7 1.1 shard_map.96
  26.8 0.0 copy-start.1
  26.8 4.1 %all-to-all-start.1 = ((bf16[4,544,256]{2,1,0:T(8,128)(2,1)}), bf16[4,544,256]{2,1,0:T(8,128)(2,1)S(1)}, u32[]{:S(2)}, u32[]{:S(2)}) async-start(bf16[4,544,256]{2,1,0:T(8,128)(2,1)} %shard_map.96), calls=%async_computation.1 | async-start | bytes 2228224 | tf_op jit(solution)/shard_map/all_to_all | solution.py:303
  31.0 10.9 %collective-permute-start.2 = (bf16[272,256]{1,0:T(8,128)(2,1)S(1)}, bf16[272,256]{1,0:T(8,128)(2,1)S(1)}, u32[]{:S(2)}, u32[]{:S(2)}) collective-permute-start(bf16[272,256]{1,0:T(8,128)(2,1)S(1)} %pad_maximum_fusion.near_ref), channel_id=1, source_target_pairs={{0,32},{16,48},{32,64},{48,80},{64,96},{80,112},{96,128},{112,144}... | collective-permute-start | bytes 417800 | tf_op jit(solution)/shard_map/ppermute | solution.py:299
  41.9 2.0 %collective-permute-done.2.far_ref = bf16[272,256]{1,0:T(8,128)(2,1)S(1)} collective-permute-done((bf16[272,256]{1,0:T(8,128)(2,1)S(1)}, bf16[272,256]{1,0:T(8,128)(2,1)S(1)}, u32[]{:S(2)}, u32[]{:S(2)}) %collective-permute-start.2) | collective-permute-done | bytes 139296 | tf_op jit(solution)/shard_map/ppermute | solution.py:299
  43.9 0.0 copy-done.1
  43.9 1.1 shard_map.95
  45.0 0.0 all-to-all-done.1.win_ref
  45.0 4.2 %all-to-all-start = ((bf16[4,544,256]{2,1,0:T(8,128)(2,1)}), bf16[4,544,256]{2,1,0:T(8,128)(2,1)S(1)}, u32[]{:S(2)}, u32[]{:S(2)}) async-start(bf16[4,544,256]{2,1,0:T(8,128)(2,1)} %shard_map.95), calls=%async_computation | async-start | bytes 2228224 | tf_op jit(solution)/shard_map/all_to_all | solution.py:303
  49.2 9.2 %shard_map.97 = (bf16[128,2048]{1,0:T(8,128)(2,1)}, bf16[4,512,256]{2,1,0:T(8,128)(2,1)}, f32[128,256]{1,0:T(8,128)S(1)}) custom-call(bf16[128,2048]{1,0:T(8,128)(2,1)} %bitcast.27, bf16[128,2048]{1,0:T(8,128)(2,1)} %bitcast.30, bf16[4,544,256]{2,1,0:T(8,128)(2,1)S(1)} %all-to-all-done.1.win_ref, bf16[136,512]{1,0:T(8,128)(2,1)S(1)} %copy-done.1, ...), custom_call_target="tpu_custom_call" | custom-call | flops 2852126720 | bytes 4194304 | tf_op jit(solution)/shard_map/pallas_call | solution.py:117
  58.3 4.3 %all-to-all-done.win_ref = bf16[4,544,256]{2,1,0:T(8,128)(2,1)S(1)} async-done(((bf16[4,544,256]{2,1,0:T(8,128)(2,1)}), bf16[4,544,256]{2,1,0:T(8,128)(2,1)S(1)}, u32[]{:S(2)}, u32[]{:S(2)}) %all-to-all-start) | async-done | bytes 1114144 | tf_op jit(solution)/shard_map/all_to_all | solution.py:303
  62.6 3.7 %all-to-all-start.2 = ((bf16[4,512,256]{2,1,0:T(8,128)(2,1)}), bf16[4,512,256]{2,1,0:T(8,128)(2,1)S(1)}, u32[]{:S(2)}, u32[]{:S(2)}) async-start(bf16[4,512,256]{2,1,0:T(8,128)(2,1)} %get-tuple-element.19), calls=%async_computation.2 | async-start | bytes 2097152 | tf_op jit(solution)/shard_map/all_to_all | solution.py:303
  66.3 9.2 %shard_map.98 = (bf16[128,2048]{1,0:T(8,128)(2,1)}, bf16[4,512,256]{2,1,0:T(8,128)(2,1)}, f32[128,256]{1,0:T(8,128)S(1)}) custom-call(bf16[128,2048]{1,0:T(8,128)(2,1)} %bitcast.29, bf16[128,2048]{1,0:T(8,128)(2,1)} %bitcast.31, bf16[4,544,256]{2,1,0:T(8,128)(2,1)S(1)} %all-to-all-done.win_ref, ...), custom_call_target="tpu_custom_call", output_to_operand_aliasing={{0}: (4, {})} | custom-call | flops 2852126720 | bytes 4194304 | tf_op jit(solution)/shard_map/pallas_call | solution.py:117
  75.4 2.1 %all-to-all-done.2.back_ref = bf16[4,512,256]{2,1,0:T(8,128)(2,1)S(1)} async-done(((bf16[4,512,256]{2,1,0:T(8,128)(2,1)}), bf16[4,512,256]{2,1,0:T(8,128)(2,1)S(1)}, u32[]{:S(2)}, u32[]{:S(2)}) %all-to-all-start.2) | async-done | bytes 1048608 | tf_op jit(solution)/shard_map/all_to_all | solution.py:303
  77.6 3.5 %all-to-all-start.3 = ((bf16[4,512,256]{2,1,0:T(8,128)(2,1)}), bf16[4,512,256]{2,1,0:T(8,128)(2,1)S(1)}, u32[]{:S(2)}, u32[]{:S(2)}) async-start(bf16[4,512,256]{2,1,0:T(8,128)(2,1)} %get-tuple-element.22), calls=%async_computation.3 | async-start | bytes 2097152 | tf_op jit(solution)/shard_map/all_to_all | solution.py:303
  81.1 0.2 shard_map.99
  81.3 1.3 collective-permute-start.4
  82.6 8.7 %all-to-all-done.3.back_ref = bf16[4,512,256]{2,1,0:T(8,128)(2,1)S(1)} async-done(((bf16[4,512,256]{2,1,0:T(8,128)(2,1)}), bf16[4,512,256]{2,1,0:T(8,128)(2,1)S(1)}, u32[]{:S(2)}, u32[]{:S(2)}) %all-to-all-start.3) | async-done | bytes 1048608 | tf_op jit(solution)/shard_map/all_to_all | solution.py:303
  91.3 0.2 shard_map.100
  91.5 1.3 collective-permute-start.5
  92.8 3.0 %collective-permute-done.4 = bf16[256,256]{1,0:T(8,128)(2,1)S(1)} collective-permute-done((bf16[256,256]{1,0:T(8,128)(2,1)S(1)}, bf16[256,256]{1,0:T(8,128)(2,1)S(1)}, u32[]{:S(2)}, u32[]{:S(2)}) %collective-permute-start.4) | collective-permute-done | bytes 131104 | tf_op jit(solution)/shard_map/ppermute | solution.py:299
  95.9 10.5 %collective-permute-done.5 = bf16[256,256]{1,0:T(8,128)(2,1)S(1)} collective-permute-done((bf16[256,256]{1,0:T(8,128)(2,1)S(1)}, bf16[256,256]{1,0:T(8,128)(2,1)S(1)}, u32[]{:S(2)}, u32[]{:S(2)}) %collective-permute-start.5) | collective-permute-done | bytes 131104 | tf_op jit(solution)/shard_map/ppermute | solution.py:299
  106.4 0.0 copy-start.2
  106.4 0.0 copy-start.3
  106.5 1.4 collective-permute-start.7
  107.9 1.3 collective-permute-start.6
  109.2 6.5 %collective-permute-done.7 = bf16[128,512]{1,0:T(8,128)(2,1)S(1)} collective-permute-done((bf16[128,512]{1,0:T(8,128)(2,1)S(1)}, bf16[128,512]{1,0:T(8,128)(2,1)S(1)}, u32[]{:S(2)}, u32[]{:S(2)}) %collective-permute-start.7) | collective-permute-done | bytes 131104 | tf_op jit(solution)/shard_map/ppermute | solution.py:299
  115.8 0.1 collective-permute-done.6
  116.0 0.0 copy-done.2
  116.0 0.0 copy-done.3
  116.0 0.2 multiply_reduce_fusion.4
  116.2 0.6 broadcast_in_dim.24
  116.9 13.9 %all-to-all-start.4 = ((f32[32,3,128]{2,1,0:T(4,128)}), f32[32,3,128]{2,1,0:T(4,128)S(1)}, u32[]{:S(2)}, u32[]{:S(2)}) async-start(f32[32,3,128]{2,1,0:T(4,128)} %broadcast_in_dim.24), calls=%async_computation.4 | async-start | bytes 131072 | tf_op jit(solution)/shard_map/all_to_all | solution.py:308
  130.8 7.1 %all-to-all-done.4.plane_ref = f32[32,3,128]{2,1,0:T(4,128)S(1)} async-done(((f32[32,3,128]{2,1,0:T(4,128)}), f32[32,3,128]{2,1,0:T(4,128)S(1)}, u32[]{:S(2)}, u32[]{:S(2)}) %all-to-all-start.4) | async-done | bytes 49184 | tf_op jit(solution)/shard_map/all_to_all | solution.py:308
  137.9 0.1 shard_map.101
  138.1 25.0 %all_to_all.30.all_ref = f32[16,1,128]{2,1,0:T(1,128)S(1)} all-to-all(f32[16,1,128]{2,1,0:T(1,128)S(1)} %get-tuple-element.27), channel_id=1, replica_groups=mesh['dp'=2,'cz'=16,'cx'=4,'tp'=4] {'cz'}, dimensions={0} | all-to-all | bytes 16384 | tf_op jit(solution)/shard_map/all_to_all | solution.py:361
  163.0 0.9 shard_map.102
  (14 shorter events, 0.2 us)
Async XLA Ops:
  2.4 9.3 %collective-permute-start.1 = (bf16[136,512]{1,0:T(8,128)(2,1)}, bf16[136,512]{1,0:T(8,128)(2,1)S(1)}, u32[]{:S(2)}, u32[]{:S(2)}) collective-permute-start(bf16[136,512]{1,0:T(8,128)(2,1)} %shard_map.94.row_ref.own_ref), channel_id=1, source_target_pairs={{0,32},{16,48},{32,64},{48,80},{64,96},{80,112},{96,128},{112,144}... | collective-permute-start | bytes 417800 | tf_op jit(solution)/shard_map/ppermute | solution.py:299
  8.1 7.0 %collective-permute-start = (bf16[136,512]{1,0:T(8,128)(2,1)}, bf16[136,512]{1,0:T(8,128)(2,1)S(1)}, u32[]{:S(2)}, u32[]{:S(2)}) collective-permute-start(bf16[136,512]{1,0:T(8,128)(2,1)} %shard_map.94.row_ref.own_ref), channel_id=1, source_target_pairs={{0,16},{16,32},{32,48},{48,64},{64,80},{80,96},{96,112},{112,128},... | collective-permute-start | bytes 417800 | tf_op jit(solution)/shard_map/ppermute | solution.py:299
  15.1 9.7 %collective-permute-start.3 = (bf16[272,256]{1,0:T(8,128)(2,1)S(1)}, bf16[272,256]{1,0:T(8,128)(2,1)S(1)}, u32[]{:S(2)}, u32[]{:S(2)}) collective-permute-start(bf16[272,256]{1,0:T(8,128)(2,1)S(1)} %pad_maximum_fusion.1.near_ref), channel_id=1, source_target_pairs={{0,32},{16,48},{32,64},{48,80},{64,96},{80,112},{96,128},{112,144}... | collective-permute-start | bytes 417800 | tf_op jit(solution)/shard_map/ppermute | solution.py:299
  24.8 0.9 copy-start
  26.8 17.0 %copy-start.1 = (bf16[136,512]{1,0:T(8,128)(2,1)S(1)}, bf16[136,512]{1,0:T(8,128)(2,1)}, u32[]{:S(2)}) copy-start(bf16[136,512]{1,0:T(8,128)(2,1)} %shard_map.94.row_ref.own_ref) | copy-start | bytes 417796
  26.8 18.2 %all-to-all-start.1 = ((bf16[4,544,256]{2,1,0:T(8,128)(2,1)}), bf16[4,544,256]{2,1,0:T(8,128)(2,1)S(1)}, u32[]{:S(2)}, u32[]{:S(2)}) async-start(bf16[4,544,256]{2,1,0:T(8,128)(2,1)} %shard_map.96), calls=%async_computation.1 | async-start | bytes 2228224 | tf_op jit(solution)/shard_map/all_to_all | solution.py:303
  31.0 12.9 %collective-permute-start.2 = (bf16[272,256]{1,0:T(8,128)(2,1)S(1)}, bf16[272,256]{1,0:T(8,128)(2,1)S(1)}, u32[]{:S(2)}, u32[]{:S(2)}) collective-permute-start(bf16[272,256]{1,0:T(8,128)(2,1)S(1)} %pad_maximum_fusion.near_ref), channel_id=1, source_target_pairs={{0,32},{16,48},{32,64},{48,80},{64,96},{80,112},{96,128},{112,144}... | collective-permute-start | bytes 417800 | tf_op jit(solution)/shard_map/ppermute | solution.py:299
  45.0 17.6 %all-to-all-start = ((bf16[4,544,256]{2,1,0:T(8,128)(2,1)}), bf16[4,544,256]{2,1,0:T(8,128)(2,1)S(1)}, u32[]{:S(2)}, u32[]{:S(2)}) async-start(bf16[4,544,256]{2,1,0:T(8,128)(2,1)} %shard_map.95), calls=%async_computation | async-start | bytes 2228224 | tf_op jit(solution)/shard_map/all_to_all | solution.py:303
  62.6 15.0 %all-to-all-start.2 = ((bf16[4,512,256]{2,1,0:T(8,128)(2,1)}), bf16[4,512,256]{2,1,0:T(8,128)(2,1)S(1)}, u32[]{:S(2)}, u32[]{:S(2)}) async-start(bf16[4,512,256]{2,1,0:T(8,128)(2,1)} %get-tuple-element.19), calls=%async_computation.2 | async-start | bytes 2097152 | tf_op jit(solution)/shard_map/all_to_all | solution.py:303
  77.6 13.8 %all-to-all-start.3 = ((bf16[4,512,256]{2,1,0:T(8,128)(2,1)}), bf16[4,512,256]{2,1,0:T(8,128)(2,1)S(1)}, u32[]{:S(2)}, u32[]{:S(2)}) async-start(bf16[4,512,256]{2,1,0:T(8,128)(2,1)} %get-tuple-element.22), calls=%async_computation.3 | async-start | bytes 2097152 | tf_op jit(solution)/shard_map/all_to_all | solution.py:303
  81.3 14.6 %collective-permute-start.4 = (bf16[256,256]{1,0:T(8,128)(2,1)S(1)}, bf16[256,256]{1,0:T(8,128)(2,1)S(1)}, u32[]{:S(2)}, u32[]{:S(2)}) collective-permute-start(bf16[256,256]{1,0:T(8,128)(2,1)S(1)} %get-tuple-element.25), channel_id=1, source_target_pairs={{32,0},{48,16},{64,32},{80,48},{96,64},{112,80},{128,96},{144,112}... | collective-permute-start | bytes 393224 | tf_op jit(solution)/shard_map/ppermute | solution.py:299
  91.5 14.9 %collective-permute-start.5 = (bf16[256,256]{1,0:T(8,128)(2,1)S(1)}, bf16[256,256]{1,0:T(8,128)(2,1)S(1)}, u32[]{:S(2)}, u32[]{:S(2)}) collective-permute-start(bf16[256,256]{1,0:T(8,128)(2,1)S(1)} %get-tuple-element.26), channel_id=1, source_target_pairs={{32,0},{48,16},{64,32},{80,48},{96,64},{112,80},{128,96},{144,112}... | collective-permute-start | bytes 393224 | tf_op jit(solution)/shard_map/ppermute | solution.py:299
  106.4 9.6 %copy-start.2 = (f32[1,128,256]{2,1,0:T(8,128)S(1)}, f32[1,128,256]{2,1,0:T(8,128)}, u32[]{:S(2)}) copy-start(f32[1,128,256]{2,1,0:T(8,128)} %param.10) | copy-start | bytes 393220
  106.4 9.6 %copy-start.3 = (f32[1,128,256]{2,1,0:T(8,128)S(1)}, f32[1,128,256]{2,1,0:T(8,128)}, u32[]{:S(2)}) copy-start(f32[1,128,256]{2,1,0:T(8,128)} %param.11) | copy-start | bytes 393220
  106.5 9.3 %collective-permute-start.7 = (bf16[128,512]{1,0:T(8,128)(2,1)S(1)}, bf16[128,512]{1,0:T(8,128)(2,1)S(1)}, u32[]{:S(2)}, u32[]{:S(2)}) collective-permute-start(bf16[128,512]{1,0:T(8,128)(2,1)S(1)} %pad_maximum_fusion.3), channel_id=1, source_target_pairs={{32,0},{48,16},{64,32},{80,48},{96,64},{112,80},{128,96},{144,112}... | collective-permute-start | bytes 393224 | tf_op jit(solution)/shard_map/ppermute | solution.py:299
  107.9 8.0 %collective-permute-start.6 = (bf16[128,512]{1,0:T(8,128)(2,1)S(1)}, bf16[128,512]{1,0:T(8,128)(2,1)S(1)}, u32[]{:S(2)}, u32[]{:S(2)}) collective-permute-start(bf16[128,512]{1,0:T(8,128)(2,1)S(1)} %pad_maximum_fusion.2), channel_id=1, source_target_pairs={{16,0},{32,16},{48,32},{64,48},{80,64},{96,80},{112,96},{128,112},... | collective-permute-start | bytes 393224 | tf_op jit(solution)/shard_map/ppermute | solution.py:299
  116.9 21.0 %all-to-all-start.4 = ((f32[32,3,128]{2,1,0:T(4,128)}), f32[32,3,128]{2,1,0:T(4,128)S(1)}, u32[]{:S(2)}, u32[]{:S(2)}) async-start(f32[32,3,128]{2,1,0:T(4,128)} %broadcast_in_dim.24), calls=%async_computation.4 | async-start | bytes 131072 | tf_op jit(solution)/shard_map/all_to_all | solution.py:308

commit v5 on v4

--- a/solution.py
+++ b/solution.py
@@ -155,7 +155,7 @@
     )
 
 
-def prepare_kernel(k_ref, v_ref, ks_ref, vs_ref, docs_ref, row_ref):
+def prepare_kernel(k_ref, v_ref, ks_ref, vs_ref, docs_ref, row_ref, first_ref):
     tokens = k_ref.shape[0]
     k = (k_ref[...].astype(F32) + ks_ref[...]).astype(BF)
     v = (v_ref[...].astype(F32) + vs_ref[...]).astype(BF)
@@ -167,18 +167,24 @@
         row_ref[0:tokens, at + HEAD : at + 2 * HEAD] = v[:, h * HEAD : (h + 1) * HEAD]
         row_ref[tokens:, at : at + tokens] = docs
         row_ref[tokens:, at + HEAD : at + HEAD + tokens] = docs
+    first_ref[...] = row_ref[:, 0 : 2 * HEAD]
 
 
 def prepare(k, v, ks, vs, docs):
     tokens, width = k.shape
+    hbm = [pltpu.with_memory_space_constraint(x, pltpu.HBM) for x in (k, v, ks, vs, docs)]
     return pl.pallas_call(
         prepare_kernel,
-        out_shape=jax.ShapeDtypeStruct((tokens + TAIL, 2 * width), BF),
+        out_shape=[
+            jax.ShapeDtypeStruct((tokens + TAIL, 2 * width), BF),
+            jax.ShapeDtypeStruct((tokens + TAIL, 2 * HEAD), BF),
+        ],
+        compiler_params=pltpu.CompilerParams(vmem_limit_bytes=4 << 20),
         cost_estimate=pl.CostEstimate(flops=1 << 17, bytes_accessed=1 << 19, transcendentals=0),
-    )(k, v, ks, vs, docs)
-
-
-def spread_kernel(x_ref, row_ref, near_ref, far_ref, out_ref):
+    )(*hbm)
+
+
+def spread_kernel(x_ref, row_ref, one_ref, two_ref, three_ref, four_ref, out_ref):
     rows = row_ref.shape[0]
     for i in range(out_ref.shape[0]):
         @pl.when(i > x_ref[0])
@@ -187,29 +193,33 @@
 
         @pl.when(i <= x_ref[0])
         def _():
-            out_ref[i, 0:rows, :] = far_ref[rows:, :]
-
-        out_ref[i, rows : 3 * rows, :] = near_ref[...]
-        out_ref[i, 3 * rows :, :] = far_ref[0:rows, :]
-
-
-def spread(where_x, row, near, far, head, n):
-    rows, width = near.shape
-    whole = pl.BlockSpec(memory_space=pltpu.VMEM)
+            out_ref[i, 0:rows, :] = four_ref[...]
+
+        out_ref[i, rows : 2 * rows, :] = one_ref[...]
+        out_ref[i, 2 * rows : 3 * rows, :] = two_ref[...]
+        out_ref[i, 3 * rows :, :] = three_ref[...]
+
+
+def spread(where_x, row, one, two, three, four, head, n):
+    rows, width = row.shape[0], 2 * HEAD
+    at_head = pl.BlockSpec((rows, width), lambda g: (0, head))
+    below = 0 if four.shape[0] == rows else 1
     return pl.pallas_call(
         spread_kernel,
         grid=(1,),
         in_specs=[
             pl.BlockSpec(memory_space=pltpu.SMEM),
-            pl.BlockSpec((rows // 2, width), lambda g: (0, head)),
-            whole,
-            whole,
-        ],
-        out_specs=whole,
-        out_shape=jax.ShapeDtypeStruct((n, 2 * rows, width), BF),
+            at_head,
+            at_head,
+            at_head,
+            pl.BlockSpec((rows, width), lambda g: (0, 0)),
+            pl.BlockSpec((rows, width), lambda g: (below, 0)),
+        ],
+        out_specs=pl.BlockSpec(memory_space=pltpu.VMEM),
+        out_shape=jax.ShapeDtypeStruct((n, ROWS * rows, width), BF),
         compiler_params=pltpu.CompilerParams(vmem_limit_bytes=8 << 20),
         cost_estimate=pl.CostEstimate(flops=0, bytes_accessed=2 << 20, transcendentals=0),
-    )(where_x, row, near, far)
+    )(where_x, row, one, two, three, four)
 
 
 def fold_kernel(x_ref, back_ref, gown_ref, sent_ref, kept_ref):
@@ -314,14 +324,16 @@
     where_x = lax.axis_index("cx")
     n_x = lax.axis_size("cx")
     at_x = where_x.astype(jnp.int32)[None]
-    row = prepare(key[0], value[0], key_shift[0], value_shift[0], doc_ids)
+    row, row_first = prepare(key[0], value[0], key_shift[0], value_shift[0], doc_ids)
     one, two = along_z(row, 1), along_z(row, 2)
     wins = []
     for h in range(kv_local):
-        part = slice(2 * h * HEAD, 2 * (h + 1) * HEAD)
-        near = jnp.concatenate([one[:, part], two[:, part]], 0)
-        far = along_z(near, 2)
-        wins.append(swap_x(spread(at_x, row, near, far, h, n_x)))
+        if h == 0:
+            three, four = along_z(row_first, 3), along_z(row_first, 4)
+        else:
+            part = slice(2 * h * HEAD, 2 * (h + 1) * HEAD)
+            three = four = along_z(jnp.concatenate([one[:, part], two[:, part]], 0), 2)
+        wins.append(swap_x(spread(at_x, row, one, two, three, four, h, n_x)))
     attn = query[0]
     kept = []
     for h in range(kv_local):

time: 165 us -> 163 us (0.988)
  starting transfers between devices: 62.6 us -> 59.2 us
  blocking collectives: 25 us -> 27.4 us
    all_to_all x4, waiting for transfers between devices: 15.1 us -> 17.7 us  [swap_x(): return lax.all_to_all(x, 'cx', 0, 0)]
    all_to_all x1, blocking collectives: 25 us -> 27.4 us  [per_device(): everything = lax.all_to_all(square, 'cz', 0, 0)]
    ppermute x8 -> x9, waiting for transfers between devices: 27.6 us -> 25.3 us  [along_z(): lax.ppermute(x, 'cz', [(i - d, i) for i in range(n) if 0 <= i - d < n])]
    ppermute x8 -> x9, starting transfers between devices: 33.2 us -> 32.2 us  [along_z(): lax.ppermute(x, 'cz', [(i - d, i) for i in range(n) if 0 <= i - d < n])]
  transfers between devices with their start and end apart: 13 -> 14, of which waited for: 11 -> 10; matrix products, arithmetic and copies ran while one was open for 0% -> 0% of each run, Pallas kernels for 12% -> 12%
where the time goes in v5:
time: 163 us; the launch traced here: 162 us
  starting transfers between devices  59.2 us (36%)
  waiting for transfers between devices  50.1 us (31%)
  blocking collectives  27.4 us (17%)
  Pallas kernels  23 us (14%)
    ppermute x9, starting transfers between devices, along_z(): lax.ppermute(x, 'cz', [(i - d, i) for i in range(n) if 0 <= i - d < n])  32.2 us
    all_to_all x1, blocking collectives, per_device(): everything = lax.all_to_all(square, 'cz', 0, 0)  27.4 us
    ppermute x9, waiting for transfers between devices, along_z(): lax.ppermute(x, 'cz', [(i - d, i) for i in range(n) if 0 <= i - d < n])  25.3 us
    pallas_call x2, Pallas kernels, attention(): pl.pallas_call(attn_kernel, grid=(1,), in_specs=[wide, wide, whole, pl.Bl...  18.3 us
    all_to_all x4, waiting for transfers between devices, swap_x(): return lax.all_to_all(x, 'cx', 0, 0)  17.7 us
    all_to_all x4, starting transfers between devices, swap_x(): return lax.all_to_all(x, 'cx', 0, 0)  14.8 us
    all_to_all x1, starting transfers between devices, sum_among(): return lax.all_to_all(jnp.broadcast_to(x[None], (n,) + x.shape), axes, 0, 0)  12.2 us
    all_to_all x1, waiting for transfers between devices, sum_among(): return lax.all_to_all(jnp.broadcast_to(x[None], (n,) + x.shape), axes, 0, 0)  7.13 us
  transfers between devices with their start and end apart: 14, of which 10 were waited for; matrix products, arithmetic and copies ran while one was open for 0% of the time, Pallas kernels for 12%

profile of v5, /device:TPU:1, one launch (start us, length us, event | category | flops | bytes accessed | tf_op | source)
XLA Modules:
  0.0 161.8 jit_solution(11767477967693412787)
XLA Ops:
  0.6 1.1 shard_map.94
  1.7 4.4 %collective-permute-start = (bf16[136,512]{1,0:T(8,128)(2,1)S(1)}, bf16[136,512]{1,0:T(8,128)(2,1)S(1)}, u32[]{:S(2)}, u32[]{:S(2)}) collective-permute-start(bf16[136,512]{1,0:T(8,128)(2,1)S(1)} %get-tuple-element.19.row_ref.own_ref), channel_id=1, source_target_pairs={{0,16},{16,32},{32,48},{48,64},{64,80},{80,96},{96,112},{112,128},... | collective-permute-start | bytes 417800 | tf_op jit(solution)/shard_map/ppermute | solution.py:309
  6.1 4.9 %collective-permute-start.1 = (bf16[136,512]{1,0:T(8,128)(2,1)S(1)}, bf16[136,512]{1,0:T(8,128)(2,1)S(1)}, u32[]{:S(2)}, u32[]{:S(2)}) collective-permute-start(bf16[136,512]{1,0:T(8,128)(2,1)S(1)} %get-tuple-element.19.row_ref.own_ref), channel_id=1, source_target_pairs={{0,32},{16,48},{32,64},{48,80},{64,96},{80,112},{96,128},{112,144}... | collective-permute-start | bytes 417800 | tf_op jit(solution)/shard_map/ppermute | solution.py:309
  11.0 7.5 %collective-permute-start.3 = (bf16[136,256]{1,0:T(8,128)(2,1)S(1)}, bf16[136,256]{1,0:T(8,128)(2,1)S(1)}, u32[]{:S(2)}, u32[]{:S(2)}) collective-permute-start(bf16[136,256]{1,0:T(8,128)(2,1)S(1)} %get-tuple-element.20), channel_id=1, source_target_pairs={{0,48},{16,64},{32,80},{48,96},{64,112},{80,128},{96,144},{112,160... | collective-permute-start | bytes 208904 | tf_op jit(solution)/shard_map/ppermute | solution.py:309
  18.5 7.0 %collective-permute-start.4 = (bf16[136,256]{1,0:T(8,128)(2,1)S(1)}, bf16[136,256]{1,0:T(8,128)(2,1)S(1)}, u32[]{:S(2)}, u32[]{:S(2)}) collective-permute-start(bf16[136,256]{1,0:T(8,128)(2,1)S(1)} %get-tuple-element.20), channel_id=1, source_target_pairs={{0,64},{16,80},{32,96},{48,112},{64,128},{80,144},{96,160},{112,17... | collective-permute-start | bytes 208904 | tf_op jit(solution)/shard_map/ppermute | solution.py:309
  25.5 0.0 collective-permute-done.3.three_ref
  25.5 1.3 collective-permute-done.4.four_ref
  26.9 0.0 collective-permute-done.one_ref
  26.9 0.0 collective-permute-done.1.two_ref
  26.9 1.1 shard_map.96
  28.0 4.0 %all-to-all-start.1 = ((bf16[4,544,256]{2,1,0:T(8,128)(2,1)}), bf16[4,544,256]{2,1,0:T(8,128)(2,1)S(1)}, u32[]{:S(2)}, u32[]{:S(2)}) async-start(bf16[4,544,256]{2,1,0:T(8,128)(2,1)} %shard_map.96), calls=%async_computation.1 | async-start | bytes 2228224 | tf_op jit(solution)/shard_map/all_to_all | solution.py:313
  32.0 3.1 %collective-permute-start.2 = (bf16[272,256]{1,0:T(8,128)(2,1)S(1)}, bf16[272,256]{1,0:T(8,128)(2,1)S(1)}, u32[]{:S(2)}, u32[]{:S(2)}) collective-permute-start(bf16[272,256]{1,0:T(8,128)(2,1)S(1)} %pad_maximum_fusion), channel_id=1, source_target_pairs={{0,32},{16,48},{32,64},{48,80},{64,96},{80,112},{96,128},{112,144}... | collective-permute-start | bytes 417800 | tf_op jit(solution)/shard_map/ppermute | solution.py:309
  35.1 2.0 %collective-permute-done.2.three_ref.four_ref = bf16[272,256]{1,0:T(8,128)(2,1)S(1)} collective-permute-done((bf16[272,256]{1,0:T(8,128)(2,1)S(1)}, bf16[272,256]{1,0:T(8,128)(2,1)S(1)}, u32[]{:S(2)}, u32[]{:S(2)}) %collective-permute-start.2) | collective-permute-done | bytes 139296 | tf_op jit(solution)/shard_map/ppermute | solution.py:309
  37.1 1.1 shard_map.95
  38.3 6.6 %all-to-all-done.1.win_ref = bf16[4,544,256]{2,1,0:T(8,128)(2,1)S(1)} async-done(((bf16[4,544,256]{2,1,0:T(8,128)(2,1)}), bf16[4,544,256]{2,1,0:T(8,128)(2,1)S(1)}, u32[]{:S(2)}, u32[]{:S(2)}) %all-to-all-start.1) | async-done | bytes 1114144 | tf_op jit(solution)/shard_map/all_to_all | solution.py:313
  44.9 3.5 %all-to-all-start = ((bf16[4,544,256]{2,1,0:T(8,128)(2,1)}), bf16[4,544,256]{2,1,0:T(8,128)(2,1)S(1)}, u32[]{:S(2)}, u32[]{:S(2)}) async-start(bf16[4,544,256]{2,1,0:T(8,128)(2,1)} %shard_map.95), calls=%async_computation | async-start | bytes 2228224 | tf_op jit(solution)/shard_map/all_to_all | solution.py:313
  48.4 9.2 %shard_map.97 = (bf16[128,2048]{1,0:T(8,128)(2,1)}, bf16[4,512,256]{2,1,0:T(8,128)(2,1)}, f32[128,256]{1,0:T(8,128)S(1)}) custom-call(bf16[128,2048]{1,0:T(8,128)(2,1)} %bitcast.27, bf16[128,2048]{1,0:T(8,128)(2,1)} %bitcast.30, bf16[4,544,256]{2,1,0:T(8,128)(2,1)S(1)} %all-to-all-done.1.win_ref, bf16[136,512]{1,0:T(8,128)(2,1)S(1)} %get-tuple-element.19.row_ref.own_ref, ...), custom_call_target="tpu_custom_call" | custom-call | flops 2852126720 | bytes 4194304 | tf_op jit(solution)/shard_map/pallas_call | solution.py:117
  57.6 2.5 %all-to-all-done.win_ref = bf16[4,544,256]{2,1,0:T(8,128)(2,1)S(1)} async-done(((bf16[4,544,256]{2,1,0:T(8,128)(2,1)}), bf16[4,544,256]{2,1,0:T(8,128)(2,1)S(1)}, u32[]{:S(2)}, u32[]{:S(2)}) %all-to-all-start) | async-done | bytes 1114144 | tf_op jit(solution)/shard_map/all_to_all | solution.py:313
  60.0 3.7 %all-to-all-start.2 = ((bf16[4,512,256]{2,1,0:T(8,128)(2,1)}), bf16[4,512,256]{2,1,0:T(8,128)(2,1)S(1)}, u32[]{:S(2)}, u32[]{:S(2)}) async-start(bf16[4,512,256]{2,1,0:T(8,128)(2,1)} %get-tuple-element.23), calls=%async_computation.2 | async-start | bytes 2097152 | tf_op jit(solution)/shard_map/all_to_all | solution.py:313
  63.7 9.1 %shard_map.98 = (bf16[128,2048]{1,0:T(8,128)(2,1)}, bf16[4,512,256]{2,1,0:T(8,128)(2,1)}, f32[128,256]{1,0:T(8,128)S(1)}) custom-call(bf16[128,2048]{1,0:T(8,128)(2,1)} %bitcast.29, bf16[128,2048]{1,0:T(8,128)(2,1)} %bitcast.31, bf16[4,544,256]{2,1,0:T(8,128)(2,1)S(1)} %all-to-all-done.win_ref, ...), custom_call_target="tpu_custom_call", output_to_operand_aliasing={{0}: (4, {})} | custom-call | flops 2852126720 | bytes 4194304 | tf_op jit(solution)/shard_map/pallas_call | solution.py:117
  72.9 0.4 all-to-all-done.2.back_ref
  73.3 3.6 %all-to-all-start.3 = ((bf16[4,512,256]{2,1,0:T(8,128)(2,1)}), bf16[4,512,256]{2,1,0:T(8,128)(2,1)S(1)}, u32[]{:S(2)}, u32[]{:S(2)}) async-start(bf16[4,512,256]{2,1,0:T(8,128)(2,1)} %get-tuple-element.26), calls=%async_computation.3 | async-start | bytes 2097152 | tf_op jit(solution)/shard_map/all_to_all | solution.py:313
  76.9 0.2 shard_map.99
  77.1 1.3 collective-permute-start.5
  78.4 8.2 %all-to-all-done.3.back_ref = bf16[4,512,256]{2,1,0:T(8,128)(2,1)S(1)} async-done(((bf16[4,512,256]{2,1,0:T(8,128)(2,1)}), bf16[4,512,256]{2,1,0:T(8,128)(2,1)S(1)}, u32[]{:S(2)}, u32[]{:S(2)}) %all-to-all-start.3) | async-done | bytes 1048608 | tf_op jit(solution)/shard_map/all_to_all | solution.py:313
  86.7 0.2 shard_map.100
  86.9 1.3 collective-permute-start.6
  88.2 0.0 collective-permute-done.5
  88.2 6.7 %collective-permute-done.6 = bf16[256,256]{1,0:T(8,128)(2,1)S(1)} collective-permute-done((bf16[256,256]{1,0:T(8,128)(2,1)S(1)}, bf16[256,256]{1,0:T(8,128)(2,1)S(1)}, u32[]{:S(2)}, u32[]{:S(2)}) %collective-permute-start.6) | collective-permute-done | bytes 131104 | tf_op jit(solution)/shard_map/ppermute | solution.py:309
  94.9 0.0 copy-start
  94.9 0.0 copy-start.1
  95.0 1.4 collective-permute-start.7
  96.4 1.3 collective-permute-start.8
  97.7 11.4 %collective-permute-done.7 = bf16[128,512]{1,0:T(8,128)(2,1)S(1)} collective-permute-done((bf16[128,512]{1,0:T(8,128)(2,1)S(1)}, bf16[128,512]{1,0:T(8,128)(2,1)S(1)}, u32[]{:S(2)}, u32[]{:S(2)}) %collective-permute-start.7) | collective-permute-done | bytes 131104 | tf_op jit(solution)/shard_map/ppermute | solution.py:309
  109.1 3.9 %collective-permute-done.8 = bf16[128,512]{1,0:T(8,128)(2,1)S(1)} collective-permute-done((bf16[128,512]{1,0:T(8,128)(2,1)S(1)}, bf16[128,512]{1,0:T(8,128)(2,1)S(1)}, u32[]{:S(2)}, u32[]{:S(2)}) %collective-permute-start.8) | collective-permute-done | bytes 131104 | tf_op jit(solution)/shard_map/ppermute | solution.py:309
  113.0 0.0 copy-done
  113.0 0.0 copy-done.1
  113.1 0.2 multiply_reduce_fusion.4
  113.3 0.6 broadcast_in_dim.24
  113.9 12.2 %all-to-all-start.4 = ((f32[32,3,128]{2,1,0:T(4,128)}), f32[32,3,128]{2,1,0:T(4,128)S(1)}, u32[]{:S(2)}, u32[]{:S(2)}) async-start(f32[32,3,128]{2,1,0:T(4,128)} %broadcast_in_dim.24), calls=%async_computation.4 | async-start | bytes 131072 | tf_op jit(solution)/shard_map/all_to_all | solution.py:318
  126.2 7.1 %all-to-all-done.4.plane_ref = f32[32,3,128]{2,1,0:T(4,128)S(1)} async-done(((f32[32,3,128]{2,1,0:T(4,128)}), f32[32,3,128]{2,1,0:T(4,128)S(1)}, u32[]{:S(2)}, u32[]{:S(2)}) %all-to-all-start.4) | async-done | bytes 49184 | tf_op jit(solution)/shard_map/all_to_all | solution.py:318
  133.3 0.1 shard_map.101
  133.5 27.4 %all_to_all.30.all_ref = f32[16,1,128]{2,1,0:T(1,128)S(1)} all-to-all(f32[16,1,128]{2,1,0:T(1,128)S(1)} %get-tuple-element.31), channel_id=1, replica_groups=mesh['dp'=2,'cz'=16,'cx'=4,'tp'=4] {'cz'}, dimensions={0} | all-to-all | bytes 16384 | tf_op jit(solution)/shard_map/all_to_all | solution.py:373
  160.9 0.9 shard_map.102
  (13 shorter events, 0.2 us)
Async XLA Ops:
  1.7 25.1 %collective-permute-start = (bf16[136,512]{1,0:T(8,128)(2,1)S(1)}, bf16[136,512]{1,0:T(8,128)(2,1)S(1)}, u32[]{:S(2)}, u32[]{:S(2)}) collective-permute-start(bf16[136,512]{1,0:T(8,128)(2,1)S(1)} %get-tuple-element.19.row_ref.own_ref), channel_id=1, source_target_pairs={{0,16},{16,32},{32,48},{48,64},{64,80},{80,96},{96,112},{112,128},... | collective-permute-start | bytes 417800 | tf_op jit(solution)/shard_map/ppermute | solution.py:309
  6.1 20.8 %collective-permute-start.1 = (bf16[136,512]{1,0:T(8,128)(2,1)S(1)}, bf16[136,512]{1,0:T(8,128)(2,1)S(1)}, u32[]{:S(2)}, u32[]{:S(2)}) collective-permute-start(bf16[136,512]{1,0:T(8,128)(2,1)S(1)} %get-tuple-element.19.row_ref.own_ref), channel_id=1, source_target_pairs={{0,32},{16,48},{32,64},{48,80},{64,96},{80,112},{96,128},{112,144}... | collective-permute-start | bytes 417800 | tf_op jit(solution)/shard_map/ppermute | solution.py:309
  11.0 14.5 %collective-permute-start.3 = (bf16[136,256]{1,0:T(8,128)(2,1)S(1)}, bf16[136,256]{1,0:T(8,128)(2,1)S(1)}, u32[]{:S(2)}, u32[]{:S(2)}) collective-permute-start(bf16[136,256]{1,0:T(8,128)(2,1)S(1)} %get-tuple-element.20), channel_id=1, source_target_pairs={{0,48},{16,64},{32,80},{48,96},{64,112},{80,128},{96,144},{112,160... | collective-permute-start | bytes 208904 | tf_op jit(solution)/shard_map/ppermute | solution.py:309
  18.5 8.4 %collective-permute-start.4 = (bf16[136,256]{1,0:T(8,128)(2,1)S(1)}, bf16[136,256]{1,0:T(8,128)(2,1)S(1)}, u32[]{:S(2)}, u32[]{:S(2)}) collective-permute-start(bf16[136,256]{1,0:T(8,128)(2,1)S(1)} %get-tuple-element.20), channel_id=1, source_target_pairs={{0,64},{16,80},{32,96},{48,112},{64,128},{80,144},{96,160},{112,17... | collective-permute-start | bytes 208904 | tf_op jit(solution)/shard_map/ppermute | solution.py:309
  28.0 16.9 %all-to-all-start.1 = ((bf16[4,544,256]{2,1,0:T(8,128)(2,1)}), bf16[4,544,256]{2,1,0:T(8,128)(2,1)S(1)}, u32[]{:S(2)}, u32[]{:S(2)}) async-start(bf16[4,544,256]{2,1,0:T(8,128)(2,1)} %shard_map.96), calls=%async_computation.1 | async-start | bytes 2228224 | tf_op jit(solution)/shard_map/all_to_all | solution.py:313
  32.0 5.1 %collective-permute-start.2 = (bf16[272,256]{1,0:T(8,128)(2,1)S(1)}, bf16[272,256]{1,0:T(8,128)(2,1)S(1)}, u32[]{:S(2)}, u32[]{:S(2)}) collective-permute-start(bf16[272,256]{1,0:T(8,128)(2,1)S(1)} %pad_maximum_fusion), channel_id=1, source_target_pairs={{0,32},{16,48},{32,64},{48,80},{64,96},{80,112},{96,128},{112,144}... | collective-permute-start | bytes 417800 | tf_op jit(solution)/shard_map/ppermute | solution.py:309
  44.9 15.2 %all-to-all-start = ((bf16[4,544,256]{2,1,0:T(8,128)(2,1)}), bf16[4,544,256]{2,1,0:T(8,128)(2,1)S(1)}, u32[]{:S(2)}, u32[]{:S(2)}) async-start(bf16[4,544,256]{2,1,0:T(8,128)(2,1)} %shard_map.95), calls=%async_computation | async-start | bytes 2228224 | tf_op jit(solution)/shard_map/all_to_all | solution.py:313
  60.0 13.3 %all-to-all-start.2 = ((bf16[4,512,256]{2,1,0:T(8,128)(2,1)}), bf16[4,512,256]{2,1,0:T(8,128)(2,1)S(1)}, u32[]{:S(2)}, u32[]{:S(2)}) async-start(bf16[4,512,256]{2,1,0:T(8,128)(2,1)} %get-tuple-element.23), calls=%async_computation.2 | async-start | bytes 2097152 | tf_op jit(solution)/shard_map/all_to_all | solution.py:313
  73.3 13.4 %all-to-all-start.3 = ((bf16[4,512,256]{2,1,0:T(8,128)(2,1)}), bf16[4,512,256]{2,1,0:T(8,128)(2,1)S(1)}, u32[]{:S(2)}, u32[]{:S(2)}) async-start(bf16[4,512,256]{2,1,0:T(8,128)(2,1)} %get-tuple-element.26), calls=%async_computation.3 | async-start | bytes 2097152 | tf_op jit(solution)/shard_map/all_to_all | solution.py:313
  77.1 11.0 %collective-permute-start.5 = (bf16[256,256]{1,0:T(8,128)(2,1)S(1)}, bf16[256,256]{1,0:T(8,128)(2,1)S(1)}, u32[]{:S(2)}, u32[]{:S(2)}) collective-permute-start(bf16[256,256]{1,0:T(8,128)(2,1)S(1)} %get-tuple-element.29), channel_id=1, source_target_pairs={{32,0},{48,16},{64,32},{80,48},{96,64},{112,80},{128,96},{144,112}... | collective-permute-start | bytes 393224 | tf_op jit(solution)/shard_map/ppermute | solution.py:309
  86.9 8.0 %collective-permute-start.6 = (bf16[256,256]{1,0:T(8,128)(2,1)S(1)}, bf16[256,256]{1,0:T(8,128)(2,1)S(1)}, u32[]{:S(2)}, u32[]{:S(2)}) collective-permute-start(bf16[256,256]{1,0:T(8,128)(2,1)S(1)} %get-tuple-element.30), channel_id=1, source_target_pairs={{32,0},{48,16},{64,32},{80,48},{96,64},{112,80},{128,96},{144,112}... | collective-permute-start | bytes 393224 | tf_op jit(solution)/shard_map/ppermute | solution.py:309
  94.9 18.1 %copy-start = (f32[1,128,256]{2,1,0:T(8,128)S(1)}, f32[1,128,256]{2,1,0:T(8,128)}, u32[]{:S(2)}) copy-start(f32[1,128,256]{2,1,0:T(8,128)} %param.10) | copy-start | bytes 393220
  94.9 18.1 %copy-start.1 = (f32[1,128,256]{2,1,0:T(8,128)S(1)}, f32[1,128,256]{2,1,0:T(8,128)}, u32[]{:S(2)}) copy-start(f32[1,128,256]{2,1,0:T(8,128)} %param.11) | copy-start | bytes 393220
  95.0 14.1 %collective-permute-start.7 = (bf16[128,512]{1,0:T(8,128)(2,1)S(1)}, bf16[128,512]{1,0:T(8,128)(2,1)S(1)}, u32[]{:S(2)}, u32[]{:S(2)}) collective-permute-start(bf16[128,512]{1,0:T(8,128)(2,1)S(1)} %pad_maximum_fusion.1), channel_id=1, source_target_pairs={{16,0},{32,16},{48,32},{64,48},{80,64},{96,80},{112,96},{128,112},... | collective-permute-start | bytes 393224 | tf_op jit(solution)/shard_map/ppermute | solution.py:309
  96.4 16.6 %collective-permute-start.8 = (bf16[128,512]{1,0:T(8,128)(2,1)S(1)}, bf16[128,512]{1,0:T(8,128)(2,1)S(1)}, u32[]{:S(2)}, u32[]{:S(2)}) collective-permute-start(bf16[128,512]{1,0:T(8,128)(2,1)S(1)} %pad_maximum_fusion.2), channel_id=1, source_target_pairs={{32,0},{48,16},{64,32},{80,48},{96,64},{112,80},{128,96},{144,112}... | collective-permute-start | bytes 393224 | tf_op jit(solution)/shard_map/ppermute | solution.py:309
  113.9 19.4 %all-to-all-start.4 = ((f32[32,3,128]{2,1,0:T(4,128)}), f32[32,3,128]{2,1,0:T(4,128)S(1)}, u32[]{:S(2)}, u32[]{:S(2)}) async-start(f32[32,3,128]{2,1,0:T(4,128)} %broadcast_in_dim.24), calls=%async_computation.4 | async-start | bytes 131072 | tf_op jit(solution)/shard_map/all_to_all | solution.py:318

commit v6 on v5

--- a/solution.py
+++ b/solution.py
@@ -222,7 +222,7 @@
     )(where_x, row, one, two, three, four)
 
 
-def fold_kernel(x_ref, back_ref, gown_ref, sent_ref, kept_ref):
+def fold_kernel(x_ref, back_ref, gown_ref, kept_ref, *sent_refs):
     tokens = gown_ref.shape[0]
     n = back_ref.shape[0]
 
@@ -239,21 +239,19 @@
     kept_ref[0:tokens, :] = own
     for b in (1, 2):
         kept_ref[b * tokens : (b + 1) * tokens, :] = sum(part(i, b) for i in range(n))
-    sent_ref[0:tokens, :] = sum(part(i, 3) for i in range(n)).astype(BF)
-    sent_ref[tokens:, :] = last.astype(BF)
-
-
-def fold(where_x, back, gown):
+    sent_refs[0][0:tokens, :] = sum(part(i, 3) for i in range(n)).astype(BF)
+    sent_refs[-1][(2 - len(sent_refs)) * tokens :, :] = last.astype(BF)
+
+
+def fold(where_x, back, gown, apart):
     tokens, width = gown.shape
     vmem = pl.BlockSpec(memory_space=pltpu.VMEM)
     return pl.pallas_call(
         fold_kernel,
         in_specs=[pl.BlockSpec(memory_space=pltpu.SMEM), vmem, vmem],
-        out_specs=[vmem, vmem],
-        out_shape=[
-            jax.ShapeDtypeStruct((2 * tokens, width), BF),
-            jax.ShapeDtypeStruct((3 * tokens, width), F32),
-        ],
+        out_specs=[vmem] * (3 if apart else 2),
+        out_shape=[jax.ShapeDtypeStruct((3 * tokens, width), F32)]
+        + [jax.ShapeDtypeStruct((tokens if apart else 2 * tokens, width), BF)] * (2 if apart else 1),
         compiler_params=pltpu.CompilerParams(vmem_limit_bytes=8 << 20),
         cost_estimate=pl.CostEstimate(flops=1 << 19, bytes_accessed=2 << 20, transcendentals=0),
     )(where_x, back, gown)
@@ -335,23 +333,26 @@
             three = four = along_z(jnp.concatenate([one[:, part], two[:, part]], 0), 2)
         wins.append(swap_x(spread(at_x, row, one, two, three, four, h, n_x)))
     attn = query[0]
-    kept = []
+    kept, ones, twos, late = [], [], [], []
     for h in range(kv_local):
         attn, gwin, gown = attention(query[0], target[0], wins[h], row, attn, h)
-        sent, mine = fold(at_x, swap_x(gwin), gown)
-        kept.append((along_z(sent, -2), mine))
-    near = [
-        jnp.concatenate(
-            [
-                (mine[(b + 1) * tokens : (b + 2) * tokens] + far[b * tokens : (b + 1) * tokens]).astype(BF)
-                for far, mine in kept
-            ],
-            1,
-        )
-        for b in range(2)
-    ]
-    two, one = along_z(near[1], -2), along_z(near[0], -1)
-    grad = jnp.concatenate([mine[:tokens] for _, mine in kept], 1) + one.astype(F32) + two.astype(F32)
+        last = h == kv_local - 1
+        gwin = pltpu.with_memory_space_constraint(gwin, pltpu.HBM)
+        back = pltpu.with_memory_space_constraint(swap_x(gwin), pltpu.HBM)
+        mine, *sent = fold(at_x, back, gown, last)
+        part1, part2 = mine[tokens : 2 * tokens], mine[2 * tokens :]
+        if last:
+            late = [along_z(sent[0], -3), along_z(sent[1], -4)]
+        else:
+            far = along_z(sent[0], -2).astype(F32)
+            part1, part2 = part1 + far[:tokens], part2 + far[tokens:]
+        kept.append(mine[:tokens])
+        ones.append(part1.astype(BF))
+        twos.append(part2.astype(BF))
+    two = along_z(jnp.concatenate(twos, 1), -2).astype(F32)
+    one = along_z(jnp.concatenate(ones, 1), -1).astype(F32)
+    kept[-1] = kept[-1] + sum(x.astype(F32) for x in late)
+    grad = jnp.concatenate(kept, 1) + one + two
     grad_key = jnp.concatenate(
         [grad[:, 2 * h * HEAD : (2 * h + 1) * HEAD] for h in range(kv_local)], 1
     )

time: 163 us -> 167 us (1.025)
  starting transfers between devices: 59.2 us -> 64.1 us
  waiting for transfers between devices: 50.1 us -> 46.1 us
  Pallas kernels: 23 us -> 25.4 us
    all_to_all x4, waiting for transfers between devices: 17.7 us -> 11.2 us  [swap_x(): return lax.all_to_all(x, 'cx', 0, 0)]
    all_to_all x1, starting transfers between devices: 12.2 us -> 15.9 us  [sum_among(): return lax.all_to_all(jnp.broadcast_to(x[None], (n,) + x.shape), axes, 0, 0)]
    ppermute x9 -> x10, waiting for transfers between devices: 25.3 us -> 27.8 us  [along_z(): lax.ppermute(x, 'cz', [(i - d, i) for i in range(n) if 0 <= i - d < n])]
    pallas_call x2, Pallas kernels: 0.39 us -> 2.85 us  [fold(): pl.pallas_call(fold_kernel, in_specs=[pl.BlockSpec(memory_space=pltpu.SME...]
    ppermute x9 -> x10, starting transfers between devices: 32.2 us -> 33.5 us  [along_z(): lax.ppermute(x, 'cz', [(i - d, i) for i in range(n) if 0 <= i - d < n])]
  transfers between devices with their start and end apart: 14 -> 15, of which waited for: 10 -> 10; matrix products, arithmetic and copies ran while one was open for 0% -> 0% of each run, Pallas kernels for 12% -> 13%
where the time goes in v6:
time: 167 us; the launch traced here: 166 us
  starting transfers between devices  64.1 us (38%)
  waiting for transfers between devices  46.1 us (28%)
  blocking collectives  27.2 us (16%)
  Pallas kernels  25.4 us (15%)
  local copies, waits for them, and re-layouts  1.68 us (1%)
    ppermute x10, starting transfers between devices, along_z(): lax.ppermute(x, 'cz', [(i - d, i) for i in range(n) if 0 <= i - d < n])  33.5 us
    ppermute x10, waiting for transfers between devices, along_z(): lax.ppermute(x, 'cz', [(i - d, i) for i in range(n) if 0 <= i - d < n])  27.8 us
    all_to_all x1, blocking collectives, per_device(): everything = lax.all_to_all(square, 'cz', 0, 0)  27.2 us
    pallas_call x2, Pallas kernels, attention(): pl.pallas_call(attn_kernel, grid=(1,), in_specs=[wide, wide, whole, pl.Bl...  18.3 us
    all_to_all x1, starting transfers between devices, sum_among(): return lax.all_to_all(jnp.broadcast_to(x[None], (n,) + x.shape), axes, 0, 0)  15.9 us
    all_to_all x4, starting transfers between devices, swap_x(): return lax.all_to_all(x, 'cx', 0, 0)  14.8 us
    all_to_all x4, waiting for transfers between devices, swap_x(): return lax.all_to_all(x, 'cx', 0, 0)  11.2 us
    all_to_all x1, waiting for transfers between devices, sum_among(): return lax.all_to_all(jnp.broadcast_to(x[None], (n,) + x.shape), axes, 0, 0)  7.13 us
  transfers between devices with their start and end apart: 15, of which 10 were waited for; matrix products, arithmetic and copies ran while one was open for 0% of the time, Pallas kernels for 13%

profile of v6, /device:TPU:1, one launch (start us, length us, event | category | flops | bytes accessed | tf_op | source)
XLA Modules:
  0.0 165.9 jit_solution(2843507048025952301)
XLA Ops:
  0.6 1.1 shard_map.94
  1.7 4.4 %collective-permute-start = (bf16[136,512]{1,0:T(8,128)(2,1)S(1)}, bf16[136,512]{1,0:T(8,128)(2,1)S(1)}, u32[]{:S(2)}, u32[]{:S(2)}) collective-permute-start(bf16[136,512]{1,0:T(8,128)(2,1)S(1)} %get-tuple-element.20.row_ref.own_ref), channel_id=1, source_target_pairs={{0,16},{16,32},{32,48},{48,64},{64,80},{80,96},{96,112},{112,128},... | collective-permute-start | bytes 417800 | tf_op jit(solution)/shard_map/ppermute | solution.py:307
  6.1 4.9 %collective-permute-start.1 = (bf16[136,512]{1,0:T(8,128)(2,1)S(1)}, bf16[136,512]{1,0:T(8,128)(2,1)S(1)}, u32[]{:S(2)}, u32[]{:S(2)}) collective-permute-start(bf16[136,512]{1,0:T(8,128)(2,1)S(1)} %get-tuple-element.20.row_ref.own_ref), channel_id=1, source_target_pairs={{0,32},{16,48},{32,64},{48,80},{64,96},{80,112},{96,128},{112,144}... | collective-permute-start | bytes 417800 | tf_op jit(solution)/shard_map/ppermute | solution.py:307
  11.0 7.5 %collective-permute-start.3 = (bf16[136,256]{1,0:T(8,128)(2,1)S(1)}, bf16[136,256]{1,0:T(8,128)(2,1)S(1)}, u32[]{:S(2)}, u32[]{:S(2)}) collective-permute-start(bf16[136,256]{1,0:T(8,128)(2,1)S(1)} %get-tuple-element.21), channel_id=1, source_target_pairs={{0,48},{16,64},{32,80},{48,96},{64,112},{80,128},{96,144},{112,160... | collective-permute-start | bytes 208904 | tf_op jit(solution)/shard_map/ppermute | solution.py:307
  18.5 7.0 %collective-permute-start.4 = (bf16[136,256]{1,0:T(8,128)(2,1)S(1)}, bf16[136,256]{1,0:T(8,128)(2,1)S(1)}, u32[]{:S(2)}, u32[]{:S(2)}) collective-permute-start(bf16[136,256]{1,0:T(8,128)(2,1)S(1)} %get-tuple-element.21), channel_id=1, source_target_pairs={{0,64},{16,80},{32,96},{48,112},{64,128},{80,144},{96,160},{112,17... | collective-permute-start | bytes 208904 | tf_op jit(solution)/shard_map/ppermute | solution.py:307
  25.5 0.0 collective-permute-done.3.three_ref
  25.5 1.3 collective-permute-done.4.four_ref
  26.9 0.0 collective-permute-done.one_ref
  26.9 0.0 collective-permute-done.1.two_ref
  26.9 1.1 shard_map.96
  28.0 4.0 %all-to-all-start.1 = ((bf16[4,544,256]{2,1,0:T(8,128)(2,1)}), bf16[4,544,256]{2,1,0:T(8,128)(2,1)S(1)}, u32[]{:S(2)}, u32[]{:S(2)}) async-start(bf16[4,544,256]{2,1,0:T(8,128)(2,1)} %shard_map.96), calls=%async_computation.1 | async-start | bytes 2228224 | tf_op jit(solution)/shard_map/all_to_all | solution.py:311
  32.0 3.1 %collective-permute-start.2 = (bf16[272,256]{1,0:T(8,128)(2,1)S(1)}, bf16[272,256]{1,0:T(8,128)(2,1)S(1)}, u32[]{:S(2)}, u32[]{:S(2)}) collective-permute-start(bf16[272,256]{1,0:T(8,128)(2,1)S(1)} %pad_maximum_fusion), channel_id=1, source_target_pairs={{0,32},{16,48},{32,64},{48,80},{64,96},{80,112},{96,128},{112,144}... | collective-permute-start | bytes 417800 | tf_op jit(solution)/shard_map/ppermute | solution.py:307
  35.1 2.0 %collective-permute-done.2.three_ref.four_ref = bf16[272,256]{1,0:T(8,128)(2,1)S(1)} collective-permute-done((bf16[272,256]{1,0:T(8,128)(2,1)S(1)}, bf16[272,256]{1,0:T(8,128)(2,1)S(1)}, u32[]{:S(2)}, u32[]{:S(2)}) %collective-permute-start.2) | collective-permute-done | bytes 139296 | tf_op jit(solution)/shard_map/ppermute | solution.py:307
  37.1 1.1 shard_map.95
  38.3 6.6 %all-to-all-done.1.win_ref = bf16[4,544,256]{2,1,0:T(8,128)(2,1)S(1)} async-done(((bf16[4,544,256]{2,1,0:T(8,128)(2,1)}), bf16[4,544,256]{2,1,0:T(8,128)(2,1)S(1)}, u32[]{:S(2)}, u32[]{:S(2)}) %all-to-all-start.1) | async-done | bytes 1114144 | tf_op jit(solution)/shard_map/all_to_all | solution.py:311
  44.9 3.5 %all-to-all-start = ((bf16[4,544,256]{2,1,0:T(8,128)(2,1)}), bf16[4,544,256]{2,1,0:T(8,128)(2,1)S(1)}, u32[]{:S(2)}, u32[]{:S(2)}) async-start(bf16[4,544,256]{2,1,0:T(8,128)(2,1)} %shard_map.95), calls=%async_computation | async-start | bytes 2228224 | tf_op jit(solution)/shard_map/all_to_all | solution.py:311
  48.4 9.1 %shard_map.97 = (bf16[128,2048]{1,0:T(8,128)(2,1)}, bf16[4,512,256]{2,1,0:T(8,128)(2,1)}, f32[128,256]{1,0:T(8,128)S(1)}) custom-call(bf16[128,2048]{1,0:T(8,128)(2,1)} %bitcast.27, bf16[128,2048]{1,0:T(8,128)(2,1)} %bitcast.30, bf16[4,544,256]{2,1,0:T(8,128)(2,1)S(1)} %all-to-all-done.1.win_ref, bf16[136,512]{1,0:T(8,128)(2,1)S(1)} %get-tuple-element.20.row_ref.own_ref, ...), custom_call_target="tpu_custom_call" | custom-call | flops 2852126720 | bytes 4194304 | tf_op jit(solution)/shard_map/pallas_call | solution.py:117
  57.5 2.5 %all-to-all-done.win_ref = bf16[4,544,256]{2,1,0:T(8,128)(2,1)S(1)} async-done(((bf16[4,544,256]{2,1,0:T(8,128)(2,1)}), bf16[4,544,256]{2,1,0:T(8,128)(2,1)S(1)}, u32[]{:S(2)}, u32[]{:S(2)}) %all-to-all-start) | async-done | bytes 1114144 | tf_op jit(solution)/shard_map/all_to_all | solution.py:311
  60.0 3.7 %all-to-all-start.2 = ((bf16[4,512,256]{2,1,0:T(8,128)(2,1)}), bf16[4,512,256]{2,1,0:T(8,128)(2,1)S(1)}, u32[]{:S(2)}, u32[]{:S(2)}) async-start(bf16[4,512,256]{2,1,0:T(8,128)(2,1)} %get-tuple-element.24), calls=%async_computation.2 | async-start | bytes 2097152 | tf_op jit(solution)/shard_map/all_to_all | solution.py:311
  63.7 9.1 %shard_map.98 = (bf16[128,2048]{1,0:T(8,128)(2,1)}, bf16[4,512,256]{2,1,0:T(8,128)(2,1)}, f32[128,256]{1,0:T(8,128)S(1)}) custom-call(bf16[128,2048]{1,0:T(8,128)(2,1)} %bitcast.29, bf16[128,2048]{1,0:T(8,128)(2,1)} %bitcast.31, bf16[4,544,256]{2,1,0:T(8,128)(2,1)S(1)} %all-to-all-done.win_ref, ...), custom_call_target="tpu_custom_call", output_to_operand_aliasing={{0}: (4, {})} | custom-call | flops 2852126720 | bytes 4194304 | tf_op jit(solution)/shard_map/pallas_call | solution.py:117
  72.9 0.4 all-to-all-done.2.back_ref
  73.3 0.0 copy-start.3
  73.3 3.6 %all-to-all-start.3 = ((bf16[4,512,256]{2,1,0:T(8,128)(2,1)}), bf16[4,512,256]{2,1,0:T(8,128)(2,1)S(1)}, u32[]{:S(2)}, u32[]{:S(2)}) async-start(bf16[4,512,256]{2,1,0:T(8,128)(2,1)} %get-tuple-element.27), calls=%async_computation.3 | async-start | bytes 2097152 | tf_op jit(solution)/shard_map/all_to_all | solution.py:311
  76.9 0.0 copy-done.3
  76.9 1.4 shard_map.99
  78.3 1.3 collective-permute-start.7
  79.6 5.3 %collective-permute-done.7 = bf16[256,256]{1,0:T(8,128)(2,1)S(1)} collective-permute-done((bf16[256,256]{1,0:T(8,128)(2,1)S(1)}, bf16[256,256]{1,0:T(8,128)(2,1)S(1)}, u32[]{:S(2)}, u32[]{:S(2)}) %collective-permute-start.7) | collective-permute-done | bytes 131104 | tf_op jit(solution)/shard_map/ppermute | solution.py:307
  85.0 1.6 all-to-all-done.3.back_ref
  86.7 0.0 copy-start.2
  86.7 1.0 copy-done.2
  87.6 1.4 shard_map.100
  89.1 0.0 copy-start
  89.1 0.0 copy-start.1
  89.2 1.4 collective-permute-start.8
  90.6 1.3 collective-permute-start.5
  91.9 1.3 collective-permute-start.6
  93.2 1.3 collective-permute-start.9
  94.5 13.7 %collective-permute-done.5 = bf16[128,256]{1,0:T(8,128)(2,1)S(1)} collective-permute-done((bf16[128,256]{1,0:T(8,128)(2,1)S(1)}, bf16[128,256]{1,0:T(8,128)(2,1)S(1)}, u32[]{:S(2)}, u32[]{:S(2)}) %collective-permute-start.5) | collective-permute-done | bytes 65568 | tf_op jit(solution)/shard_map/ppermute | solution.py:307
  108.2 5.5 %collective-permute-done.6 = bf16[128,256]{1,0:T(8,128)(2,1)S(1)} collective-permute-done((bf16[128,256]{1,0:T(8,128)(2,1)S(1)}, bf16[128,256]{1,0:T(8,128)(2,1)S(1)}, u32[]{:S(2)}, u32[]{:S(2)}) %collective-permute-start.6) | collective-permute-done | bytes 65568 | tf_op jit(solution)/shard_map/ppermute | solution.py:307
  113.7 0.0 collective-permute-done.8
  113.7 0.0 collective-permute-done.9
  113.8 0.0 copy-done
  113.8 0.0 copy-done.1
  113.8 0.2 multiply_reduce_fusion.4
  114.1 0.6 broadcast_in_dim.24
  114.7 15.9 %all-to-all-start.4 = ((f32[32,3,128]{2,1,0:T(4,128)}), f32[32,3,128]{2,1,0:T(4,128)S(1)}, u32[]{:S(2)}, u32[]{:S(2)}) async-start(f32[32,3,128]{2,1,0:T(4,128)} %broadcast_in_dim.24), calls=%async_computation.4 | async-start | bytes 131072 | tf_op jit(solution)/shard_map/all_to_all | solution.py:316
  130.6 7.1 %all-to-all-done.4.plane_ref = f32[32,3,128]{2,1,0:T(4,128)S(1)} async-done(((f32[32,3,128]{2,1,0:T(4,128)}), f32[32,3,128]{2,1,0:T(4,128)S(1)}, u32[]{:S(2)}, u32[]{:S(2)}) %all-to-all-start.4) | async-done | bytes 49184 | tf_op jit(solution)/shard_map/all_to_all | solution.py:316
  137.7 0.1 shard_map.101
  137.9 27.2 %all_to_all.30.all_ref = f32[16,1,128]{2,1,0:T(1,128)S(1)} all-to-all(f32[16,1,128]{2,1,0:T(1,128)S(1)} %get-tuple-element.33), channel_id=1, replica_groups=mesh['dp'=2,'cz'=16,'cx'=4,'tp'=4] {'cz'}, dimensions={0} | all-to-all | bytes 16384 | tf_op jit(solution)/shard_map/all_to_all | solution.py:374
  165.0 0.9 shard_map.102
  (16 shorter events, 0.2 us)
Async XLA Ops:
  1.7 25.1 %collective-permute-start = (bf16[136,512]{1,0:T(8,128)(2,1)S(1)}, bf16[136,512]{1,0:T(8,128)(2,1)S(1)}, u32[]{:S(2)}, u32[]{:S(2)}) collective-permute-start(bf16[136,512]{1,0:T(8,128)(2,1)S(1)} %get-tuple-element.20.row_ref.own_ref), channel_id=1, source_target_pairs={{0,16},{16,32},{32,48},{48,64},{64,80},{80,96},{96,112},{112,128},... | collective-permute-start | bytes 417800 | tf_op jit(solution)/shard_map/ppermute | solution.py:307
  6.1 20.8 %collective-permute-start.1 = (bf16[136,512]{1,0:T(8,128)(2,1)S(1)}, bf16[136,512]{1,0:T(8,128)(2,1)S(1)}, u32[]{:S(2)}, u32[]{:S(2)}) collective-permute-start(bf16[136,512]{1,0:T(8,128)(2,1)S(1)} %get-tuple-element.20.row_ref.own_ref), channel_id=1, source_target_pairs={{0,32},{16,48},{32,64},{48,80},{64,96},{80,112},{96,128},{112,144}... | collective-permute-start | bytes 417800 | tf_op jit(solution)/shard_map/ppermute | solution.py:307
  11.0 14.5 %collective-permute-start.3 = (bf16[136,256]{1,0:T(8,128)(2,1)S(1)}, bf16[136,256]{1,0:T(8,128)(2,1)S(1)}, u32[]{:S(2)}, u32[]{:S(2)}) collective-permute-start(bf16[136,256]{1,0:T(8,128)(2,1)S(1)} %get-tuple-element.21), channel_id=1, source_target_pairs={{0,48},{16,64},{32,80},{48,96},{64,112},{80,128},{96,144},{112,160... | collective-permute-start | bytes 208904 | tf_op jit(solution)/shard_map/ppermute | solution.py:307
  18.5 8.4 %collective-permute-start.4 = (bf16[136,256]{1,0:T(8,128)(2,1)S(1)}, bf16[136,256]{1,0:T(8,128)(2,1)S(1)}, u32[]{:S(2)}, u32[]{:S(2)}) collective-permute-start(bf16[136,256]{1,0:T(8,128)(2,1)S(1)} %get-tuple-element.21), channel_id=1, source_target_pairs={{0,64},{16,80},{32,96},{48,112},{64,128},{80,144},{96,160},{112,17... | collective-permute-start | bytes 208904 | tf_op jit(solution)/shard_map/ppermute | solution.py:307
  28.0 16.9 %all-to-all-start.1 = ((bf16[4,544,256]{2,1,0:T(8,128)(2,1)}), bf16[4,544,256]{2,1,0:T(8,128)(2,1)S(1)}, u32[]{:S(2)}, u32[]{:S(2)}) async-start(bf16[4,544,256]{2,1,0:T(8,128)(2,1)} %shard_map.96), calls=%async_computation.1 | async-start | bytes 2228224 | tf_op jit(solution)/shard_map/all_to_all | solution.py:311
  32.0 5.1 %collective-permute-start.2 = (bf16[272,256]{1,0:T(8,128)(2,1)S(1)}, bf16[272,256]{1,0:T(8,128)(2,1)S(1)}, u32[]{:S(2)}, u32[]{:S(2)}) collective-permute-start(bf16[272,256]{1,0:T(8,128)(2,1)S(1)} %pad_maximum_fusion), channel_id=1, source_target_pairs={{0,32},{16,48},{32,64},{48,80},{64,96},{80,112},{96,128},{112,144}... | collective-permute-start | bytes 417800 | tf_op jit(solution)/shard_map/ppermute | solution.py:307
  44.9 15.2 %all-to-all-start = ((bf16[4,544,256]{2,1,0:T(8,128)(2,1)}), bf16[4,544,256]{2,1,0:T(8,128)(2,1)S(1)}, u32[]{:S(2)}, u32[]{:S(2)}) async-start(bf16[4,544,256]{2,1,0:T(8,128)(2,1)} %shard_map.95), calls=%async_computation | async-start | bytes 2228224 | tf_op jit(solution)/shard_map/all_to_all | solution.py:311
  60.0 13.3 %all-to-all-start.2 = ((bf16[4,512,256]{2,1,0:T(8,128)(2,1)}), bf16[4,512,256]{2,1,0:T(8,128)(2,1)S(1)}, u32[]{:S(2)}, u32[]{:S(2)}) async-start(bf16[4,512,256]{2,1,0:T(8,128)(2,1)} %get-tuple-element.24), calls=%async_computation.2 | async-start | bytes 2097152 | tf_op jit(solution)/shard_map/all_to_all | solution.py:311
  73.3 3.6 %copy-start.3 = (bf16[4,512,256]{2,1,0:T(8,128)(2,1)}, bf16[4,512,256]{2,1,0:T(8,128)(2,1)S(1)}, u32[]{:S(2)}) copy-start(bf16[4,512,256]{2,1,0:T(8,128)(2,1)S(1)} %all-to-all-done.2.back_ref) | copy-start | bytes 3145732
  73.3 13.3 %all-to-all-start.3 = ((bf16[4,512,256]{2,1,0:T(8,128)(2,1)}), bf16[4,512,256]{2,1,0:T(8,128)(2,1)S(1)}, u32[]{:S(2)}, u32[]{:S(2)}) async-start(bf16[4,512,256]{2,1,0:T(8,128)(2,1)} %get-tuple-element.27), calls=%async_computation.3 | async-start | bytes 2097152 | tf_op jit(solution)/shard_map/all_to_all | solution.py:311
  78.3 6.6 %collective-permute-start.7 = (bf16[256,256]{1,0:T(8,128)(2,1)S(1)}, bf16[256,256]{1,0:T(8,128)(2,1)S(1)}, u32[]{:S(2)}, u32[]{:S(2)}) collective-permute-start(bf16[256,256]{1,0:T(8,128)(2,1)S(1)} %get-tuple-element.32), channel_id=1, source_target_pairs={{32,0},{48,16},{64,32},{80,48},{96,64},{112,80},{128,96},{144,112}... | collective-permute-start | bytes 393224 | tf_op jit(solution)/shard_map/ppermute | solution.py:307
  86.7 1.0 copy-start.2
  89.1 24.7 %copy-start = (f32[1,128,256]{2,1,0:T(8,128)S(1)}, f32[1,128,256]{2,1,0:T(8,128)}, u32[]{:S(2)}) copy-start(f32[1,128,256]{2,1,0:T(8,128)} %param.10) | copy-start | bytes 393220
  89.1 24.7 %copy-start.1 = (f32[1,128,256]{2,1,0:T(8,128)S(1)}, f32[1,128,256]{2,1,0:T(8,128)}, u32[]{:S(2)}) copy-start(f32[1,128,256]{2,1,0:T(8,128)} %param.11) | copy-start | bytes 393220
  89.2 24.5 %collective-permute-start.8 = (bf16[128,512]{1,0:T(8,128)(2,1)S(1)}, bf16[128,512]{1,0:T(8,128)(2,1)S(1)}, u32[]{:S(2)}, u32[]{:S(2)}) collective-permute-start(bf16[128,512]{1,0:T(8,128)(2,1)S(1)} %pad_maximum_fusion.1), channel_id=1, source_target_pairs={{16,0},{32,16},{48,32},{64,48},{80,64},{96,80},{112,96},{128,112},... | collective-permute-start | bytes 393224 | tf_op jit(solution)/shard_map/ppermute | solution.py:307
  90.6 17.6 %collective-permute-start.5 = (bf16[128,256]{1,0:T(8,128)(2,1)S(1)}, bf16[128,256]{1,0:T(8,128)(2,1)S(1)}, u32[]{:S(2)}, u32[]{:S(2)}) collective-permute-start(bf16[128,256]{1,0:T(8,128)(2,1)S(1)} %get-tuple-element.30), channel_id=1, source_target_pairs={{48,0},{64,16},{80,32},{96,48},{112,64},{128,80},{144,96},{160,112... | collective-permute-start | bytes 196616 | tf_op jit(solution)/shard_map/ppermute | solution.py:307
  91.9 21.8 %collective-permute-start.6 = (bf16[128,256]{1,0:T(8,128)(2,1)S(1)}, bf16[128,256]{1,0:T(8,128)(2,1)S(1)}, u32[]{:S(2)}, u32[]{:S(2)}) collective-permute-start(bf16[128,256]{1,0:T(8,128)(2,1)S(1)} %get-tuple-element.31), channel_id=1, source_target_pairs={{64,0},{80,16},{96,32},{112,48},{128,64},{144,80},{160,96},{176,11... | collective-permute-start | bytes 196616 | tf_op jit(solution)/shard_map/ppermute | solution.py:307
  93.2 20.5 %collective-permute-start.9 = (bf16[128,512]{1,0:T(8,128)(2,1)S(1)}, bf16[128,512]{1,0:T(8,128)(2,1)S(1)}, u32[]{:S(2)}, u32[]{:S(2)}) collective-permute-start(bf16[128,512]{1,0:T(8,128)(2,1)S(1)} %pad_maximum_fusion.2), channel_id=1, source_target_pairs={{32,0},{48,16},{64,32},{80,48},{96,64},{112,80},{128,96},{144,112}... | collective-permute-start | bytes 393224 | tf_op jit(solution)/shard_map/ppermute | solution.py:307
  114.7 23.0 %all-to-all-start.4 = ((f32[32,3,128]{2,1,0:T(4,128)}), f32[32,3,128]{2,1,0:T(4,128)S(1)}, u32[]{:S(2)}, u32[]{:S(2)}) async-start(f32[32,3,128]{2,1,0:T(4,128)} %broadcast_in_dim.24), calls=%async_computation.4 | async-start | bytes 131072 | tf_op jit(solution)/shard_map/all_to_all | solution.py:316

commit v7 on v5

--- a/solution.py
+++ b/solution.py
@@ -184,7 +184,7 @@
     )(*hbm)
 
 
-def spread_kernel(x_ref, row_ref, one_ref, two_ref, three_ref, four_ref, out_ref):
+def spread_kernel(x_ref, four_ref, three_ref, two_ref, one_ref, row_ref, out_ref):
     rows = row_ref.shape[0]
     for i in range(out_ref.shape[0]):
         @pl.when(i > x_ref[0])
@@ -209,17 +209,17 @@
         grid=(1,),
         in_specs=[
             pl.BlockSpec(memory_space=pltpu.SMEM),
+            pl.BlockSpec((rows, width), lambda g: (below, 0)),
+            pl.BlockSpec((rows, width), lambda g: (0, 0)),
             at_head,
             at_head,
             at_head,
-            pl.BlockSpec((rows, width), lambda g: (0, 0)),
-            pl.BlockSpec((rows, width), lambda g: (below, 0)),
         ],
         out_specs=pl.BlockSpec(memory_space=pltpu.VMEM),
         out_shape=jax.ShapeDtypeStruct((n, ROWS * rows, width), BF),
         compiler_params=pltpu.CompilerParams(vmem_limit_bytes=8 << 20),
         cost_estimate=pl.CostEstimate(flops=0, bytes_accessed=2 << 20, transcendentals=0),
-    )(where_x, row, one, two, three, four)
+    )(where_x, four, three, two, one, row)
 
 
 def fold_kernel(x_ref, back_ref, gown_ref, sent_ref, kept_ref):
@@ -325,12 +325,11 @@
     n_x = lax.axis_size("cx")
     at_x = where_x.astype(jnp.int32)[None]
     row, row_first = prepare(key[0], value[0], key_shift[0], value_shift[0], doc_ids)
-    one, two = along_z(row, 1), along_z(row, 2)
+    four, three = along_z(row_first, 4), along_z(row_first, 3)
+    two, one = along_z(row, 2), along_z(row, 1)
     wins = []
     for h in range(kv_local):
-        if h == 0:
-            three, four = along_z(row_first, 3), along_z(row_first, 4)
-        else:
+        if h > 0:
             part = slice(2 * h * HEAD, 2 * (h + 1) * HEAD)
             three = four = along_z(jnp.concatenate([one[:, part], two[:, part]], 0), 2)
         wins.append(swap_x(spread(at_x, row, one, two, three, four, h, n_x)))
@@ -367,8 +366,9 @@
         ]
     )
     n_dp, n_tp = lax.axis_size("dp"), lax.axis_size("tp")
+    first = ((lax.axis_index("dp") * n_x + where_x) * n_tp).astype(jnp.int32)[None]
+    sums, first = lax.optimization_barrier((sums, first))
     plane = sum_among(sums, ("dp", "cx", "tp"))
-    first = ((lax.axis_index("dp") * n_x + where_x) * n_tp).astype(jnp.int32)[None]
     near, square = gather(first, plane, lax.axis_size("cz"), n_tp)
     everything = lax.all_to_all(square, "cz", 0, 0)
     count = n_dp * tokens * n_x * lax.axis_size("cz") * 2 * KV_HEADS * HEAD

time: 163 us -> 162 us (level)
  blocking collectives: 27.4 us -> 46.9 us
  starting transfers between devices: 59.2 us -> 48.7 us
  waiting for transfers between devices: 50.1 us -> 41.2 us
    all_to_all x0 -> x1, blocking collectives: none -> 21.1 us  [sum_among(): return lax.all_to_all(jnp.broadcast_to(x[None], (n,) + x.shape), axes, 0, 0)]
    all_to_all x1 -> x0, starting transfers between devices: 12.2 us -> none  [sum_among(): return lax.all_to_all(jnp.broadcast_to(x[None], (n,) + x.shape), axes, 0, 0)]
    all_to_all x1 -> x0, waiting for transfers between devices: 7.13 us -> none  [sum_among(): return lax.all_to_all(jnp.broadcast_to(x[None], (n,) + x.shape), axes, 0, 0)]
    ppermute x9, starting transfers between devices: 32.2 us -> 33.9 us  [along_z(): lax.ppermute(x, 'cz', [(i - d, i) for i in range(n) if 0 <= i - d < n])]
    all_to_all x1, blocking collectives: 27.4 us -> 25.7 us  [per_device(): everything = lax.all_to_all(square, 'cz', 0, 0)]
    all_to_all x4, waiting for transfers between devices: 17.7 us -> 16.1 us  [swap_x(): return lax.all_to_all(x, 'cx', 0, 0)]
  transfers between devices with their start and end apart: 14 -> 13, of which waited for: 10 -> 9; matrix products, arithmetic and copies ran while one was open for 0% -> 0% of each run, Pallas kernels for 12% -> 12%
where the time goes in v7:
time: 162 us; the launch traced here: 161 us
  starting transfers between devices  48.7 us (30%)
  blocking collectives  46.9 us (29%)
  waiting for transfers between devices  41.2 us (25%)
  Pallas kernels  23 us (14%)
    ppermute x9, starting transfers between devices, along_z(): lax.ppermute(x, 'cz', [(i - d, i) for i in range(n) if 0 <= i - d < n])  33.9 us
    all_to_all x1, blocking collectives, per_device(): everything = lax.all_to_all(square, 'cz', 0, 0)  25.7 us
    ppermute x9, waiting for transfers between devices, along_z(): lax.ppermute(x, 'cz', [(i - d, i) for i in range(n) if 0 <= i - d < n])  25.1 us
    all_to_all x1, blocking collectives, sum_among(): return lax.all_to_all(jnp.broadcast_to(x[None], (n,) + x.shape), axes, 0, 0)  21.1 us
    pallas_call x2, Pallas kernels, attention(): pl.pallas_call(attn_kernel, grid=(1,), in_specs=[wide, wide, whole, pl.Bl...  18.3 us
    all_to_all x4, waiting for transfers between devices, swap_x(): return lax.all_to_all(x, 'cx', 0, 0)  16.1 us
    all_to_all x4, starting transfers between devices, swap_x(): return lax.all_to_all(x, 'cx', 0, 0)  14.8 us
  transfers between devices with their start and end apart: 13, of which 9 were waited for; matrix products, arithmetic and copies ran while one was open for 0% of the time, Pallas kernels for 12%

profile of v7, /device:TPU:1, one launch (start us, length us, event | category | flops | bytes accessed | tf_op | source)
XLA Modules:
  0.0 161.0 jit_solution(16917993619158757310)
XLA Ops:
  0.6 1.1 shard_map.94
  1.7 4.4 %collective-permute-start = (bf16[136,512]{1,0:T(8,128)(2,1)S(1)}, bf16[136,512]{1,0:T(8,128)(2,1)S(1)}, u32[]{:S(2)}, u32[]{:S(2)}) collective-permute-start(bf16[136,512]{1,0:T(8,128)(2,1)S(1)} %get-tuple-element.21.row_ref.own_ref), channel_id=1, source_target_pairs={{0,16},{16,32},{32,48},{48,64},{64,80},{80,96},{96,112},{112,128},... | collective-permute-start | bytes 417800 | tf_op jit(solution)/shard_map/ppermute | solution.py:309
  6.1 4.9 %collective-permute-start.1 = (bf16[136,512]{1,0:T(8,128)(2,1)S(1)}, bf16[136,512]{1,0:T(8,128)(2,1)S(1)}, u32[]{:S(2)}, u32[]{:S(2)}) collective-permute-start(bf16[136,512]{1,0:T(8,128)(2,1)S(1)} %get-tuple-element.21.row_ref.own_ref), channel_id=1, source_target_pairs={{0,32},{16,48},{32,64},{48,80},{64,96},{80,112},{96,128},{112,144}... | collective-permute-start | bytes 417800 | tf_op jit(solution)/shard_map/ppermute | solution.py:309
  11.0 8.8 %collective-permute-start.3 = (bf16[136,256]{1,0:T(8,128)(2,1)S(1)}, bf16[136,256]{1,0:T(8,128)(2,1)S(1)}, u32[]{:S(2)}, u32[]{:S(2)}) collective-permute-start(bf16[136,256]{1,0:T(8,128)(2,1)S(1)} %get-tuple-element.22), channel_id=1, source_target_pairs={{0,64},{16,80},{32,96},{48,112},{64,128},{80,144},{96,160},{112,17... | collective-permute-start | bytes 208904 | tf_op jit(solution)/shard_map/ppermute | solution.py:309
  19.8 5.7 %collective-permute-start.4 = (bf16[136,256]{1,0:T(8,128)(2,1)S(1)}, bf16[136,256]{1,0:T(8,128)(2,1)S(1)}, u32[]{:S(2)}, u32[]{:S(2)}) collective-permute-start(bf16[136,256]{1,0:T(8,128)(2,1)S(1)} %get-tuple-element.22), channel_id=1, source_target_pairs={{0,48},{16,64},{32,80},{48,96},{64,112},{80,128},{96,144},{112,160... | collective-permute-start | bytes 208904 | tf_op jit(solution)/shard_map/ppermute | solution.py:309
  25.5 0.0 collective-permute-done.3.four_ref
  25.5 1.3 collective-permute-done.4.three_ref
  26.9 0.0 collective-permute-done.one_ref
  26.9 0.0 collective-permute-done.1.two_ref
  26.9 1.1 shard_map.96
  28.0 4.0 %all-to-all-start.1 = ((bf16[4,544,256]{2,1,0:T(8,128)(2,1)}), bf16[4,544,256]{2,1,0:T(8,128)(2,1)S(1)}, u32[]{:S(2)}, u32[]{:S(2)}) async-start(bf16[4,544,256]{2,1,0:T(8,128)(2,1)} %shard_map.96), calls=%async_computation.1 | async-start | bytes 2228224 | tf_op jit(solution)/shard_map/all_to_all | solution.py:313
  32.0 4.8 %collective-permute-start.2 = (bf16[272,256]{1,0:T(8,128)(2,1)S(1)}, bf16[272,256]{1,0:T(8,128)(2,1)S(1)}, u32[]{:S(2)}, u32[]{:S(2)}) collective-permute-start(bf16[272,256]{1,0:T(8,128)(2,1)S(1)} %pad_maximum_fusion), channel_id=1, source_target_pairs={{0,32},{16,48},{32,64},{48,80},{64,96},{80,112},{96,128},{112,144}... | collective-permute-start | bytes 417800 | tf_op jit(solution)/shard_map/ppermute | solution.py:309
  36.9 2.0 %collective-permute-done.2.four_ref.three_ref = bf16[272,256]{1,0:T(8,128)(2,1)S(1)} collective-permute-done((bf16[272,256]{1,0:T(8,128)(2,1)S(1)}, bf16[272,256]{1,0:T(8,128)(2,1)S(1)}, u32[]{:S(2)}, u32[]{:S(2)}) %collective-permute-start.2) | collective-permute-done | bytes 139296 | tf_op jit(solution)/shard_map/ppermute | solution.py:309
  38.9 1.1 shard_map.95
  40.0 4.9 %all-to-all-done.1.win_ref = bf16[4,544,256]{2,1,0:T(8,128)(2,1)S(1)} async-done(((bf16[4,544,256]{2,1,0:T(8,128)(2,1)}), bf16[4,544,256]{2,1,0:T(8,128)(2,1)S(1)}, u32[]{:S(2)}, u32[]{:S(2)}) %all-to-all-start.1) | async-done | bytes 1114144 | tf_op jit(solution)/shard_map/all_to_all | solution.py:313
  44.9 3.5 %all-to-all-start = ((bf16[4,544,256]{2,1,0:T(8,128)(2,1)}), bf16[4,544,256]{2,1,0:T(8,128)(2,1)S(1)}, u32[]{:S(2)}, u32[]{:S(2)}) async-start(bf16[4,544,256]{2,1,0:T(8,128)(2,1)} %shard_map.95), calls=%async_computation | async-start | bytes 2228224 | tf_op jit(solution)/shard_map/all_to_all | solution.py:313
  48.4 9.1 %shard_map.97 = (bf16[128,2048]{1,0:T(8,128)(2,1)}, bf16[4,512,256]{2,1,0:T(8,128)(2,1)}, f32[128,256]{1,0:T(8,128)S(1)}) custom-call(bf16[128,2048]{1,0:T(8,128)(2,1)} %bitcast.27, bf16[128,2048]{1,0:T(8,128)(2,1)} %bitcast.30, bf16[4,544,256]{2,1,0:T(8,128)(2,1)S(1)} %all-to-all-done.1.win_ref, bf16[136,512]{1,0:T(8,128)(2,1)S(1)} %get-tuple-element.21.row_ref.own_ref, ...), custom_call_target="tpu_custom_call" | custom-call | flops 2852126720 | bytes 4194304 | tf_op jit(solution)/shard_map/pallas_call | solution.py:117
  57.6 2.5 %all-to-all-done.win_ref = bf16[4,544,256]{2,1,0:T(8,128)(2,1)S(1)} async-done(((bf16[4,544,256]{2,1,0:T(8,128)(2,1)}), bf16[4,544,256]{2,1,0:T(8,128)(2,1)S(1)}, u32[]{:S(2)}, u32[]{:S(2)}) %all-to-all-start) | async-done | bytes 1114144 | tf_op jit(solution)/shard_map/all_to_all | solution.py:313
  60.0 3.7 %all-to-all-start.2 = ((bf16[4,512,256]{2,1,0:T(8,128)(2,1)}), bf16[4,512,256]{2,1,0:T(8,128)(2,1)S(1)}, u32[]{:S(2)}, u32[]{:S(2)}) async-start(bf16[4,512,256]{2,1,0:T(8,128)(2,1)} %get-tuple-element.25), calls=%async_computation.2 | async-start | bytes 2097152 | tf_op jit(solution)/shard_map/all_to_all | solution.py:313
  63.7 9.1 %shard_map.98 = (bf16[128,2048]{1,0:T(8,128)(2,1)}, bf16[4,512,256]{2,1,0:T(8,128)(2,1)}, f32[128,256]{1,0:T(8,128)S(1)}) custom-call(bf16[128,2048]{1,0:T(8,128)(2,1)} %bitcast.29, bf16[128,2048]{1,0:T(8,128)(2,1)} %bitcast.31, bf16[4,544,256]{2,1,0:T(8,128)(2,1)S(1)} %all-to-all-done.win_ref, ...), custom_call_target="tpu_custom_call", output_to_operand_aliasing={{0}: (4, {})} | custom-call | flops 2852126720 | bytes 4194304 | tf_op jit(solution)/shard_map/pallas_call | solution.py:117
  72.9 0.4 all-to-all-done.2.back_ref
  73.3 3.6 %all-to-all-start.3 = ((bf16[4,512,256]{2,1,0:T(8,128)(2,1)}), bf16[4,512,256]{2,1,0:T(8,128)(2,1)S(1)}, u32[]{:S(2)}, u32[]{:S(2)}) async-start(bf16[4,512,256]{2,1,0:T(8,128)(2,1)} %get-tuple-element.28), calls=%async_computation.3 | async-start | bytes 2097152 | tf_op jit(solution)/shard_map/all_to_all | solution.py:313
  76.9 0.2 shard_map.99
  77.1 1.3 collective-permute-start.5
  78.4 8.2 %all-to-all-done.3.back_ref = bf16[4,512,256]{2,1,0:T(8,128)(2,1)S(1)} async-done(((bf16[4,512,256]{2,1,0:T(8,128)(2,1)}), bf16[4,512,256]{2,1,0:T(8,128)(2,1)S(1)}, u32[]{:S(2)}, u32[]{:S(2)}) %all-to-all-start.3) | async-done | bytes 1048608 | tf_op jit(solution)/shard_map/all_to_all | solution.py:313
  86.7 0.2 shard_map.100
  86.9 1.3 collective-permute-start.6
  88.2 0.0 collective-permute-done.5
  88.2 6.3 %collective-permute-done.6 = bf16[256,256]{1,0:T(8,128)(2,1)S(1)} collective-permute-done((bf16[256,256]{1,0:T(8,128)(2,1)S(1)}, bf16[256,256]{1,0:T(8,128)(2,1)S(1)}, u32[]{:S(2)}, u32[]{:S(2)}) %collective-permute-start.6) | collective-permute-done | bytes 131104 | tf_op jit(solution)/shard_map/ppermute | solution.py:309
  94.6 0.0 copy-start
  94.6 0.0 copy-start.1
  94.6 1.4 collective-permute-start.7
  96.1 1.3 collective-permute-start.8
  97.4 12.1 %collective-permute-done.7 = bf16[128,512]{1,0:T(8,128)(2,1)S(1)} collective-permute-done((bf16[128,512]{1,0:T(8,128)(2,1)S(1)}, bf16[128,512]{1,0:T(8,128)(2,1)S(1)}, u32[]{:S(2)}, u32[]{:S(2)}) %collective-permute-start.7) | collective-permute-done | bytes 131104 | tf_op jit(solution)/shard_map/ppermute | solution.py:309
  109.4 3.3 %collective-permute-done.8 = bf16[128,512]{1,0:T(8,128)(2,1)S(1)} collective-permute-done((bf16[128,512]{1,0:T(8,128)(2,1)S(1)}, bf16[128,512]{1,0:T(8,128)(2,1)S(1)}, u32[]{:S(2)}, u32[]{:S(2)}) %collective-permute-start.8) | collective-permute-done | bytes 131104 | tf_op jit(solution)/shard_map/ppermute | solution.py:309
  112.9 0.0 copy-done
  112.9 0.0 copy-done.1
  112.9 0.2 multiply_reduce_fusion.4
  113.1 21.1 %all_to_all.30.plane_ref = f32[32,3,128]{2,1,0:T(4,128)S(1)} all-to-all(f32[32,3,128]{2,1,0:T(4,128)S(1)} %broadcast_in_dim.24), channel_id=1, replica_groups=mesh['dp'=2,'cz'=16,'cx'=4,'tp'=4] {'dp','cx','tp'}, dimensions={0} | all-to-all | bytes 98304 | tf_op jit(solution)/shard_map/all_to_all | solution.py:318
  134.3 0.1 shard_map.101
  134.4 25.7 %all_to_all.31.all_ref = f32[16,1,128]{2,1,0:T(1,128)S(1)} all-to-all(f32[16,1,128]{2,1,0:T(1,128)S(1)} %get-tuple-element.35), channel_id=1, replica_groups=mesh['dp'=2,'cz'=16,'cx'=4,'tp'=4] {'cz'}, dimensions={0} | all-to-all | bytes 16384 | tf_op jit(solution)/shard_map/all_to_all | solution.py:373
  160.2 0.9 shard_map.102
  (14 shorter events, 0.2 us)
Async XLA Ops:
  1.7 25.1 %collective-permute-start = (bf16[136,512]{1,0:T(8,128)(2,1)S(1)}, bf16[136,512]{1,0:T(8,128)(2,1)S(1)}, u32[]{:S(2)}, u32[]{:S(2)}) collective-permute-start(bf16[136,512]{1,0:T(8,128)(2,1)S(1)} %get-tuple-element.21.row_ref.own_ref), channel_id=1, source_target_pairs={{0,16},{16,32},{32,48},{48,64},{64,80},{80,96},{96,112},{112,128},... | collective-permute-start | bytes 417800 | tf_op jit(solution)/shard_map/ppermute | solution.py:309
  6.1 20.8 %collective-permute-start.1 = (bf16[136,512]{1,0:T(8,128)(2,1)S(1)}, bf16[136,512]{1,0:T(8,128)(2,1)S(1)}, u32[]{:S(2)}, u32[]{:S(2)}) collective-permute-start(bf16[136,512]{1,0:T(8,128)(2,1)S(1)} %get-tuple-element.21.row_ref.own_ref), channel_id=1, source_target_pairs={{0,32},{16,48},{32,64},{48,80},{64,96},{80,112},{96,128},{112,144}... | collective-permute-start | bytes 417800 | tf_op jit(solution)/shard_map/ppermute | solution.py:309
  11.0 14.5 %collective-permute-start.3 = (bf16[136,256]{1,0:T(8,128)(2,1)S(1)}, bf16[136,256]{1,0:T(8,128)(2,1)S(1)}, u32[]{:S(2)}, u32[]{:S(2)}) collective-permute-start(bf16[136,256]{1,0:T(8,128)(2,1)S(1)} %get-tuple-element.22), channel_id=1, source_target_pairs={{0,64},{16,80},{32,96},{48,112},{64,128},{80,144},{96,160},{112,17... | collective-permute-start | bytes 208904 | tf_op jit(solution)/shard_map/ppermute | solution.py:309
  19.8 7.0 %collective-permute-start.4 = (bf16[136,256]{1,0:T(8,128)(2,1)S(1)}, bf16[136,256]{1,0:T(8,128)(2,1)S(1)}, u32[]{:S(2)}, u32[]{:S(2)}) collective-permute-start(bf16[136,256]{1,0:T(8,128)(2,1)S(1)} %get-tuple-element.22), channel_id=1, source_target_pairs={{0,48},{16,64},{32,80},{48,96},{64,112},{80,128},{96,144},{112,160... | collective-permute-start | bytes 208904 | tf_op jit(solution)/shard_map/ppermute | solution.py:309
  28.0 16.9 %all-to-all-start.1 = ((bf16[4,544,256]{2,1,0:T(8,128)(2,1)}), bf16[4,544,256]{2,1,0:T(8,128)(2,1)S(1)}, u32[]{:S(2)}, u32[]{:S(2)}) async-start(bf16[4,544,256]{2,1,0:T(8,128)(2,1)} %shard_map.96), calls=%async_computation.1 | async-start | bytes 2228224 | tf_op jit(solution)/shard_map/all_to_all | solution.py:313
  32.0 6.8 %collective-permute-start.2 = (bf16[272,256]{1,0:T(8,128)(2,1)S(1)}, bf16[272,256]{1,0:T(8,128)(2,1)S(1)}, u32[]{:S(2)}, u32[]{:S(2)}) collective-permute-start(bf16[272,256]{1,0:T(8,128)(2,1)S(1)} %pad_maximum_fusion), channel_id=1, source_target_pairs={{0,32},{16,48},{32,64},{48,80},{64,96},{80,112},{96,128},{112,144}... | collective-permute-start | bytes 417800 | tf_op jit(solution)/shard_map/ppermute | solution.py:309
  44.9 15.2 %all-to-all-start = ((bf16[4,544,256]{2,1,0:T(8,128)(2,1)}), bf16[4,544,256]{2,1,0:T(8,128)(2,1)S(1)}, u32[]{:S(2)}, u32[]{:S(2)}) async-start(bf16[4,544,256]{2,1,0:T(8,128)(2,1)} %shard_map.95), calls=%async_computation | async-start | bytes 2228224 | tf_op jit(solution)/shard_map/all_to_all | solution.py:313
  60.0 13.3 %all-to-all-start.2 = ((bf16[4,512,256]{2,1,0:T(8,128)(2,1)}), bf16[4,512,256]{2,1,0:T(8,128)(2,1)S(1)}, u32[]{:S(2)}, u32[]{:S(2)}) async-start(bf16[4,512,256]{2,1,0:T(8,128)(2,1)} %get-tuple-element.25), calls=%async_computation.2 | async-start | bytes 2097152 | tf_op jit(solution)/shard_map/all_to_all | solution.py:313
  73.3 13.3 %all-to-all-start.3 = ((bf16[4,512,256]{2,1,0:T(8,128)(2,1)}), bf16[4,512,256]{2,1,0:T(8,128)(2,1)S(1)}, u32[]{:S(2)}, u32[]{:S(2)}) async-start(bf16[4,512,256]{2,1,0:T(8,128)(2,1)} %get-tuple-element.28), calls=%async_computation.3 | async-start | bytes 2097152 | tf_op jit(solution)/shard_map/all_to_all | solution.py:313
  77.1 11.0 %collective-permute-start.5 = (bf16[256,256]{1,0:T(8,128)(2,1)S(1)}, bf16[256,256]{1,0:T(8,128)(2,1)S(1)}, u32[]{:S(2)}, u32[]{:S(2)}) collective-permute-start(bf16[256,256]{1,0:T(8,128)(2,1)S(1)} %get-tuple-element.31), channel_id=1, source_target_pairs={{32,0},{48,16},{64,32},{80,48},{96,64},{112,80},{128,96},{144,112}... | collective-permute-start | bytes 393224 | tf_op jit(solution)/shard_map/ppermute | solution.py:309
  86.9 7.7 %collective-permute-start.6 = (bf16[256,256]{1,0:T(8,128)(2,1)S(1)}, bf16[256,256]{1,0:T(8,128)(2,1)S(1)}, u32[]{:S(2)}, u32[]{:S(2)}) collective-permute-start(bf16[256,256]{1,0:T(8,128)(2,1)S(1)} %get-tuple-element.32), channel_id=1, source_target_pairs={{32,0},{48,16},{64,32},{80,48},{96,64},{112,80},{128,96},{144,112}... | collective-permute-start | bytes 393224 | tf_op jit(solution)/shard_map/ppermute | solution.py:309
  94.6 18.3 %copy-start = (f32[1,128,256]{2,1,0:T(8,128)S(1)}, f32[1,128,256]{2,1,0:T(8,128)}, u32[]{:S(2)}) copy-start(f32[1,128,256]{2,1,0:T(8,128)} %param.10) | copy-start | bytes 393220
  94.6 18.3 %copy-start.1 = (f32[1,128,256]{2,1,0:T(8,128)S(1)}, f32[1,128,256]{2,1,0:T(8,128)}, u32[]{:S(2)}) copy-start(f32[1,128,256]{2,1,0:T(8,128)} %param.11) | copy-start | bytes 393220
  94.6 14.8 %collective-permute-start.7 = (bf16[128,512]{1,0:T(8,128)(2,1)S(1)}, bf16[128,512]{1,0:T(8,128)(2,1)S(1)}, u32[]{:S(2)}, u32[]{:S(2)}) collective-permute-start(bf16[128,512]{1,0:T(8,128)(2,1)S(1)} %pad_maximum_fusion.1), channel_id=1, source_target_pairs={{16,0},{32,16},{48,32},{64,48},{80,64},{96,80},{112,96},{128,112},... | collective-permute-start | bytes 393224 | tf_op jit(solution)/shard_map/ppermute | solution.py:309
  96.1 16.7 %collective-permute-start.8 = (bf16[128,512]{1,0:T(8,128)(2,1)S(1)}, bf16[128,512]{1,0:T(8,128)(2,1)S(1)}, u32[]{:S(2)}, u32[]{:S(2)}) collective-permute-start(bf16[128,512]{1,0:T(8,128)(2,1)S(1)} %pad_maximum_fusion.2), channel_id=1, source_target_pairs={{32,0},{48,16},{64,32},{80,48},{96,64},{112,80},{128,96},{144,112}... | collective-permute-start | bytes 393224 | tf_op jit(solution)/shard_map/ppermute | solution.py:309

commit v8 on v7

--- a/solution.py
+++ b/solution.py
@@ -350,7 +350,8 @@
         for b in range(2)
     ]
     two, one = along_z(near[1], -2), along_z(near[0], -1)
-    grad = jnp.concatenate([mine[:tokens] for _, mine in kept], 1) + one.astype(F32) + two.astype(F32)
+    own = jnp.concatenate([mine[:tokens] for _, mine in kept], 1)
+    grad = two.astype(F32) + one.astype(F32) + own
     grad_key = jnp.concatenate(
         [grad[:, 2 * h * HEAD : (2 * h + 1) * HEAD] for h in range(kv_local)], 1
     )

time: 162 us -> 161 us (level)
  waiting for transfers between devices: 41.2 us -> 39.3 us
    all_to_all x1, blocking collectives: 25.7 us -> 28.6 us  [per_device(): everything = lax.all_to_all(square, 'cz', 0, 0)]
    ppermute x9, waiting for transfers between devices: 25.1 us -> 23.2 us  [along_z(): lax.ppermute(x, 'cz', [(i - d, i) for i in range(n) if 0 <= i - d < n])]
    all_to_all x1, blocking collectives: 21.1 us -> 19.4 us  [sum_among(): return lax.all_to_all(jnp.broadcast_to(x[None], (n,) + x.shape), axes, 0, 0)]
where the time goes in v8:
time: 161 us; the launch traced here: 160 us
  starting transfers between devices  48.7 us (30%)
  blocking collectives  48 us (30%)
  waiting for transfers between devices  39.3 us (24%)
  Pallas kernels  23 us (14%)
    ppermute x9, starting transfers between devices, along_z(): lax.ppermute(x, 'cz', [(i - d, i) for i in range(n) if 0 <= i - d < n])  33.9 us
    all_to_all x1, blocking collectives, per_device(): everything = lax.all_to_all(square, 'cz', 0, 0)  28.6 us
    ppermute x9, waiting for transfers between devices, along_z(): lax.ppermute(x, 'cz', [(i - d, i) for i in range(n) if 0 <= i - d < n])  23.2 us
    all_to_all x1, blocking collectives, sum_among(): return lax.all_to_all(jnp.broadcast_to(x[None], (n,) + x.shape), axes, 0, 0)  19.4 us
    pallas_call x2, Pallas kernels, attention(): pl.pallas_call(attn_kernel, grid=(1,), in_specs=[wide, wide, whole, pl.Bl...  18.3 us
    all_to_all x4, waiting for transfers between devices, swap_x(): return lax.all_to_all(x, 'cx', 0, 0)  16.1 us
    all_to_all x4, starting transfers between devices, swap_x(): return lax.all_to_all(x, 'cx', 0, 0)  14.8 us
  transfers between devices with their start and end apart: 13, of which 9 were waited for; matrix products, arithmetic and copies ran while one was open for 0% of the time, Pallas kernels for 12%

profile of v8, /device:TPU:1, one launch (start us, length us, event | category | flops | bytes accessed | tf_op | source)
XLA Modules:
  0.0 160.2 jit_solution(17354005104769324143)
XLA Ops:
  0.6 1.1 shard_map.94
  1.7 4.4 %collective-permute-start = (bf16[136,512]{1,0:T(8,128)(2,1)S(1)}, bf16[136,512]{1,0:T(8,128)(2,1)S(1)}, u32[]{:S(2)}, u32[]{:S(2)}) collective-permute-start(bf16[136,512]{1,0:T(8,128)(2,1)S(1)} %get-tuple-element.21.row_ref.own_ref), channel_id=1, source_target_pairs={{0,16},{16,32},{32,48},{48,64},{64,80},{80,96},{96,112},{112,128},... | collective-permute-start | bytes 417800 | tf_op jit(solution)/shard_map/ppermute | solution.py:309
  6.1 4.9 %collective-permute-start.1 = (bf16[136,512]{1,0:T(8,128)(2,1)S(1)}, bf16[136,512]{1,0:T(8,128)(2,1)S(1)}, u32[]{:S(2)}, u32[]{:S(2)}) collective-permute-start(bf16[136,512]{1,0:T(8,128)(2,1)S(1)} %get-tuple-element.21.row_ref.own_ref), channel_id=1, source_target_pairs={{0,32},{16,48},{32,64},{48,80},{64,96},{80,112},{96,128},{112,144}... | collective-permute-start | bytes 417800 | tf_op jit(solution)/shard_map/ppermute | solution.py:309
  11.0 8.8 %collective-permute-start.3 = (bf16[136,256]{1,0:T(8,128)(2,1)S(1)}, bf16[136,256]{1,0:T(8,128)(2,1)S(1)}, u32[]{:S(2)}, u32[]{:S(2)}) collective-permute-start(bf16[136,256]{1,0:T(8,128)(2,1)S(1)} %get-tuple-element.22), channel_id=1, source_target_pairs={{0,64},{16,80},{32,96},{48,112},{64,128},{80,144},{96,160},{112,17... | collective-permute-start | bytes 208904 | tf_op jit(solution)/shard_map/ppermute | solution.py:309
  19.8 5.7 %collective-permute-start.4 = (bf16[136,256]{1,0:T(8,128)(2,1)S(1)}, bf16[136,256]{1,0:T(8,128)(2,1)S(1)}, u32[]{:S(2)}, u32[]{:S(2)}) collective-permute-start(bf16[136,256]{1,0:T(8,128)(2,1)S(1)} %get-tuple-element.22), channel_id=1, source_target_pairs={{0,48},{16,64},{32,80},{48,96},{64,112},{80,128},{96,144},{112,160... | collective-permute-start | bytes 208904 | tf_op jit(solution)/shard_map/ppermute | solution.py:309
  25.5 0.0 collective-permute-done.3.four_ref
  25.5 1.3 collective-permute-done.4.three_ref
  26.9 0.0 collective-permute-done.one_ref
  26.9 0.0 collective-permute-done.1.two_ref
  26.9 1.1 shard_map.96
  28.0 4.0 %all-to-all-start.1 = ((bf16[4,544,256]{2,1,0:T(8,128)(2,1)}), bf16[4,544,256]{2,1,0:T(8,128)(2,1)S(1)}, u32[]{:S(2)}, u32[]{:S(2)}) async-start(bf16[4,544,256]{2,1,0:T(8,128)(2,1)} %shard_map.96), calls=%async_computation.1 | async-start | bytes 2228224 | tf_op jit(solution)/shard_map/all_to_all | solution.py:313
  32.0 4.8 %collective-permute-start.2 = (bf16[272,256]{1,0:T(8,128)(2,1)S(1)}, bf16[272,256]{1,0:T(8,128)(2,1)S(1)}, u32[]{:S(2)}, u32[]{:S(2)}) collective-permute-start(bf16[272,256]{1,0:T(8,128)(2,1)S(1)} %pad_maximum_fusion), channel_id=1, source_target_pairs={{0,32},{16,48},{32,64},{48,80},{64,96},{80,112},{96,128},{112,144}... | collective-permute-start | bytes 417800 | tf_op jit(solution)/shard_map/ppermute | solution.py:309
  36.9 2.0 %collective-permute-done.2.four_ref.three_ref = bf16[272,256]{1,0:T(8,128)(2,1)S(1)} collective-permute-done((bf16[272,256]{1,0:T(8,128)(2,1)S(1)}, bf16[272,256]{1,0:T(8,128)(2,1)S(1)}, u32[]{:S(2)}, u32[]{:S(2)}) %collective-permute-start.2) | collective-permute-done | bytes 139296 | tf_op jit(solution)/shard_map/ppermute | solution.py:309
  38.9 1.1 shard_map.95
  40.0 4.9 %all-to-all-done.1.win_ref = bf16[4,544,256]{2,1,0:T(8,128)(2,1)S(1)} async-done(((bf16[4,544,256]{2,1,0:T(8,128)(2,1)}), bf16[4,544,256]{2,1,0:T(8,128)(2,1)S(1)}, u32[]{:S(2)}, u32[]{:S(2)}) %all-to-all-start.1) | async-done | bytes 1114144 | tf_op jit(solution)/shard_map/all_to_all | solution.py:313
  44.9 3.5 %all-to-all-start = ((bf16[4,544,256]{2,1,0:T(8,128)(2,1)}), bf16[4,544,256]{2,1,0:T(8,128)(2,1)S(1)}, u32[]{:S(2)}, u32[]{:S(2)}) async-start(bf16[4,544,256]{2,1,0:T(8,128)(2,1)} %shard_map.95), calls=%async_computation | async-start | bytes 2228224 | tf_op jit(solution)/shard_map/all_to_all | solution.py:313
  48.4 9.1 %shard_map.97 = (bf16[128,2048]{1,0:T(8,128)(2,1)}, bf16[4,512,256]{2,1,0:T(8,128)(2,1)}, f32[128,256]{1,0:T(8,128)S(1)}) custom-call(bf16[128,2048]{1,0:T(8,128)(2,1)} %bitcast.27, bf16[128,2048]{1,0:T(8,128)(2,1)} %bitcast.30, bf16[4,544,256]{2,1,0:T(8,128)(2,1)S(1)} %all-to-all-done.1.win_ref, bf16[136,512]{1,0:T(8,128)(2,1)S(1)} %get-tuple-element.21.row_ref.own_ref, ...), custom_call_target="tpu_custom_call" | custom-call | flops 2852126720 | bytes 4194304 | tf_op jit(solution)/shard_map/pallas_call | solution.py:117
  57.6 2.5 %all-to-all-done.win_ref = bf16[4,544,256]{2,1,0:T(8,128)(2,1)S(1)} async-done(((bf16[4,544,256]{2,1,0:T(8,128)(2,1)}), bf16[4,544,256]{2,1,0:T(8,128)(2,1)S(1)}, u32[]{:S(2)}, u32[]{:S(2)}) %all-to-all-start) | async-done | bytes 1114144 | tf_op jit(solution)/shard_map/all_to_all | solution.py:313
  60.0 3.7 %all-to-all-start.2 = ((bf16[4,512,256]{2,1,0:T(8,128)(2,1)}), bf16[4,512,256]{2,1,0:T(8,128)(2,1)S(1)}, u32[]{:S(2)}, u32[]{:S(2)}) async-start(bf16[4,512,256]{2,1,0:T(8,128)(2,1)} %get-tuple-element.25), calls=%async_computation.2 | async-start | bytes 2097152 | tf_op jit(solution)/shard_map/all_to_all | solution.py:313
  63.7 9.1 %shard_map.98 = (bf16[128,2048]{1,0:T(8,128)(2,1)}, bf16[4,512,256]{2,1,0:T(8,128)(2,1)}, f32[128,256]{1,0:T(8,128)S(1)}) custom-call(bf16[128,2048]{1,0:T(8,128)(2,1)} %bitcast.29, bf16[128,2048]{1,0:T(8,128)(2,1)} %bitcast.31, bf16[4,544,256]{2,1,0:T(8,128)(2,1)S(1)} %all-to-all-done.win_ref, ...), custom_call_target="tpu_custom_call", output_to_operand_aliasing={{0}: (4, {})} | custom-call | flops 2852126720 | bytes 4194304 | tf_op jit(solution)/shard_map/pallas_call | solution.py:117
  72.9 0.4 all-to-all-done.2.back_ref
  73.3 3.6 %all-to-all-start.3 = ((bf16[4,512,256]{2,1,0:T(8,128)(2,1)}), bf16[4,512,256]{2,1,0:T(8,128)(2,1)S(1)}, u32[]{:S(2)}, u32[]{:S(2)}) async-start(bf16[4,512,256]{2,1,0:T(8,128)(2,1)} %get-tuple-element.29), calls=%async_computation.3 | async-start | bytes 2097152 | tf_op jit(solution)/shard_map/all_to_all | solution.py:313
  76.9 0.2 shard_map.99
  77.1 1.3 collective-permute-start.5
  78.4 8.2 %all-to-all-done.3.back_ref = bf16[4,512,256]{2,1,0:T(8,128)(2,1)S(1)} async-done(((bf16[4,512,256]{2,1,0:T(8,128)(2,1)}), bf16[4,512,256]{2,1,0:T(8,128)(2,1)S(1)}, u32[]{:S(2)}, u32[]{:S(2)}) %all-to-all-start.3) | async-done | bytes 1048608 | tf_op jit(solution)/shard_map/all_to_all | solution.py:313
  86.7 0.2 shard_map.100
  86.9 1.3 collective-permute-start.6
  88.2 0.0 collective-permute-done.5
  88.2 6.3 %collective-permute-done.6 = bf16[256,256]{1,0:T(8,128)(2,1)S(1)} collective-permute-done((bf16[256,256]{1,0:T(8,128)(2,1)S(1)}, bf16[256,256]{1,0:T(8,128)(2,1)S(1)}, u32[]{:S(2)}, u32[]{:S(2)}) %collective-permute-start.6) | collective-permute-done | bytes 131104 | tf_op jit(solution)/shard_map/ppermute | solution.py:309
  94.6 0.0 copy-start
  94.6 0.0 copy-start.1
  94.6 1.4 collective-permute-start.7
  96.1 1.3 collective-permute-start.8
  97.4 12.2 %collective-permute-done.7 = bf16[128,512]{1,0:T(8,128)(2,1)S(1)} collective-permute-done((bf16[128,512]{1,0:T(8,128)(2,1)S(1)}, bf16[128,512]{1,0:T(8,128)(2,1)S(1)}, u32[]{:S(2)}, u32[]{:S(2)}) %collective-permute-start.7) | collective-permute-done | bytes 131104 | tf_op jit(solution)/shard_map/ppermute | solution.py:309
  109.5 1.4 collective-permute-done.8
  111.0 0.0 copy-done
  111.0 0.0 copy-done.1
  111.0 0.2 multiply_reduce_fusion.4
  111.3 19.4 %all_to_all.30.plane_ref = f32[32,3,128]{2,1,0:T(4,128)S(1)} all-to-all(f32[32,3,128]{2,1,0:T(4,128)S(1)} %broadcast_in_dim.24), channel_id=1, replica_groups=mesh['dp'=2,'cz'=16,'cx'=4,'tp'=4] {'dp','cx','tp'}, dimensions={0} | all-to-all | bytes 98304 | tf_op jit(solution)/shard_map/all_to_all | solution.py:318
  130.7 0.1 shard_map.101
  130.8 28.6 %all_to_all.31.all_ref = f32[16,1,128]{2,1,0:T(1,128)S(1)} all-to-all(f32[16,1,128]{2,1,0:T(1,128)S(1)} %get-tuple-element.35), channel_id=1, replica_groups=mesh['dp'=2,'cz'=16,'cx'=4,'tp'=4] {'cz'}, dimensions={0} | all-to-all | bytes 16384 | tf_op jit(solution)/shard_map/all_to_all | solution.py:374
  159.4 0.9 shard_map.102
  (14 shorter events, 0.2 us)
Async XLA Ops:
  1.7 25.1 %collective-permute-start = (bf16[136,512]{1,0:T(8,128)(2,1)S(1)}, bf16[136,512]{1,0:T(8,128)(2,1)S(1)}, u32[]{:S(2)}, u32[]{:S(2)}) collective-permute-start(bf16[136,512]{1,0:T(8,128)(2,1)S(1)} %get-tuple-element.21.row_ref.own_ref), channel_id=1, source_target_pairs={{0,16},{16,32},{32,48},{48,64},{64,80},{80,96},{96,112},{112,128},... | collective-permute-start | bytes 417800 | tf_op jit(solution)/shard_map/ppermute | solution.py:309
  6.1 20.8 %collective-permute-start.1 = (bf16[136,512]{1,0:T(8,128)(2,1)S(1)}, bf16[136,512]{1,0:T(8,128)(2,1)S(1)}, u32[]{:S(2)}, u32[]{:S(2)}) collective-permute-start(bf16[136,512]{1,0:T(8,128)(2,1)S(1)} %get-tuple-element.21.row_ref.own_ref), channel_id=1, source_target_pairs={{0,32},{16,48},{32,64},{48,80},{64,96},{80,112},{96,128},{112,144}... | collective-permute-start | bytes 417800 | tf_op jit(solution)/shard_map/ppermute | solution.py:309
  11.0 14.5 %collective-permute-start.3 = (bf16[136,256]{1,0:T(8,128)(2,1)S(1)}, bf16[136,256]{1,0:T(8,128)(2,1)S(1)}, u32[]{:S(2)}, u32[]{:S(2)}) collective-permute-start(bf16[136,256]{1,0:T(8,128)(2,1)S(1)} %get-tuple-element.22), channel_id=1, source_target_pairs={{0,64},{16,80},{32,96},{48,112},{64,128},{80,144},{96,160},{112,17... | collective-permute-start | bytes 208904 | tf_op jit(solution)/shard_map/ppermute | solution.py:309
  19.8 7.0 %collective-permute-start.4 = (bf16[136,256]{1,0:T(8,128)(2,1)S(1)}, bf16[136,256]{1,0:T(8,128)(2,1)S(1)}, u32[]{:S(2)}, u32[]{:S(2)}) collective-permute-start(bf16[136,256]{1,0:T(8,128)(2,1)S(1)} %get-tuple-element.22), channel_id=1, source_target_pairs={{0,48},{16,64},{32,80},{48,96},{64,112},{80,128},{96,144},{112,160... | collective-permute-start | bytes 208904 | tf_op jit(solution)/shard_map/ppermute | solution.py:309
  28.0 16.9 %all-to-all-start.1 = ((bf16[4,544,256]{2,1,0:T(8,128)(2,1)}), bf16[4,544,256]{2,1,0:T(8,128)(2,1)S(1)}, u32[]{:S(2)}, u32[]{:S(2)}) async-start(bf16[4,544,256]{2,1,0:T(8,128)(2,1)} %shard_map.96), calls=%async_computation.1 | async-start | bytes 2228224 | tf_op jit(solution)/shard_map/all_to_all | solution.py:313
  32.0 6.8 %collective-permute-start.2 = (bf16[272,256]{1,0:T(8,128)(2,1)S(1)}, bf16[272,256]{1,0:T(8,128)(2,1)S(1)}, u32[]{:S(2)}, u32[]{:S(2)}) collective-permute-start(bf16[272,256]{1,0:T(8,128)(2,1)S(1)} %pad_maximum_fusion), channel_id=1, source_target_pairs={{0,32},{16,48},{32,64},{48,80},{64,96},{80,112},{96,128},{112,144}... | collective-permute-start | bytes 417800 | tf_op jit(solution)/shard_map/ppermute | solution.py:309
  44.9 15.2 %all-to-all-start = ((bf16[4,544,256]{2,1,0:T(8,128)(2,1)}), bf16[4,544,256]{2,1,0:T(8,128)(2,1)S(1)}, u32[]{:S(2)}, u32[]{:S(2)}) async-start(bf16[4,544,256]{2,1,0:T(8,128)(2,1)} %shard_map.95), calls=%async_computation | async-start | bytes 2228224 | tf_op jit(solution)/shard_map/all_to_all | solution.py:313
  60.0 13.3 %all-to-all-start.2 = ((bf16[4,512,256]{2,1,0:T(8,128)(2,1)}), bf16[4,512,256]{2,1,0:T(8,128)(2,1)S(1)}, u32[]{:S(2)}, u32[]{:S(2)}) async-start(bf16[4,512,256]{2,1,0:T(8,128)(2,1)} %get-tuple-element.25), calls=%async_computation.2 | async-start | bytes 2097152 | tf_op jit(solution)/shard_map/all_to_all | solution.py:313
  73.3 13.3 %all-to-all-start.3 = ((bf16[4,512,256]{2,1,0:T(8,128)(2,1)}), bf16[4,512,256]{2,1,0:T(8,128)(2,1)S(1)}, u32[]{:S(2)}, u32[]{:S(2)}) async-start(bf16[4,512,256]{2,1,0:T(8,128)(2,1)} %get-tuple-element.29), calls=%async_computation.3 | async-start | bytes 2097152 | tf_op jit(solution)/shard_map/all_to_all | solution.py:313
  77.1 11.0 %collective-permute-start.5 = (bf16[256,256]{1,0:T(8,128)(2,1)S(1)}, bf16[256,256]{1,0:T(8,128)(2,1)S(1)}, u32[]{:S(2)}, u32[]{:S(2)}) collective-permute-start(bf16[256,256]{1,0:T(8,128)(2,1)S(1)} %get-tuple-element.28), channel_id=1, source_target_pairs={{32,0},{48,16},{64,32},{80,48},{96,64},{112,80},{128,96},{144,112}... | collective-permute-start | bytes 393224 | tf_op jit(solution)/shard_map/ppermute | solution.py:309
  86.9 7.7 %collective-permute-start.6 = (bf16[256,256]{1,0:T(8,128)(2,1)S(1)}, bf16[256,256]{1,0:T(8,128)(2,1)S(1)}, u32[]{:S(2)}, u32[]{:S(2)}) collective-permute-start(bf16[256,256]{1,0:T(8,128)(2,1)S(1)} %get-tuple-element.32), channel_id=1, source_target_pairs={{32,0},{48,16},{64,32},{80,48},{96,64},{112,80},{128,96},{144,112}... | collective-permute-start | bytes 393224 | tf_op jit(solution)/shard_map/ppermute | solution.py:309
  94.6 16.4 %copy-start = (f32[1,128,256]{2,1,0:T(8,128)S(1)}, f32[1,128,256]{2,1,0:T(8,128)}, u32[]{:S(2)}) copy-start(f32[1,128,256]{2,1,0:T(8,128)} %param.10) | copy-start | bytes 393220
  94.6 16.4 %copy-start.1 = (f32[1,128,256]{2,1,0:T(8,128)S(1)}, f32[1,128,256]{2,1,0:T(8,128)}, u32[]{:S(2)}) copy-start(f32[1,128,256]{2,1,0:T(8,128)} %param.11) | copy-start | bytes 393220
  94.6 14.9 %collective-permute-start.7 = (bf16[128,512]{1,0:T(8,128)(2,1)S(1)}, bf16[128,512]{1,0:T(8,128)(2,1)S(1)}, u32[]{:S(2)}, u32[]{:S(2)}) collective-permute-start(bf16[128,512]{1,0:T(8,128)(2,1)S(1)} %pad_maximum_fusion.1), channel_id=1, source_target_pairs={{32,0},{48,16},{64,32},{80,48},{96,64},{112,80},{128,96},{144,112}... | collective-permute-start | bytes 393224 | tf_op jit(solution)/shard_map/ppermute | solution.py:309
  96.1 14.9 %collective-permute-start.8 = (bf16[128,512]{1,0:T(8,128)(2,1)S(1)}, bf16[128,512]{1,0:T(8,128)(2,1)S(1)}, u32[]{:S(2)}, u32[]{:S(2)}) collective-permute-start(bf16[128,512]{1,0:T(8,128)(2,1)S(1)} %pad_maximum_fusion.2), channel_id=1, source_target_pairs={{16,0},{32,16},{48,32},{64,48},{80,64},{96,80},{112,96},{128,112},... | collective-permute-start | bytes 393224 | tf_op jit(solution)/shard_map/ppermute | solution.py:309
